TPU v7x, 32 devices: a whole 2x2x4 slice. The times are simulated.
32 devices in a mesh: ctx: 16 (over z, y, core), fsdp: 2 (over x).
Axes of the slice: x: 2, y: 2, z: 4, core: 2. Of those that a mesh axis runs over, the one named last changes fastest.
Arguments:
- tokens: bfloat16 [2, 2, 1024, 1024], P(None, 'fsdp', 'ctx'), may hold values from -6 to 6
- cotangent: bfloat16 [2, 2, 1024, 1024], P(None, 'fsdp', 'ctx'), may hold values from -6 to 6
- qkv_weight: bfloat16 [1024, 3072], P(('ctx', 'fsdp')), may hold values from -0.25 to 0.25
- out_weight: bfloat16 [1024, 1024], P(('ctx', 'fsdp')), may hold values from -1.5 to 1.5
- up_weight: bfloat16 [1024, 4096], P(('ctx', 'fsdp')), may hold values from -0.1875 to 0.1875
- down_weight: bfloat16 [4096, 1024], P(('ctx', 'fsdp')), may hold values from -0.09375 to 0.09375
- qkv_bias: bfloat16 [3072], P(('ctx', 'fsdp')), may hold values from -1.5 to 1.5
- out_bias: bfloat16 [1024], P(('ctx', 'fsdp')), may hold values from -1.5 to 1.5
- up_bias: bfloat16 [4096], P(('ctx', 'fsdp')), may hold values from -1.5 to 1.5
- down_bias: bfloat16 [1024], P(('ctx', 'fsdp')), may hold values from -1.5 to 1.5
- first_gain: bfloat16 [1024], P(('ctx', 'fsdp')), may hold values from 0.5 to 1.5
- first_shift: bfloat16 [1024], P(('ctx', 'fsdp')), may hold values from -1.5 to 1.5
- second_gain: bfloat16 [1024], P(('ctx', 'fsdp')), may hold values from 0.5 to 1.5
- second_shift: bfloat16 [1024], P(('ctx', 'fsdp')), may hold values from -1.5 to 1.5
Outputs:
- output: bfloat16 [2, 2, 1024, 1024], P(None, 'fsdp', 'ctx')
- token_grad: float32 [2, 2, 1024, 1024], P(None, 'fsdp', 'ctx')
- qkv_weight_grad: float32 [1024, 3072], P(('ctx', 'fsdp'))
- out_weight_grad: float32 [1024, 1024], P(('ctx', 'fsdp'))
- up_weight_grad: float32 [1024, 4096], P(('ctx', 'fsdp'))
- down_weight_grad: float32 [4096, 1024], P(('ctx', 'fsdp'))
- qkv_bias_grad: float32 [3072], P(('ctx', 'fsdp'))
- out_bias_grad: float32 [1024], P(('ctx', 'fsdp'))
- up_bias_grad: float32 [4096], P(('ctx', 'fsdp'))
- down_bias_grad: float32 [1024], P(('ctx', 'fsdp'))
- first_gain_grad: float32 [1024], P(('ctx', 'fsdp'))
- first_shift_grad: float32 [1024], P(('ctx', 'fsdp'))
- second_gain_grad: float32 [1024], P(('ctx', 'fsdp'))
- second_shift_grad: float32 [1024], P(('ctx', 'fsdp'))
All inputs are finite; a program needn't handle non-finite values.
Results may differ from a plain program's by a relative error of at most 0.017.
The roundings to bfloat16 on the way count: a program that leaves them out, or rounds other values in their place, can miss the bound.
Values may be sent and summed in bfloat16 or wider, within the bound.
A program may use at most 576 MiB of HBM per device.

v0:
```python
from functools import partial
import math

import jax
import jax.numpy as jnp
from jax import lax
from jax.sharding import PartitionSpec as P

HEADS = 16
HEAD = 64
MICRO = 2


def layernorm(resid, gain, shift):
    center = resid - jnp.mean(resid, axis=-1, keepdims=True)
    spread = jnp.mean(center * center, axis=-1, keepdims=True)
    return center * lax.rsqrt(spread + 1e-05) * gain + shift


def tables(position):
    freqs = 10000.0 ** (-jnp.arange(0, HEAD, 2, dtype=jnp.float32) / HEAD)
    angles = position[:, None] * freqs[None, :]
    return (jnp.cos(angles)[:, None, :], jnp.sin(angles)[:, None, :])


def rotate(heads_in, cosine, sine):
    middle = heads_in.shape[-1] // 2
    first = heads_in[..., :middle]
    second = heads_in[..., middle:]
    return jnp.concatenate(
        [first * cosine - second * sine, second * cosine + first * sine], axis=-1
    )


def unrotate(heads_in, cosine, sine):
    middle = heads_in.shape[-1] // 2
    first = heads_in[..., :middle]
    second = heads_in[..., middle:]
    return jnp.concatenate(
        [first * cosine + second * sine, second * cosine - first * sine], axis=-1
    )


def split_heads(flat_rows):
    return flat_rows.reshape(flat_rows.shape[0], HEADS, HEAD)


def over_blocks(update, carried, count, limit):
    size = math.gcd(count, limit)

    def advance(block_idx, state):
        return update(state, block_idx * size, size)

    return lax.fori_loop(0, count // size, advance, carried)


def column_sum(matrix):
    return jnp.sum(matrix.astype(jnp.float32), axis=0)


def forward_local(sequence, weights_now, cosine, sine, group):
    (
        qkv_full,
        out_full,
        up_full,
        down_full,
        qkv_vector,
        out_vector,
        up_vector,
        down_vector,
        gain_first,
        shift_first,
        gain_second,
        shift_second,
    ) = weights_now
    rows = sequence.shape[0]
    width = sequence.shape[1]
    joined = jnp.dot(sequence, qkv_full, preferred_element_type=jnp.float32) + qkv_vector.astype(
        jnp.float32
    )
    query_flat = (
        rotate(split_heads(joined[:, :width]), cosine, sine)
        .astype(jnp.bfloat16)
        .reshape(rows, width)
    )
    keys_flat = (
        rotate(split_heads(joined[:, width : 2 * width]), cosine, sine)
        .astype(jnp.bfloat16)
        .reshape(rows, width)
    )
    values_flat = joined[:, 2 * width :].astype(jnp.bfloat16)
    query_heads = split_heads(query_flat)
    start_state = (
        jnp.full((HEADS, rows), -1e30, jnp.float32),
        jnp.zeros((HEADS, rows), jnp.float32),
        jnp.zeros((rows, HEADS, HEAD), jnp.float32),
    )
    keys_piece = lax.all_gather(keys_flat, "ctx", axis=0, tiled=True)
    values_piece = lax.all_gather(values_flat, "ctx", axis=0, tiled=True)

    def absorb_block(state, offset, size):
        running, total, accum = state
        key_block = split_heads(lax.dynamic_slice_in_dim(keys_piece, offset, size, 0))
        value_block = split_heads(lax.dynamic_slice_in_dim(values_piece, offset, size, 0))
        scores = (
            jnp.einsum("qhd,khd->hqk", query_heads, key_block, preferred_element_type=jnp.float32)
            * 0.125
        )
        highest_new = jnp.maximum(running, jnp.max(scores, axis=-1))
        factor = jnp.exp(running - highest_new)
        expo = jnp.exp(scores - highest_new[:, :, None])
        total = total * factor + jnp.sum(expo, axis=-1)
        accum = accum * factor.T[:, :, None] + jnp.einsum(
            "hqk,khd->qhd",
            expo.astype(jnp.bfloat16),
            value_block,
            preferred_element_type=jnp.float32,
        )
        return (highest_new, total, accum)

    running, total, accum = over_blocks(absorb_block, start_state, keys_piece.shape[0], group)
    attended = accum / total.T[:, :, None]
    logsum = running + jnp.log(total)
    att_low = attended.reshape(rows, width).astype(jnp.bfloat16)
    projected = jnp.dot(att_low, out_full, preferred_element_type=jnp.float32) + out_vector.astype(
        jnp.float32
    )
    resid_first = sequence.astype(jnp.float32) + projected
    hidden = layernorm(resid_first, gain_first.astype(jnp.float32), shift_first.astype(jnp.float32))
    hidden_low = hidden.astype(jnp.bfloat16)
    preact = jnp.dot(hidden_low, up_full, preferred_element_type=jnp.float32) + up_vector.astype(
        jnp.float32
    )
    activ_low = jax.nn.gelu(preact, approximate=False).astype(jnp.bfloat16)
    branch = jnp.dot(activ_low, down_full, preferred_element_type=jnp.float32) + down_vector.astype(
        jnp.float32
    )
    resid_second = hidden + branch
    output = layernorm(
        resid_second, gain_second.astype(jnp.float32), shift_second.astype(jnp.float32)
    )
    saved = (
        query_flat,
        keys_flat,
        values_flat,
        attended,
        logsum,
        att_low,
        resid_first,
        hidden_low,
        preact,
        activ_low,
        resid_second,
    )
    return (output.astype(jnp.bfloat16), saved)


def body(
    tokens,
    cotangent,
    qkv_weight,
    out_weight,
    up_weight,
    down_weight,
    qkv_bias,
    out_bias,
    up_bias,
    down_bias,
    first_gain,
    first_shift,
    second_gain,
    second_shift,
):
    gathered = (
        lax.all_gather(qkv_weight, ("ctx", "fsdp"), axis=0, tiled=True),
        lax.all_gather(out_weight, ("ctx", "fsdp"), axis=0, tiled=True),
        lax.all_gather(up_weight, ("ctx", "fsdp"), axis=0, tiled=True),
        lax.all_gather(down_weight, ("ctx", "fsdp"), axis=0, tiled=True),
        lax.all_gather(qkv_bias, ("ctx", "fsdp"), axis=0, tiled=True),
        lax.all_gather(out_bias, ("ctx", "fsdp"), axis=0, tiled=True),
        lax.all_gather(up_bias, ("ctx", "fsdp"), axis=0, tiled=True),
        lax.all_gather(down_bias, ("ctx", "fsdp"), axis=0, tiled=True),
        lax.all_gather(first_gain, ("ctx", "fsdp"), axis=0, tiled=True),
        lax.all_gather(first_shift, ("ctx", "fsdp"), axis=0, tiled=True),
        lax.all_gather(second_gain, ("ctx", "fsdp"), axis=0, tiled=True),
        lax.all_gather(second_shift, ("ctx", "fsdp"), axis=0, tiled=True),
    )
    rows = tokens.shape[2]
    width = tokens.shape[3]
    cycle_size = lax.axis_size("ctx")
    group = rows * math.gcd(cycle_size, 8)
    length = rows * cycle_size
    position = (lax.axis_index("ctx") * rows + jnp.arange(rows)).astype(jnp.float32)
    cosine, sine = tables(position)
    outputs = []
    savings = []
    for micro_idx in range(MICRO):
        output, saved = forward_local(tokens[micro_idx, 0], gathered, cosine, sine, group)
        outputs.append(output)
        savings.append(saved)
    weights_back = (
        lax.all_gather(qkv_weight, ("ctx", "fsdp"), axis=0, tiled=True),
        lax.all_gather(out_weight, ("ctx", "fsdp"), axis=0, tiled=True),
        lax.all_gather(up_weight, ("ctx", "fsdp"), axis=0, tiled=True),
        lax.all_gather(down_weight, ("ctx", "fsdp"), axis=0, tiled=True),
        lax.all_gather(qkv_bias, ("ctx", "fsdp"), axis=0, tiled=True),
        lax.all_gather(out_bias, ("ctx", "fsdp"), axis=0, tiled=True),
        lax.all_gather(up_bias, ("ctx", "fsdp"), axis=0, tiled=True),
        lax.all_gather(down_bias, ("ctx", "fsdp"), axis=0, tiled=True),
        lax.all_gather(first_gain, ("ctx", "fsdp"), axis=0, tiled=True),
        lax.all_gather(first_shift, ("ctx", "fsdp"), axis=0, tiled=True),
        lax.all_gather(second_gain, ("ctx", "fsdp"), axis=0, tiled=True),
        lax.all_gather(second_shift, ("ctx", "fsdp"), axis=0, tiled=True),
    )
    (
        qkv_full,
        out_full,
        up_full,
        down_full,
        qkv_vector,
        out_vector,
        up_vector,
        down_vector,
        gain_first,
        shift_first,
        gain_second,
        shift_second,
    ) = weights_back
    token_grads = []
    totals = []
    for micro_idx in range(MICRO):
        (
            query_flat,
            keys_flat,
            values_flat,
            attended,
            logsum,
            att_low,
            resid_first,
            hidden_low,
            preact,
            activ_low,
            resid_second,
        ) = savings[micro_idx]
        sequence = tokens[micro_idx, 0]
        grad_out = cotangent[micro_idx, 0].astype(jnp.float32)
        unused_two, second_back = jax.vjp(
            layernorm,
            resid_second,
            gain_second.astype(jnp.float32),
            shift_second.astype(jnp.float32),
        )
        grad_second, second_gain_grad, second_shift_grad = second_back(grad_out)
        branch_grad = grad_second.astype(jnp.bfloat16)
        down_bias_grad = column_sum(branch_grad)
        down_weight_grad = jnp.einsum(
            "tf,td->fd", activ_low, branch_grad, preferred_element_type=jnp.float32
        )
        activ_grad = jnp.einsum(
            "td,fd->tf", branch_grad, down_full, preferred_element_type=jnp.float32
        )
        unused_gelu, gelu_back = jax.vjp(partial(jax.nn.gelu, approximate=False), preact)
        preact_grad = gelu_back(activ_grad)[0].astype(jnp.bfloat16)
        up_bias_grad = column_sum(preact_grad)
        up_weight_grad = jnp.einsum(
            "td,tf->df", hidden_low, preact_grad, preferred_element_type=jnp.float32
        )
        hidden_grad = grad_second + jnp.einsum(
            "tf,df->td", preact_grad, up_full, preferred_element_type=jnp.float32
        )
        unused_one, first_back = jax.vjp(
            layernorm, resid_first, gain_first.astype(jnp.float32), shift_first.astype(jnp.float32)
        )
        grad_first, first_gain_grad, first_shift_grad = first_back(hidden_grad)
        proj_grad = grad_first.astype(jnp.bfloat16)
        out_bias_grad = column_sum(proj_grad)
        out_weight_grad = jnp.einsum(
            "tc,te->ce", att_low, proj_grad, preferred_element_type=jnp.float32
        )
        att_grad = jnp.einsum(
            "te,ce->tc", proj_grad, out_full, preferred_element_type=jnp.float32
        ).astype(jnp.bfloat16)
        att_heads = split_heads(att_grad)
        query_heads = split_heads(query_flat)
        delta = jnp.sum(att_heads.astype(jnp.float32) * attended, axis=-1).T
        key_all, value_all = (
            lax.all_gather(keys_flat, "ctx", axis=0, tiled=True),
            lax.all_gather(values_flat, "ctx", axis=0, tiled=True),
        )

        def query_update(state, offset, size):
            key_block = split_heads(lax.dynamic_slice_in_dim(key_all, offset, size, 0))
            value_block = split_heads(lax.dynamic_slice_in_dim(value_all, offset, size, 0))
            scores = (
                jnp.einsum(
                    "qhd,khd->hqk", query_heads, key_block, preferred_element_type=jnp.float32
                )
                * 0.125
            )
            chance = jnp.exp(scores - logsum[:, :, None])
            dprob = jnp.einsum(
                "qhd,khd->hqk", att_heads, value_block, preferred_element_type=jnp.float32
            )
            score_grad = (chance * (dprob - delta[:, :, None])).astype(jnp.bfloat16)
            return state + jnp.einsum(
                "hqk,khd->qhd", score_grad, key_block, preferred_element_type=jnp.float32
            )

        query_grad = (
            over_blocks(query_update, jnp.zeros((rows, HEADS, HEAD), jnp.float32), length, group)
            * 0.125
        )

        def fill(state, offset, size):
            key_block = split_heads(lax.dynamic_slice_in_dim(key_all, offset, size, 0))
            value_block = split_heads(lax.dynamic_slice_in_dim(value_all, offset, size, 0))
            scores = (
                jnp.einsum(
                    "qhd,khd->hqk", query_heads, key_block, preferred_element_type=jnp.float32
                )
                * 0.125
            )
            chance = jnp.exp(scores - logsum[:, :, None])
            value_part = jnp.einsum(
                "hqk,qhd->khd",
                chance.astype(jnp.bfloat16),
                att_heads,
                preferred_element_type=jnp.float32,
            )
            dprob = jnp.einsum(
                "qhd,khd->hqk", att_heads, value_block, preferred_element_type=jnp.float32
            )
            score_grad = (chance * (dprob - delta[:, :, None])).astype(jnp.bfloat16)
            key_part = (
                jnp.einsum(
                    "hqk,qhd->khd", score_grad, query_heads, preferred_element_type=jnp.float32
                )
                * 0.125
            )
            piece = jnp.concatenate(
                [key_part.reshape(size, width), value_part.reshape(size, width)], axis=1
            )
            return lax.dynamic_update_slice_in_dim(state, piece, offset, 0)

        combined = lax.psum_scatter(
            over_blocks(
                fill,
                jnp.zeros((lax.axis_size("ctx") * rows, 2 * width), jnp.float32),
                lax.axis_size("ctx") * rows,
                group,
            ),
            "ctx",
            scatter_dimension=0,
            tiled=True,
        )
        key_grad = split_heads(combined[:, :width])
        value_grad = combined[:, width:]
        joined_grad = jnp.concatenate(
            [
                unrotate(query_grad, cosine, sine).reshape(rows, width),
                unrotate(key_grad, cosine, sine).reshape(rows, width),
                value_grad,
            ],
            axis=1,
        ).astype(jnp.bfloat16)
        qkv_bias_grad = column_sum(joined_grad)
        qkv_weight_grad = jnp.einsum(
            "tc,te->ce", sequence, joined_grad, preferred_element_type=jnp.float32
        )
        token_grads.append(
            grad_first
            + jnp.einsum("te,ce->tc", joined_grad, qkv_full, preferred_element_type=jnp.float32)
        )
        fresh = [
            qkv_weight_grad,
            out_weight_grad,
            up_weight_grad,
            down_weight_grad,
            qkv_bias_grad,
            out_bias_grad,
            up_bias_grad,
            down_bias_grad,
            first_gain_grad,
            first_shift_grad,
            second_gain_grad,
            second_shift_grad,
        ]
        if micro_idx == 0:
            totals = fresh
        else:
            totals = [older + newer for older, newer in zip(totals, fresh)]
    summed = (
        lax.psum_scatter(totals[0], ("ctx", "fsdp"), scatter_dimension=0, tiled=True),
        lax.psum_scatter(totals[1], ("ctx", "fsdp"), scatter_dimension=0, tiled=True),
        lax.psum_scatter(totals[2], ("ctx", "fsdp"), scatter_dimension=0, tiled=True),
        lax.psum_scatter(totals[3], ("ctx", "fsdp"), scatter_dimension=0, tiled=True),
        lax.psum_scatter(totals[4], ("ctx", "fsdp"), scatter_dimension=0, tiled=True),
        lax.psum_scatter(totals[5], ("ctx", "fsdp"), scatter_dimension=0, tiled=True),
        lax.psum_scatter(totals[6], ("ctx", "fsdp"), scatter_dimension=0, tiled=True),
        lax.psum_scatter(totals[7], ("ctx", "fsdp"), scatter_dimension=0, tiled=True),
        lax.psum_scatter(totals[8], ("ctx", "fsdp"), scatter_dimension=0, tiled=True),
        lax.psum_scatter(totals[9], ("ctx", "fsdp"), scatter_dimension=0, tiled=True),
        lax.psum_scatter(totals[10], ("ctx", "fsdp"), scatter_dimension=0, tiled=True),
        lax.psum_scatter(totals[11], ("ctx", "fsdp"), scatter_dimension=0, tiled=True),
    )
    output_all = jnp.stack(outputs)[:, None]
    token_all = jnp.stack(token_grads)[:, None]
    return (
        output_all,
        token_all,
        summed[0],
        summed[1],
        summed[2],
        summed[3],
        summed[4],
        summed[5],
        summed[6],
        summed[7],
        summed[8],
        summed[9],
        summed[10],
        summed[11],
    )


def solution(mesh):
    in_specs = (
        P(None, "fsdp", "ctx", None),
        P(None, "fsdp", "ctx", None),
        P(("ctx", "fsdp"), None),
        P(("ctx", "fsdp"), None),
        P(("ctx", "fsdp"), None),
        P(("ctx", "fsdp"), None),
        P(("ctx", "fsdp")),
        P(("ctx", "fsdp")),
        P(("ctx", "fsdp")),
        P(("ctx", "fsdp")),
        P(("ctx", "fsdp")),
        P(("ctx", "fsdp")),
        P(("ctx", "fsdp")),
        P(("ctx", "fsdp")),
    )
    out_specs = (
        P(None, "fsdp", "ctx", None),
        P(None, "fsdp", "ctx", None),
        P(("ctx", "fsdp"), None),
        P(("ctx", "fsdp"), None),
        P(("ctx", "fsdp"), None),
        P(("ctx", "fsdp"), None),
        P(("ctx", "fsdp")),
        P(("ctx", "fsdp")),
        P(("ctx", "fsdp")),
        P(("ctx", "fsdp")),
        P(("ctx", "fsdp")),
        P(("ctx", "fsdp")),
        P(("ctx", "fsdp")),
        P(("ctx", "fsdp")),
    )
    return jax.shard_map(body, mesh=mesh, in_specs=in_specs, out_specs=out_specs, check_vma=False)
```

profile of v0, /device:TPU:0, one launch (start us, length us, event | category | flops | bytes accessed | tf_op | source)
XLA Modules:
  0.0 1800.7 jit_solution(3959227239183322083)
XLA Ops:
  13.9 42.5 %all-reduce.16 = (bf16[3072]{0:T(1024)(128)(2,1)S(1)}, bf16[1024]{0:T(1024)(128)(2,1)S(1)}, bf16[1024]{0:T(1024)(128)(2,1)S(1)}, bf16[1024]{0:T(1024)(128)(2,1)S...) all-reduce(bf16[3072]{0:T(1024)(128)(2,1)S(1)} %dynamic-update-slic, ...), channel_id=1, replica_groups=mesh['ctx'=16,'fsdp'=2] {'ctx','fsdp'}, use_global_device_ids=true, to_apply=%add | all-reduce | flops 9216 | bytes 36864
  56.6 26.7 %all-gather.10.cloned.1.call-done = bf16[1024,3072]{1,0:T(8,128)(2,1)} async-done(((bf16[32,3072]{1,0:T(8,128)(2,1)}), bf16[1024,3072]{1,0:T(8,128)(2,1)}) %all-gather.10.cloned.1.call-update) | async-done | bytes 6291472 | tf_op jit(solution)/shard_map/all_gather | solution.py:175
  83.2 4.1 convolution_add_fusion.5
  88.3 4.0 convolution_add_fusion.4
  102.8 65.8 %all-gather = bf16[32,1,128]{2,1,0:T(2,128)(2,1)S(1)} all-gather(bf16[1,1,128]{2,1,0:T(2,128)(2,1)S(1)} %bitcast.381), channel_id=1, replica_groups=mesh['ctx'=16,'fsdp'=2] {'ctx','fsdp'}, dimensions={0}, use_global_device_ids=true | all-gather | bytes 8448 | tf_op jit(solution)/shard_map/all_gather | solution.py:181
  170.0 4.0 copy.99
  173.9 6.7 all-gather.24.cloned.1.call-done
  180.7 3.9 copy.101
  184.6 38.3 %all-gather.12.cloned.1.call-done = bf16[1024,1024]{1,0:T(8,128)(2,1)} async-done(((bf16[64,1024]{1,0:T(8,128)(2,1)}), bf16[1024,1024]{1,0:T(8,128)(2,1)}) %all-gather.12.cloned.1.call-update) | async-done | bytes 2097168 | tf_op jit(solution)/shard_map/all_gather | solution.py:98
  222.9 4.0 copy.91
  226.8 38.3 %all-gather.14.cloned.1.call-done = bf16[1024,1024]{1,0:T(8,128)(2,1)} async-done(((bf16[64,1024]{1,0:T(8,128)(2,1)}), bf16[1024,1024]{1,0:T(8,128)(2,1)}) %all-gather.14.cloned.1.call-update) | async-done | bytes 2097168 | tf_op jit(solution)/shard_map/all_gather | solution.py:99
  265.1 3.9 copy.93
  269.0 9.6 while.93
  279.8 43.4 %all-gather.16.cloned.1.call-done = bf16[1024,1024]{1,0:T(8,128)(2,1)} async-done(((bf16[32,1024]{1,0:T(8,128)(2,1)}), bf16[1024,1024]{1,0:T(8,128)(2,1)}) %all-gather.16.cloned.1.call-update) | async-done | bytes 2097168 | tf_op jit(solution)/shard_map/all_gather | solution.py:176
  326.3 9.5 while.92
  339.7 62.8 %all-gather.18.cloned.1.call-done = bf16[1024,4096]{1,0:T(8,128)(2,1)} async-done(((bf16[32,4096]{1,0:T(8,128)(2,1)}), bf16[1024,4096]{1,0:T(8,128)(2,1)}) %all-gather.18.cloned.1.call-update) | async-done | bytes 8388624 | tf_op jit(solution)/shard_map/all_gather | solution.py:177
  402.5 6.6 multiply_convert_fusion.4
  409.2 72.2 %all-gather.20.cloned.1.call-done = bf16[4096,1024]{1,0:T(8,128)(2,1)} async-done(((bf16[128,1024]{1,0:T(8,128)(2,1)}), bf16[4096,1024]{1,0:T(8,128)(2,1)}) %all-gather.20.cloned.1.call-update) | async-done | bytes 8388624 | tf_op jit(solution)/shard_map/all_gather | solution.py:178
  481.4 5.2 fusion.119
  487.2 3.7 multiply_convert_fusion.5
  496.3 3.4 convert_reduce_fusion.2
  499.7 2.7 convolution_add_fusion.11
  502.4 3.6 convert_reduce_fusion.3
  506.0 3.4 multiply_reduce_fusion.3
  513.9 4.3 broadcast.428.clone2.1
  518.3 39.3 %while.90 = (s32[]{:T(128)}, f32[1024,2048]{1,0:T(8,128)}, bf16[1024,1024]{0,1:T(8,128)(2,1)}, bf16[64,16,64]{0,2,1:T(8,128)(2,1)}, f32[16,64]{1,0:T(8,128)S(1)}...) while((s32[]{:T(128)}, f32[1024,2048]{1,0:T(8,128)}, ...), condition=%wide.region_24.0_spmd, body=%wide.region_23.0_spmd.sunk | while | flops 274202624 | bytes 51392740 | solution.py:54
  520.5 3.3 convolution_multiply_fusion.4
  527.8 5.4 copy.191
  533.2 4.7 constant_dynamic-update-slice_fusion.4
  540.2 3.3 convolution_multiply_fusion.4
  547.5 5.4 copy.191
  552.9 4.6 constant_dynamic-update-slice_fusion.4
  561.2 4.7 broadcast.428.clone2
  565.9 40.6 %while.91 = (s32[]{:T(128)}, f32[1024,2048]{1,0:T(8,128)}, bf16[1024,1024]{0,1:T(8,128)(2,1)}, bf16[64,16,64]{0,2,1:T(8,128)(2,1)}, f32[16,64]{1,0:T(8,128)S(1)}...) while((s32[]{:T(128)}, f32[1024,2048]{1,0:T(8,128)}, ...), condition=%wide.region_34.0_spmd, body=%wide.region_33.0_spmd.sunk | while | flops 274202624 | bytes 51392740 | solution.py:54
  568.6 3.4 convolution_multiply_fusion.5
  576.2 5.7 copy.192
  581.9 4.7 constant_dynamic-update-slice_fusion.5
  589.0 3.4 convolution_multiply_fusion.5
  596.4 5.4 copy.192
  601.8 4.7 constant_dynamic-update-slice_fusion.5
  608.2 2.7 convolution_add_fusion.6
  613.4 12.8 while.95
  613.4 2.7 constant_dynamic-slice_fusion.23
  616.5 3.1 fusion.285
  619.7 2.8 constant_dynamic-slice_fusion.23
  622.8 3.3 fusion.285
  628.1 12.5 while.94
  628.1 2.7 constant_dynamic-slice_fusion.22
  631.2 3.1 fusion.278
  634.3 2.7 constant_dynamic-slice_fusion.22
  637.4 3.2 fusion.278
  641.7 19.3 %reduce-scatter.19.cloned.1.call-done = f32[64,2048]{1,0:T(8,128)} async-done(((f32[1024,2048]{1,0:T(8,128)}), f32[64,2048]{1,0:T(8,128)}) %reduce-scatter.19.cloned.1.call-update) | async-done | bytes 524304
  662.2 107.2 %reduce-scatter.21.cloned.1.call-done = f32[64,2048]{1,0:T(8,128)} async-done(((f32[1024,2048]{1,0:T(8,128)}), f32[64,2048]{1,0:T(8,128)}) %reduce-scatter.21.cloned.1.call-update) | async-done | bytes 524304
  775.6 6.4 add_bitcast_fusion
  782.0 12.6 copy.137
  798.3 8.2 convolution_add_fusion.1
  809.9 8.1 convolution_add_fusion
  820.7 41.8 %all-reduce.15 = (f32[3072]{0:T(1024)S(1)}, f32[1024]{0:T(1024)S(1)}, f32[4096]{0:T(1024)S(1)}, f32[1024]{0:T(1024)S(1)}, f32[1024]{0:T(1024)S(1)}, /*index=5*/f...) all-reduce(f32[3072]{0:T(1024)S(1)} %add.494, ...), channel_id=8, replica_groups=mesh['ctx'=16,'fsdp'=2] {'ctx','fsdp'}, use_global_device_ids=true, to_apply=%region_42.0.clone | all-reduce | flops 13312 | bytes 106496
  867.2 4.9 fusion.55
  872.1 4.9 fusion.54
  877.8 36.4 %reduce-scatter.13.cloned.1.call-done = f32[32,1024]{1,0:T(8,128)} async-done(((f32[1024,1024]{1,0:T(8,128)}), f32[32,1024]{1,0:T(8,128)}) %reduce-scatter.13.cloned.1.call-update) | async-done | bytes 131088 | tf_op jit(solution)/shard_map/reduce_scatter | solution.py:394
  914.1 159.0 %reduce-scatter.23.cloned.1.call-done = f32[32,3072]{1,0:T(8,128)} async-done(((f32[1024,3072]{1,0:T(8,128)}), f32[32,3072]{1,0:T(8,128)}) %reduce-scatter.23.cloned.1.call-update) | async-done | bytes 393232
  1073.1 359.4 %reduce-scatter.15.cloned.1.call-done = f32[32,4096]{1,0:T(8,128)} async-done(((f32[1024,4096]{1,0:T(8,128)}), f32[32,4096]{1,0:T(8,128)}) %reduce-scatter.15.cloned.1.call-update) | async-done | bytes 524304 | tf_op jit(solution)/shard_map/reduce_scatter | solution.py:395
  1432.5 361.5 %reduce-scatter.17.cloned.1.call-done = f32[128,1024]{1,0:T(8,128)} async-done(((f32[4096,1024]{1,0:T(8,128)}), f32[128,1024]{1,0:T(8,128)}) %reduce-scatter.17.cloned.1.call-update) | async-done | bytes 524304 | tf_op jit(solution)/shard_map/reduce_scatter | solution.py:396
  (417 shorter events, 116.4 us)
Async XLA Ops:
  7.2 76.1 %all-gather.10.cloned.1.call-start = ((), (), s32[]{:S(2)}) async-start(), calls=%async_computation.6 | async-start | bytes 6488064 | tf_op jit(solution)/shard_map/all_gather | solution.py:175
  7.9 162.0 %all-gather.22.cloned.1.call-start = ((), (), s32[]{:S(2)}) async-start(), calls=%async_computation.12 | async-start | bytes 2228224 | tf_op jit(solution)/shard_map/all_gather | solution.py:98
  56.6 38.6 %copy-start.66 = (f32[64,32]{0,1:T(8,128)}, f32[64,32]{0,1:T(8,128)S(1)}, u32[]{:S(2)}) copy-start(f32[64,32]{0,1:T(8,128)S(1)} %get-tuple-element.1321) | copy-start | bytes 24580
  56.6 38.6 %copy-start.68 = (f32[64,32]{0,1:T(8,128)}, f32[64,32]{0,1:T(8,128)S(1)}, u32[]{:S(2)}) copy-start(f32[64,32]{0,1:T(8,128)S(1)} %get-tuple-element.1322) | copy-start | bytes 24580
  97.2 5.6 copy-start.94
  97.2 71.5 %copy-start.62 = (bf16[64,16,32]{0,2,1:T(8,128)(2,1)S(1)}, bf16[64,16,32]{0,2,1:T(8,128)(2,1)}, u32[]{:S(2)}) copy-start(bf16[64,16,32]{0,2,1:T(8,128)(2,1)} %get-tuple-element.1312) | copy-start | bytes 196612
  97.3 71.5 %copy-start.63 = (bf16[64,16,32]{0,2,1:T(8,128)(2,1)S(1)}, bf16[64,16,32]{0,2,1:T(8,128)(2,1)}, u32[]{:S(2)}) copy-start(bf16[64,16,32]{0,2,1:T(8,128)(2,1)} %get-tuple-element.1313) | copy-start | bytes 196612
  97.3 72.4 %copy-start.60 = (bf16[64,16,32]{0,2,1:T(8,128)(2,1)S(1)}, bf16[64,16,32]{0,2,1:T(8,128)(2,1)}, u32[]{:S(2)}) copy-start(bf16[64,16,32]{0,2,1:T(8,128)(2,1)} %get-tuple-element.1291) | copy-start | bytes 196612
  97.3 72.4 %copy-start.61 = (bf16[64,16,32]{0,2,1:T(8,128)(2,1)S(1)}, bf16[64,16,32]{0,2,1:T(8,128)(2,1)}, u32[]{:S(2)}) copy-start(bf16[64,16,32]{0,2,1:T(8,128)(2,1)} %get-tuple-element.1292) | copy-start | bytes 196612
  98.2 82.4 %all-gather.24.cloned.1.call-start = ((), (), s32[]{:S(2)}) async-start(), calls=%async_computation.13 | async-start | bytes 2228224 | tf_op jit(solution)/shard_map/all_gather | solution.py:99
  99.0 123.9 %all-gather.12.cloned.1.call-start = ((), (), s32[]{:S(2)}) async-start(), calls=%async_computation.7 | async-start | bytes 2228224 | tf_op jit(solution)/shard_map/all_gather | solution.py:98
  99.8 165.3 %all-gather.14.cloned.1.call-start = ((), (), s32[]{:S(2)}) async-start(), calls=%async_computation.8 | async-start | bytes 2228224 | tf_op jit(solution)/shard_map/all_gather | solution.py:99
  100.6 222.7 %all-gather.16.cloned.1.call-start = ((), (), s32[]{:S(2)}) async-start(), calls=%async_computation.9 | async-start | bytes 2162688 | tf_op jit(solution)/shard_map/all_gather | solution.py:176
  101.2 301.4 %all-gather.18.cloned.1.call-start = ((), (), s32[]{:S(2)}) async-start(), calls=%async_computation.10 | async-start | bytes 8650752 | tf_op jit(solution)/shard_map/all_gather | solution.py:177
  101.9 379.5 %all-gather.20.cloned.1.call-start = ((), (), s32[]{:S(2)}) async-start(), calls=%async_computation.11 | async-start | bytes 8650752 | tf_op jit(solution)/shard_map/all_gather | solution.py:178
  102.7 558.4 %reduce-scatter.19.cloned.1.call-start = ((), (), s32[]{:S(2)}) async-start(), calls=%async_computation.17 | async-start | bytes 8912896
  102.8 406.6 %copy-start.54 = (f32[1024]{0:T(1024)}, f32[1024]{0:T(1024)S(1)}, u32[]{:S(2)}) copy-start(f32[1024]{0:T(1024)S(1)} %convert_element_type.218) | copy-start | bytes 12292
  102.8 388.1 %copy-start.64 = (f32[1024]{0:T(1024)}, f32[1024]{0:T(1024)S(1)}, u32[]{:S(2)}) copy-start(f32[1024]{0:T(1024)S(1)} %convert_element_type.219) | copy-start | bytes 12292
  168.8 5.1 copy-start.2
  169.7 4.2 copy-start.4
  278.7 279.5 %copy-start.56 = (f32[16,64]{1,0:T(8,128)}, f32[16,64]{1,0:T(8,128)S(1)}, u32[]{:S(2)}) copy-start(f32[16,64]{1,0:T(8,128)S(1)} %get-tuple-element.825) | copy-start | bytes 12292
  279.8 46.5 %copy-start.30 = (bf16[64,16,64]{0,2,1:T(8,128)(2,1)}, bf16[64,16,64]{0,2,1:T(8,128)(2,1)S(1)}, u32[]{:S(2)}) copy-start(bf16[64,16,64]{0,2,1:T(8,128)(2,1)S(1)} %fusion.87) | copy-start | bytes 393220
  325.4 184.0 %copy-start.72 = (f32[64]{0:T(128)}, f32[64]{0:T(128)S(1)}, u32[]{:S(2)}) copy-start(f32[64]{0:T(128)S(1)} %broadcast_multiply_fusion.3) | copy-start | bytes 772
  335.9 73.3 %copy-start.9 = (bf16[64,16,64]{2,0,1:T(8,128)(2,1)}, bf16[64,16,64]{2,0,1:T(8,128)(2,1)S(1)}, u32[]{:S(2)}) copy-start(bf16[64,16,64]{2,0,1:T(8,128)(2,1)S(1)} %get-tuple-element.1896) | copy-start | bytes 393220
  335.9 66.6 %copy-start.16 = (f32[64,1024]{1,0:T(8,128)S(1)}, f32[64,1024]{1,0:T(8,128)}, u32[]{:S(2)}) copy-start(f32[64,1024]{1,0:T(8,128)} %copy-done.15) | copy-start | bytes 786436
  337.1 65.4 %copy-start.32 = (bf16[64,16,64]{0,2,1:T(8,128)(2,1)}, bf16[64,16,64]{0,2,1:T(8,128)(2,1)S(1)}, u32[]{:S(2)}) copy-start(bf16[64,16,64]{0,2,1:T(8,128)(2,1)S(1)} %fusion.86) | copy-start | bytes 393220
  339.4 170.0 %copy-start.18 = (f32[64,1024]{1,0:T(8,128)}, f32[64,1024]{1,0:T(8,128)S(1)}, u32[]{:S(2)}) copy-start(f32[64,1024]{1,0:T(8,128)S(1)} %get-tuple-element.1324) | copy-start | bytes 786436
  339.4 170.0 %copy-start.74 = (f32[64]{0:T(128)}, f32[64]{0:T(128)S(1)}, u32[]{:S(2)}) copy-start(f32[64]{0:T(128)S(1)} %broadcast_multiply_fusion.5) | copy-start | bytes 772
  339.6 169.8 %copy-start.86 = (f32[64]{0:T(128)}, f32[64]{0:T(128)S(1)}, u32[]{:S(2)}) copy-start(f32[64]{0:T(128)S(1)} %fusion.101) | copy-start | bytes 772
  339.7 169.8 %copy-start.88 = (f32[64]{0:T(128)}, f32[64]{0:T(128)S(1)}, u32[]{:S(2)}) copy-start(f32[64]{0:T(128)S(1)} %fusion.99) | copy-start | bytes 772
  409.2 77.5 %copy-start.20 = (bf16[64,4096]{1,0:T(8,128)(2,1)}, bf16[64,4096]{1,0:T(8,128)(2,1)S(1)}, u32[]{:S(2)}) copy-start(bf16[64,4096]{1,0:T(8,128)(2,1)S(1)} %get-tuple-element.1261) | copy-start | bytes 1572868
  481.4 5.8 copy-start.6
  481.4 9.5 slice-start
  487.2 3.8 slice-start.1
  495.6 6.8 copy-start.45
  496.3 3.4 copy-start.47
  506.0 3.4 copy-start.26
  506.0 6.6 copy-start.7
  510.5 3.3 copy-start.13
  510.5 3.4 copy-start.90
  513.5 4.8 copy-start.38
  558.2 211.2 %reduce-scatter.21.cloned.1.call-start = ((), (), s32[]{:S(2)}) async-start(), calls=%async_computation.18 | async-start | bytes 8912896
  560.2 5.7 copy-start.40
  606.6 307.5 %reduce-scatter.13.cloned.1.call-start = ((), (), s32[]{:S(2)}) async-start(), calls=%async_computation.14 | async-start | bytes 4325376 | tf_op jit(solution)/shard_map/reduce_scatter | solution.py:394
  610.9 462.2 %reduce-scatter.23.cloned.1.call-start = ((), (), s32[]{:S(2)}) async-start(), calls=%async_computation.19 | async-start | bytes 12976128
  613.4 14.7 copy-start.10
  613.4 14.7 copy-start.52
  613.4 2.7 copy-start.12
  619.7 2.8 copy-start.12
  641.7 131.2 %copy-start.44 = (f32[64,16,64]{0,2,1:T(8,128)S(1)}, f32[64,16,64]{0,2,1:T(8,128)}, u32[]{:S(2)}) copy-start(f32[64,16,64]{0,2,1:T(8,128)} %broadcast_multiply_fusion) | copy-start | bytes 786436
  641.7 131.2 %copy-start.67 = (f32[64,32]{0,1:T(8,128)S(1)}, f32[64,32]{0,1:T(8,128)}, u32[]{:S(2)}) copy-start(f32[64,32]{0,1:T(8,128)} %copy-done.66) | copy-start | bytes 24580
  641.7 131.2 %copy-start.69 = (f32[64,32]{0,1:T(8,128)S(1)}, f32[64,32]{0,1:T(8,128)}, u32[]{:S(2)}) copy-start(f32[64,32]{0,1:T(8,128)} %copy-done.68) | copy-start | bytes 24580
  794.7 3.5 copy-start.17
  794.7 3.5 copy-start.25
  794.7 3.5 copy-start.73
  794.7 3.5 copy-start.87
  794.7 637.8 %reduce-scatter.15.cloned.1.call-start = ((), (), s32[]{:S(2)}) async-start(), calls=%async_computation.15 | async-start | bytes 17301504 | tf_op jit(solution)/shard_map/reduce_scatter | solution.py:395
  806.5 3.4 copy-start.21
  806.5 3.4 copy-start.48
  806.5 987.5 %reduce-scatter.17.cloned.1.call-start = ((), (), s32[]{:S(2)}) async-start(), calls=%async_computation.16 | async-start | bytes 17301504 | tf_op jit(solution)/shard_map/reduce_scatter | solution.py:396
  818.2 48.9 %copy-start.37 = (f32[64,1024]{1,0:T(8,128)S(1)}, f32[64,1024]{1,0:T(8,128)}, u32[]{:S(2)}) copy-start(f32[64,1024]{1,0:T(8,128)} %copy-done.36) | copy-start | bytes 786436
  818.2 48.9 %copy-start.91 = (f32[64]{0:T(128)S(1)}, f32[64]{0:T(128)}, u32[]{:S(2)}) copy-start(f32[64]{0:T(128)} %copy-done.90) | copy-start | bytes 772
  867.2 4.9 copy-start.35
  867.2 4.9 copy-start.93
  (53 other events, 70.1 us)
Sparse Core Ops, SparseCore 0:
  10.9 72.2 all-gather.9
  98.4 39.8 all-gather.21
  140.5 40.1 all-gather.23
  182.7 40.1 all-gather.11
  224.9 40.1 all-gather.13
  267.9 55.2 all-gather.15
  326.2 76.2 all-gather.17
  405.5 75.8 all-gather.19
  557.7 103.2 reduce-scatter.18
  664.9 104.4 reduce-scatter.20
  772.3 141.8 reduce-scatter.12
  920.6 152.5 reduce-scatter.22
  1076.1 356.3 reduce-scatter.14
  1435.4 358.5 reduce-scatter.16
where the time goes:
time: 1810 us; the launch traced here: 1800 us
  waiting for transfers between devices  1330 us (73%)
  blocking collectives  150 us (8%)
  local copies, waits for them, and re-layouts  141 us (8%)
  matrix products  128 us (7%)
  other arithmetic  30.4 us (2%)
    reduce_scatter x1, waiting for transfers between devices, body(): lax.psum_scatter(totals[3], ('ctx', 'fsdp'), scatter_dimension=0, tiled=T...  361 us
    reduce_scatter x1, waiting for transfers between devices, body(): lax.psum_scatter(totals[2], ('ctx', 'fsdp'), scatter_dimension=0, tiled=T...  359 us
    unnamed x17, waiting for transfers between devices  288 us
    unnamed x2, blocking collectives  84.3 us
    all_gather x1, waiting for transfers between devices, body(): lax.all_gather(down_weight, ('ctx', 'fsdp'), axis=0, tiled=True)  72.2 us
    all_gather x1, blocking collectives, body(): lax.all_gather(up_bias, ('ctx', 'fsdp'), axis=0, tiled=True)  65.8 us
    all_gather x1, waiting for transfers between devices, body(): lax.all_gather(up_weight, ('ctx', 'fsdp'), axis=0, tiled=True)  62.8 us
    unnamed x217, local copies, waits for them, and re-layouts  50.7 us
  transfers between devices with their start and end apart: 14, of which 13 were waited for; matrix products, arithmetic and copies ran while one was open for 11% of the time, Pallas kernels for 0%

commit v1 on v0

--- a/solution.py
+++ b/solution.py
@@ -4,11 +4,702 @@
 import jax
 import jax.numpy as jnp
 from jax import lax
+from jax.experimental import pallas as pl
+from jax.experimental.pallas import tpu as pltpu
 from jax.sharding import PartitionSpec as P
+import numpy as np
 
 HEADS = 16
 HEAD = 64
 MICRO = 2
+MESH = pl.DeviceIdType.MESH
+F32 = jnp.float32
+BF16 = jnp.bfloat16
+
+
+NCTX = 16
+NCHIP = 8
+BLK = 64
+D = 1024
+UNITS = 256
+CHUNK = 256
+
+
+def chip_at(place):
+    row = lax.div(place, 4)
+    return ((1 - row) * place + row * (7 - place)) * 2 + row
+
+
+def nn(a, b):
+    return jnp.dot(a, b, preferred_element_type=F32)
+
+
+def nt(a, b):
+    return lax.dot_general(a, b, (((1,), (1,)), ((), ())), preferred_element_type=F32)
+
+
+def tn(a, b):
+    return lax.dot_general(a, b, (((0,), (0,)), ((), ())), preferred_element_type=F32)
+
+
+def row_mean(v):
+    return jnp.sum(v, axis=1, keepdims=True) * (1.0 / D)
+
+
+def col_sum(v):
+    return jnp.sum(v, axis=0, keepdims=True)
+
+
+def layer_kernel(
+    x_ref, ct_ref, wq_ref, wo_ref, wu_ref, wd_ref, vec_ref, rope_ref,
+    out_ref, tg_ref, gq_ref, go_ref, gu_ref, gd_ref, gs_ref, gb_ref,
+    XF, HF, BG, WP, WB, WO, WD, VB, VF, UB, QBR, BQ, WHT, QT, KT, VT, KN, VN, PT, ATD, ATS, AT, AGT,
+    H1, Z1, R1, SEC, G2, DG, ACT, PG, PB, SS, SR, RSD, RR, TT, TMP,
+    GU, XSU, XRU, AU, RU, GD, XSD, XRD, GO, XSO, XRO, SSO, SRO, PO, RO, SG, SGR, SGT, SGC, AGQ,
+    DK, DV, JG, XSQ, XRQ, AQ, RQ, QB1, QB2, QB3,
+    agx_s, agx_r, sbx_s, sbx_r, ag_s, ag_r, sb_s, sb_r, ss_s, ss_r, rs_s, rs_r, wo_s, wo_r, wos_s, wos_r,
+    all_s, all_r, pair_s, pair_r, po_s, po_r,
+):
+    c = lax.axis_index("ctx")
+    f = lax.axis_index("fsdp")
+    core = lax.rem(c, 2)
+    chip = lax.div(c, 2)
+    yy = lax.rem(chip, 2)
+    zz = lax.div(chip, 2)
+    r = (1 - yy) * zz + yy * (7 - zz)
+    nxt = chip_at(lax.rem(r + 1, 8)) * 2 + core
+    prv = chip_at(lax.rem(r + 7, 8)) * 2 + core
+    sib = c + 1 - 2 * core
+    mine = pl.multiple_of(core * BLK, BLK)
+    other = pl.multiple_of((1 - core) * BLK, BLK)
+    lane = lax.broadcasted_iota(jnp.int32, (1, 128), 1)
+    low_half = lane < 64
+
+    def remote(src, dst, ss, rs, axis, to):
+        return pltpu.make_async_remote_copy(
+            src_ref=src, dst_ref=dst, send_sem=ss, recv_sem=rs, device_id={axis: to}, device_id_type=MESH
+        )
+
+    def target(d):
+        return nxt if d == 0 else prv
+
+    def chip_of(d, k):
+        return chip_at(lax.rem(r - k + 8, 8) if d == 0 else lax.rem(r + k, 8))
+
+    def send_all(e, src_at, dst):
+        @pl.loop(1, NCTX)
+        def _(o):
+            to = lax.rem(c + o, NCTX)
+            remote(src_at(to), dst, all_s.at[e, o], all_r.at[e, o], "ctx", to).start()
+
+    def recv_all(e, dst_at):
+        @pl.loop(1, NCTX)
+        def _(o):
+            at = dst_at(lax.rem(c + NCTX - o, NCTX))
+            remote(at, at, all_s.at[e, o], all_r.at[e, o], "ctx", sib).wait_recv()
+
+    def sent_all(e, src_at):
+        @pl.loop(1, NCTX)
+        def _(o):
+            at = src_at(lax.rem(c + o, NCTX))
+            remote(at, at, all_s.at[e, o], all_r.at[e, o], "ctx", sib).wait_send()
+
+    def pair(i, src, dst):
+        return remote(src, dst, pair_s.at[i], pair_r.at[i], "fsdp", 1 - f)
+
+    barrier = pltpu.get_barrier_semaphore()
+
+    @pl.loop(1, NCTX)
+    def _(o):
+        pl.semaphore_signal(barrier, inc=1, device_id={"ctx": lax.rem(c + o, NCTX)}, device_id_type=MESH)
+
+    pl.semaphore_signal(barrier, inc=1, device_id={"fsdp": 1 - f}, device_id_type=MESH)
+    pl.semaphore_wait(barrier, NCTX)
+
+    def block(buf, m, ch, row0):
+        return buf.at[m, ch, pl.ds(row0, BLK)]
+
+    def sub(m, ch, q):
+        return XF.at[m, ch, pl.ds(pl.multiple_of(core * BLK + 16 * q, 16), 16)]
+
+    for m in range(2):
+        XF[m, chip, pl.ds(mine, BLK)] = x_ref[m]
+    WO[c, f] = wo_ref[...]
+    WD[f] = wd_ref[...]
+    VB[c, f] = vec_ref[...]
+
+    def gather_x(k):
+        for d in range(2):
+            ch = chip_of(d, k)
+            for q in range(4):
+                at = sub(d, ch, q)
+
+                @pl.when(k > 0)
+                def _():
+                    remote(at, at, agx_s.at[d, 0], agx_r.at[d, (k - 1) * 4 + q], "ctx", target(d)).wait_recv()
+
+                @pl.when(k < 7)
+                def _():
+                    remote(at, at, agx_s.at[d, k * 4 + q], agx_r.at[d, k * 4 + q], "ctx", target(d)).start()
+
+            whole = block(XF, d, ch, mine)
+            remote(whole, whole, sbx_s.at[d, k], sbx_r.at[d, k], "ctx", sib).start()
+
+    pl.loop(0, 1)(gather_x)
+    pair(0, vec_ref, VB.at[c, f]).start()
+    pair(1, wo_ref, WO.at[c, f]).start()
+    pair(2, wd_ref, WD.at[f]).start()
+
+    for j in range(8):
+        qt = wq_ref[:, 128 * j : 128 * j + 128].astype(F32)
+        kt = wq_ref[:, D + 128 * j : D + 128 * j + 128].astype(F32)
+        vt = wq_ref[:, 2 * D + 128 * j : 2 * D + 128 * j + 128].astype(F32)
+        for e in range(2):
+            w = 2 * j + e
+            WP[w, :, 0:256] = wu_ref[:, 256 * w : 256 * w + 256]
+            qk = jnp.where(low_half, qt, pltpu.roll(kt, 64, 1)) if e == 0 else jnp.where(low_half, pltpu.roll(qt, 64, 1), kt)
+            WP[w, :, 256:384] = qk.astype(BF16)
+            WP[w, :, 384:512] = (vt if e == 0 else pltpu.roll(vt, 64, 1)).astype(BF16)
+    WB[c, f] = WP[c]
+    send_all(0, lambda to: WP.at[to], WB.at[c, f])
+    pl.loop(1, 5)(gather_x)
+    pair(0, VB.at[c, 1 - f], VB.at[c, 1 - f]).wait_recv()
+    send_all(1, lambda to: VB.at[c], VB.at[c])
+    recv_all(0, lambda s: WB.at[s, f])
+    pair(3, WB.at[:, f], WB.at[:, f]).start()
+    pl.loop(5, 8)(gather_x)
+
+    @pl.loop(0, 8)
+    def _(k):
+        for d in range(2):
+            at = block(XF, d, chip_of(d, k), other)
+            remote(at, at, sbx_s.at[d, k], sbx_r.at[d, k], "ctx", sib).wait_recv()
+
+    pair(1, WO.at[c, 1 - f], WO.at[c, 1 - f]).wait_recv()
+    pair(2, WD.at[1 - f], WD.at[1 - f]).wait_recv()
+    recv_all(1, lambda s: VB.at[s])
+
+    for j in range(8):
+        tiles = [VB[2 * j + q // 2, q % 2] for q in range(4)]
+        total = tiles[0]
+        for q in range(1, 4):
+            total = total + pltpu.roll(tiles[q], 32 * q, 1)
+        VF[:, 128 * j : 128 * j + 128] = total
+        v1 = pltpu.roll(tiles[1], 96, 1)
+        v2 = pltpu.roll(tiles[2], 64, 1)
+        v3 = pltpu.roll(tiles[3], 32, 1)
+        rows = (
+            tiles[0] + jnp.where(lane >= 96, v1, 0.0),
+            jnp.where(lane < 64, v1, 0.0) + jnp.where(lane >= 64, v2, 0.0),
+            jnp.where(lane < 32, v2, 0.0) + v3,
+        )
+        for i in range(3):
+            QBR[3 * j + i : 3 * j + i + 1, :] = rows[i][1:2, :]
+    UB[0:1, 0:128] = VB[c, 0, 0:1, :]
+    UB[0:1, 128:256] = VB[c, 1, 0:1, :]
+    for i in range(3):
+        row = QBR[pl.ds(8 * i + chip, 1), :]
+        BQ[i] = jnp.broadcast_to(row, (128, 128)).T
+    pair(3, WB.at[:, 1 - f], WB.at[:, 1 - f]).wait_recv()
+    WHT[...] = WB[:, :, :, 256:512].reshape(D, 256).T
+
+    def lanes(n):
+        return pl.ds(pl.multiple_of(n * CHUNK, CHUNK), CHUNK)
+
+    def turn(u, cosine, sine):
+        a, b = u[0:32], u[32:64]
+        return jnp.concatenate([a * cosine - b * sine, b * cosine + a * sine], axis=0)
+
+    def unturn(u, cosine, sine):
+        a, b = u[0:32], u[32:64]
+        return jnp.concatenate([a * cosine + b * sine, b * cosine - a * sine], axis=0)
+
+    @pl.loop(0, 8)
+    def _(it):
+        m = lax.div(it, 4)
+        n = lax.rem(it, 4)
+        xs = XF[m, pl.ds(2 * n, 2)].reshape(CHUNK, D)
+        joined = nt(WHT[0:192, :], xs)
+        cosine = rope_ref[0, :, lanes(n)]
+        sine = rope_ref[1, :, lanes(n)]
+        q = joined[0:64] + BQ[0, pl.ds(mine, BLK), 0:1]
+        k = joined[64:128] + BQ[1, pl.ds(mine, BLK), 0:1]
+        v = joined[128:192] + BQ[2, pl.ds(mine, BLK), 0:1]
+        q = turn(q, cosine, sine)
+        k = turn(k, cosine, sine)
+        rows = pl.ds(pl.multiple_of(n * CHUNK, CHUNK), CHUNK)
+        QT[m, :, lanes(n)] = q.astype(BF16)
+        KT[m, :, lanes(n)] = k.astype(BF16)
+        VT[m, :, lanes(n)] = v.astype(BF16)
+        KN[m, rows, :] = k.T.astype(BF16)
+        VN[m, rows, :] = v.T.astype(BF16)
+
+    def gather_wo(k):
+        for d in range(2):
+            at = WO.at[chip_of(d, k) * 2 + core, d]
+
+            @pl.when(k > 0)
+            def _():
+                remote(at, at, wo_s.at[d, 0], wo_r.at[d, k - 1], "ctx", target(d)).wait_recv()
+
+            @pl.when(k < 7)
+            def _():
+                remote(at, at, wo_s.at[d, k], wo_r.at[d, k], "ctx", target(d)).start()
+
+            remote(at, at, wos_s.at[d, k], wos_r.at[d, k], "ctx", sib).start()
+
+    @pl.loop(0, 8)
+    def _(it):
+        gather_wo(it)
+        m = lax.div(it, 4)
+        n = lax.rem(it, 4)
+        s = nn(KN[m], QT[m, :, lanes(n)]) * 0.125
+        e = jnp.exp(s - jnp.max(s, axis=0, keepdims=True))
+        p = (e * (1.0 / jnp.sum(e, axis=0, keepdims=True))).astype(BF16)
+        PT[m, :, lanes(n)] = p
+        ATD[m, :, lanes(n)] = nn(VT[m], p)
+
+    for j in range(8):
+        a0 = ATD[0, :, 128 * j : 128 * j + 128]
+        a1 = ATD[1, :, 128 * j : 128 * j + 128]
+        ATS[2 * j] = jnp.where(low_half, a0, pltpu.roll(a1, 64, 1)).astype(BF16)
+        ATS[2 * j + 1] = jnp.where(low_half, pltpu.roll(a0, 64, 1), a1).astype(BF16)
+    AT[c] = ATS[c]
+    send_all(2, lambda to: ATS.at[to], AT.at[c])
+
+    @pl.loop(0, 8)
+    def _(k):
+        for d in range(2):
+            at = WO.at[chip_of(d, k) * 2 + 1 - core, d]
+            remote(at, at, wos_s.at[d, k], wos_r.at[d, k], "ctx", sib).wait_recv()
+
+    recv_all(2, lambda s: AT.at[s])
+
+    att_rows = AT[...].reshape(D, 128).T
+    resid = x_ref[...].reshape(128, D).astype(F32) + nn(att_rows, WO[...].reshape(D, D)) + VF[2:3, :]
+    center = resid - row_mean(resid)
+    root = lax.rsqrt(row_mean(center * center) + 1e-05)
+    z = center * root
+    hidden = z * VF[4:5, :] + VF[5:6, :]
+    Z1[...] = z
+    R1[...] = jnp.broadcast_to(root, (128, 128))
+    H1[...] = hidden
+    hidden_low = hidden.astype(BF16)
+    for m in range(2):
+        HF[m, chip, pl.ds(mine, BLK)] = hidden_low[m * BLK : (m + 1) * BLK]
+
+    def ring(p, buf, make, extra, finish):
+        def first(k):
+            slot = 2 - lax.div(k + 7, 8) * (2 - lax.rem(k, 2))
+            for d in range(2):
+                ch = chip_of(d, k)
+                if buf is not None:
+                    at = block(buf, d, ch, mine)
+
+                    @pl.when(k > 0)
+                    def _():
+                        remote(at, at, ag_s.at[p, d, 0], ag_r.at[p, d, k - 1], "ctx", target(d)).wait_recv()
+
+                    @pl.when(k < 7)
+                    def _():
+                        remote(at, at, ag_s.at[p, d, k], ag_r.at[p, d, k], "ctx", target(d)).start()
+
+                    remote(at, at, sb_s.at[p, d, k], sb_r.at[p, d, k], "ctx", sib).start()
+            for d in range(2):
+                ch = chip_of(d, k)
+                if buf is not None:
+                    at = block(buf, d, ch, other)
+                    remote(at, at, sb_s.at[p, d, k], sb_r.at[p, d, k], "ctx", sib).wait_recv()
+                PB[d, slot] = make(d, ch)
+                SS[d, k] = PB[d, slot, pl.ds(other, BLK)].astype(BF16)
+                remote(SS.at[d, k], SR.at[d, k], ss_s.at[p, d, k], ss_r.at[p, d, k], "ctx", sib).start()
+
+        def second(k):
+            slot = lax.rem(k, 2)
+            for d in range(2):
+                at = SR.at[d, k]
+                remote(at, at, ss_s.at[p, d, k], ss_r.at[p, d, k], "ctx", sib).wait_recv()
+
+                @pl.when(k > 1)
+                def _():
+                    got = RR.at[d, k - 1]
+                    remote(got, got, rs_s.at[p, d, k], rs_r.at[p, d, k - 1], "ctx", sib).wait_recv()
+                    total = PB[d, slot, pl.ds(mine, BLK)] + SR[d, k].astype(F32) + RR[d, k - 1].astype(F32)
+                    RSD[d, k] = total.astype(BF16)
+
+                @pl.when(k == 1)
+                def _():
+                    total = PB[d, slot, pl.ds(mine, BLK)] + SR[d, k].astype(F32)
+                    RSD[d, k] = total.astype(BF16)
+
+                remote(RSD.at[d, k], RR.at[d, k], rs_s.at[p, d, k], rs_r.at[p, d, k], "ctx", target(d)).start()
+
+        @pl.loop(0, 9)
+        def _(it):
+            @pl.when(it < 8)
+            def _():
+                first(it)
+
+            @pl.when(it > 1)
+            def _():
+                second(it - 1)
+
+            extra(it)
+
+        for d in range(2):
+            at = SR.at[d, 0]
+            remote(at, at, ss_s.at[p, d, 0], ss_r.at[p, d, 0], "ctx", sib).wait_recv()
+            got = RR.at[d, 7]
+            remote(got, got, rs_s.at[p, d, 7], rs_r.at[p, d, 7], "ctx", sib).wait_recv()
+            finish(d, PB[d, 2, pl.ds(mine, BLK)] + SR[d, 0].astype(F32) + RR[d, 7].astype(F32))
+
+        @pl.loop(0, 8)
+        def _(k):
+            for d in range(2):
+                if buf is not None:
+                    at = block(buf, d, chip_of(d, k), mine)
+
+                    @pl.when(k < 7)
+                    def _():
+                        remote(at, at, ag_s.at[p, d, k], ag_r.at[p, d, k], "ctx", sib).wait_send()
+
+                    remote(at, at, sb_s.at[p, d, k], sb_r.at[p, d, k], "ctx", sib).wait_send()
+                remote(SS.at[d, k], SS.at[d, k], ss_s.at[p, d, k], ss_r.at[p, d, k], "ctx", sib).wait_send()
+
+                @pl.when(k > 0)
+                def _():
+                    remote(RSD.at[d, k], RSD.at[d, k], rs_s.at[p, d, k], rs_r.at[p, d, k], "ctx", sib).wait_send()
+
+    def nothing(it):
+        pass
+
+    def up_w():
+        return WB[:, :, :, 0:256].reshape(D, UNITS)
+
+    def down_w():
+        return WD[...].reshape(UNITS, D)
+
+    def make_up(m, ch):
+        u = nn(HF[m, ch], up_w()) + UB[0:1, :]
+        phi = 0.5 * (1.0 + lax.erf(u * 0.7071067811865476))
+        a = (u * phi).astype(BF16)
+        DG[m, ch] = phi + u * (jnp.exp(-0.5 * u * u) * 0.3989422804014327)
+        ACT[m, ch] = a
+        return nn(a, down_w())
+
+    def finish_up(d, total):
+        rows = slice(d * BLK, (d + 1) * BLK)
+        SEC[rows, :] = H1[rows, :] + total + VF[3:4, :]
+
+    ring(0, HF, make_up, nothing, finish_up)
+
+    resid = SEC[...]
+    center = resid - row_mean(resid)
+    root = lax.rsqrt(row_mean(center * center) + 1e-05)
+    z = center * root
+    out_ref[...] = (z * VF[6:7, :] + VF[7:8, :]).astype(BF16).reshape(2, BLK, D)
+    cot = ct_ref[...].reshape(128, D).astype(F32)
+    SG[...] = jnp.zeros((8, D), F32)
+    SG[4:5, :] = col_sum(cot * z)
+    SG[5:6, :] = col_sum(cot)
+    u = cot * VF[6:7, :]
+    grad = (u - row_mean(u) - z * row_mean(u * z)) * root
+    G2[...] = grad
+    grad_low = grad.astype(BF16)
+    SG[1:2, :] = col_sum(grad_low.astype(F32))
+    for m in range(2):
+        BG[m, chip, pl.ds(mine, BLK)] = grad_low[m * BLK : (m + 1) * BLK]
+
+    def make_down(m, ch):
+        pg = (nt(BG[m, ch], down_w()) * DG[m, ch]).astype(BF16)
+        PG[m, ch] = pg
+        return nt(pg, up_w())
+
+    def finish_down(d, total):
+        rows = slice(d * BLK, (d + 1) * BLK)
+        SEC[rows, :] = G2[rows, :] + total
+
+    ring(1, BG, make_down, nothing, finish_down)
+
+    hid = SEC[...]
+    z = Z1[...]
+    SG[2:3, :] = col_sum(hid * z)
+    SG[3:4, :] = col_sum(hid)
+    u = hid * VF[4:5, :]
+    grad = (u - row_mean(u) - z * row_mean(u * z)) * R1[:, 0:1]
+    H1[...] = grad
+    proj = grad.astype(BF16)
+    SG[0:1, :] = col_sum(proj.astype(F32))
+    sent_all(2, lambda to: ATS.at[to])
+    ATS[...] = nt(WO[...].reshape(D, D), proj).astype(BF16).reshape(NCTX, HEAD, 128)
+    AGT[c] = ATS[c]
+    send_all(3, lambda to: ATS.at[to], AGT.at[c])
+
+    TT[...] = PG[...].reshape(2048, UNITS).T
+    ones = jnp.ones((8, 2048), BF16)
+    SG[6:7, 0:256] = nn(ones, PG[...].reshape(2048, UNITS))[0:1, :]
+    pair(4, SG, SGR).start()
+
+    @pl.loop(0, NCTX)
+    def _(w):
+        TMP[...] = nn(AT[w], proj)
+        GO[w] = TMP[pl.ds(pl.multiple_of(f * 32, 32), 32)]
+        XSO[w] = TMP[pl.ds(pl.multiple_of((1 - f) * 32, 32), 32)].astype(BF16)
+
+    pair(5, XSO, XRO).start()
+
+    for n in range(4):
+        g = nn(TT[...], HF[:, :, :, CHUNK * n : CHUNK * (n + 1)].reshape(2048, CHUNK))
+        GU[4 * n : 4 * n + 4] = g.T.reshape(4, 2, 32, UNITS)
+    XSU[...] = GU[:, 1 - f].astype(BF16)
+    pair(6, XSU, XRU).start()
+    TT[...] = ACT[...].reshape(2048, UNITS).T
+    for n in range(4):
+        g = nn(TT[...], BG[:, :, :, CHUNK * n : CHUNK * (n + 1)].reshape(2048, CHUNK))
+        GD[:, :, CHUNK * n : CHUNK * (n + 1)] = g.reshape(2, 128, CHUNK)
+    XSD[...] = GD[1 - f].astype(BF16)
+    pair(7, XSD, XRD).start()
+    recv_all(3, lambda s: AGT.at[s])
+    sent_all(3, lambda to: ATS.at[to])
+
+    for j in range(8):
+        t0 = AGT[2 * j].astype(F32)
+        t1 = AGT[2 * j + 1].astype(F32)
+        AGQ[0, :, 128 * j : 128 * j + 128] = jnp.where(low_half, t0, pltpu.roll(t1, 64, 1)).astype(BF16)
+        AGQ[1, :, 128 * j : 128 * j + 128] = jnp.where(low_half, pltpu.roll(t0, 64, 1), t1).astype(BF16)
+
+    DK[...] = jnp.zeros((2, HEAD, D), F32)
+    DV[...] = jnp.zeros((2, HEAD, D), F32)
+
+    def go_sum():
+        pair(5, XRO, XRO).wait_recv()
+        for j in range(NCHIP):
+            w = 2 * j + core
+            v = 2 * j + 1 - core
+            GO[w] = GO[w] + XRO[w].astype(F32)
+            SSO[j] = (GO[v] + XRO[v].astype(F32)).astype(BF16)
+        remote(SSO, SRO, po_s.at[0], po_r.at[0], "ctx", sib).start()
+
+    def go_push():
+        remote(SRO, SRO, po_s.at[0], po_r.at[0], "ctx", sib).wait_recv()
+        for j in range(NCHIP):
+            w = 2 * j + core
+            GO[w] = GO[w] + SRO[j].astype(F32)
+            PO[j] = GO[w].astype(BF16)
+        for o in range(1, NCHIP):
+            j = lax.rem(chip + o, NCHIP)
+            remote(PO.at[j], RO.at[chip], po_s.at[o], po_r.at[o], "ctx", 2 * j + core).start()
+
+    def small_push():
+        pair(4, SGR, SGR).wait_recv()
+        SGT[...] = SG[...] + SGR[...]
+        SGC[c] = SGT[:, pl.ds(pl.multiple_of(chip * 128, 128), 128)]
+        send_all(4, lambda to: SGT.at[:, pl.ds(pl.multiple_of(lax.div(to, 2) * 128, 128), 128)], SGC.at[c])
+
+    def up_push():
+        pair(6, XRU, XRU).wait_recv()
+        AU[...] = (GU[:, f] + XRU[...].astype(F32)).astype(BF16)
+        RU[c] = AU[c]
+        send_all(5, lambda to: AU.at[to], RU.at[c])
+
+    @pl.loop(0, 8)
+    def _(it):
+        pl.when(it == 2)(small_push)
+        pl.when(it == 3)(go_sum)
+        pl.when(it == 5)(go_push)
+        pl.when(it == 6)(up_push)
+        m = lax.div(it, 4)
+        n = lax.rem(it, 4)
+        q = QT[m, :, lanes(n)]
+        g = AGQ[m, :, lanes(n)]
+        delta = jnp.sum(g.astype(F32) * ATD[m, :, lanes(n)], axis=0, keepdims=True)
+        p = PT[m, :, lanes(n)]
+        ds = (p.astype(F32) * (nn(VN[m], g) - delta)).astype(BF16)
+        DK[m] = DK[m] + nt(q, ds)
+        DV[m] = DV[m] + nt(g, p)
+        dq = nn(KT[m], ds) * 0.125
+        JG[m, 0:64, lanes(n)] = unturn(dq, rope_ref[0, :, lanes(n)], rope_ref[1, :, lanes(n)]).astype(BF16)
+
+    for m in range(2):
+        JG[m, 64:128, :] = unturn(DK[m] * 0.125, rope_ref[0], rope_ref[1]).astype(BF16)
+        JG[m, 128:192, :] = DV[m].astype(BF16)
+
+    def make_token(m, ch):
+        jg = JG[m, :, pl.ds(pl.multiple_of(ch * 128, 128), 128)]
+        return tn(jg, WHT[0:192, :])
+
+    def finish_token(d, total):
+        tg_ref[d] = H1[d * BLK : (d + 1) * BLK, :] + total
+
+    def qkv_grad():
+        for n in range(4):
+            cols = slice(CHUNK * n, CHUNK * (n + 1))
+            g = nn(JG[0], XF[0, :, :, cols].reshape(D, CHUNK)) + nn(JG[1], XF[1, :, :, cols].reshape(D, CHUNK))
+            g = jnp.concatenate([g, jnp.zeros((64, CHUNK), F32)], axis=0)
+            GU[4 * n : 4 * n + 4] = g.T.reshape(4, 2, 32, UNITS)
+        XSQ[...] = GU[:, 1 - f].astype(BF16)
+        pair(8, XSQ, XRQ).start()
+        ones8 = jnp.ones((8, D), BF16)
+        b = nt(ones8, JG[0]) + nt(ones8, JG[1])
+        QB1[...] = jnp.concatenate([b, jnp.zeros((8, 64), F32)], axis=1)
+        pair(9, QB1, QB2).start()
+
+    def qkv_push():
+        pair(8, XRQ, XRQ).wait_recv()
+        AQ[...] = (GU[:, f] + XRQ[...].astype(F32)).astype(BF16)
+        RQ[c] = AQ[c]
+        send_all(6, lambda to: AQ.at[to], RQ.at[c])
+        pair(9, QB2, QB2).wait_recv()
+        pair(9, QB1, QB1).wait_send()
+        QB1[...] = QB1[...] + QB2[...]
+        QB3[c] = QB1[...]
+        send_all(7, lambda to: QB1, QB3.at[c])
+
+    def out_rest():
+        for o in range(1, NCHIP):
+            j = lax.rem(chip + NCHIP - o, NCHIP)
+            remote(RO.at[j], RO.at[j], po_s.at[o], po_r.at[o], "ctx", sib).wait_recv()
+        total = GO[c]
+        for o in range(1, NCHIP):
+            total = total + RO[lax.rem(chip + o, NCHIP)].astype(F32)
+        go_ref[...] = total
+
+    def small_rest():
+        recv_all(4, lambda s: SGC.at[s])
+        total = SGC[0]
+        for w in range(1, NCTX):
+            total = total + SGC[w]
+        gs_ref[...] = total
+        gs_ref[6:7, :] = SGT[6:7, pl.ds(pl.multiple_of(f * 128, 128), 128)]
+        pair(7, XRD, XRD).wait_recv()
+        gd_ref[...] = GD[f] + XRD[...].astype(F32)
+
+    def up_rest():
+        recv_all(5, lambda s: RU.at[s])
+        for w in range(NCTX):
+            gu_ref[:, UNITS * w : UNITS * (w + 1)] = RU[w].astype(F32)
+
+    def on_the_way(it):
+        pl.when(it == 1)(qkv_grad)
+        pl.when(it == 3)(small_rest)
+        pl.when(it == 4)(qkv_push)
+        pl.when(it == 5)(out_rest)
+        pl.when(it == 6)(up_rest)
+
+    ring(2, None, make_token, on_the_way, finish_token)
+
+    recv_all(6, lambda s: RQ.at[s])
+    for j in range(8):
+        a = RQ[2 * j].astype(F32)
+        b = RQ[2 * j + 1].astype(F32)
+        cols = slice(128 * j, 128 * (j + 1))
+        gq_ref[:, cols] = jnp.where(low_half, a[:, 0:128], pltpu.roll(b[:, 0:128], 64, 1))
+        gq_ref[:, D + 128 * j : D + 128 * (j + 1)] = jnp.where(low_half, pltpu.roll(a[:, 0:128], 64, 1), b[:, 0:128])
+        gq_ref[:, 2 * D + 128 * j : 2 * D + 128 * (j + 1)] = jnp.where(low_half, a[:, 128:256], pltpu.roll(b[:, 128:256], 64, 1))
+    recv_all(7, lambda s: QB3.at[s])
+    for j in range(8):
+        a = QB3[2 * j]
+        b = QB3[2 * j + 1]
+        rows = (
+            jnp.where(low_half, a[:, 0:128], pltpu.roll(b[:, 0:128], 64, 1)),
+            jnp.where(low_half, pltpu.roll(a[:, 0:128], 64, 1), b[:, 0:128]),
+            jnp.where(low_half, a[:, 128:256], pltpu.roll(b[:, 128:256], 64, 1)),
+        )
+        for i in range(3):
+            gb_ref[8 * i + j : 8 * i + j + 1, :] = rows[i][0:1, :]
+
+    @pl.loop(0, 8)
+    def _(k):
+        for d in range(2):
+            ch = chip_of(d, k)
+
+            @pl.when(k < 7)
+            def _():
+                for q in range(4):
+                    at = sub(d, ch, q)
+                    remote(at, at, agx_s.at[d, k * 4 + q], agx_r.at[d, k * 4 + q], "ctx", sib).wait_send()
+                at = WO.at[ch * 2 + core, d]
+                remote(at, at, wo_s.at[d, k], wo_r.at[d, k], "ctx", sib).wait_send()
+
+            at = WO.at[ch * 2 + core, d]
+            remote(at, at, wos_s.at[d, k], wos_r.at[d, k], "ctx", sib).wait_send()
+            whole = block(XF, d, ch, mine)
+            remote(whole, whole, sbx_s.at[d, k], sbx_r.at[d, k], "ctx", sib).wait_send()
+
+    sent_all(0, lambda to: WP.at[to])
+    sent_all(1, lambda to: VB.at[c])
+    sent_all(4, lambda to: SGT.at[:, pl.ds(pl.multiple_of(lax.div(to, 2) * 128, 128), 128)])
+    sent_all(5, lambda to: AU.at[to])
+    sent_all(6, lambda to: AQ.at[to])
+    sent_all(7, lambda to: QB1)
+    remote(SSO, SSO, po_s.at[0], po_r.at[0], "ctx", sib).wait_send()
+    for o in range(1, NCHIP):
+        j = lax.rem(chip + o, NCHIP)
+        remote(PO.at[j], PO.at[j], po_s.at[o], po_r.at[o], "ctx", sib).wait_send()
+    for i, at in enumerate((vec_ref, wo_ref, wd_ref, WB.at[:, f], SG, XSO, XSU, XSD, XSQ)):
+        pair(i, at, at).wait_send()
+
+
+def rope_tables():
+    freqs = (np.float32(10000.0) ** (-np.arange(0, HEAD, 2, dtype=np.float32) / np.float32(HEAD))).astype(np.float32)
+    angles = freqs[:, None] * np.arange(1024, dtype=np.float32)[None, :]
+    return np.stack([np.cos(angles), np.sin(angles)]).astype(np.float32)
+
+
+def fused_body(
+    tokens, cotangent, qkv_weight, out_weight, up_weight, down_weight, qkv_bias, out_bias, up_bias, down_bias,
+    first_gain, first_shift, second_gain, second_shift,
+):
+    def wide(v):
+        return jnp.pad(v.astype(F32), (0, 128 - v.shape[0]))
+
+    vec = jnp.stack(
+        [wide(v) for v in (up_bias, qkv_bias, out_bias, down_bias, first_gain, first_shift, second_gain, second_shift)]
+    )
+    scratch = [
+        ((2, 8, 128, D), BF16), ((2, 8, 128, D), BF16), ((2, 8, 128, D), BF16),
+        ((16, 32, 512), BF16), ((16, 2, 32, 512), BF16), ((16, 2, 32, D), BF16), ((2, 128, D), BF16),
+        ((16, 2, 8, 128), F32), ((8, D), F32), ((8, UNITS), F32), ((24, 128), F32), ((3, 128, 128), F32),
+        ((256, D), BF16),
+        ((2, 64, D), BF16), ((2, 64, D), BF16), ((2, 64, D), BF16), ((2, D, 64), BF16), ((2, D, 64), BF16),
+        ((2, D, D), BF16), ((2, 64, D), F32),
+        ((16, 64, 128), BF16), ((16, 64, 128), BF16), ((16, 64, 128), BF16),
+        ((128, D), F32), ((128, D), F32), ((128, 128), F32), ((128, D), F32), ((128, D), F32),
+        ((2, 8, 128, UNITS), F32), ((2, 8, 128, UNITS), BF16), ((2, 8, 128, UNITS), BF16),
+        ((2, 3, 128, D), F32),
+        ((2, 8, BLK, D), BF16), ((2, 8, BLK, D), BF16), ((2, 8, BLK, D), BF16), ((2, 8, BLK, D), BF16),
+        ((UNITS, 2048), BF16), ((64, D), F32),
+        ((16, 2, 32, UNITS), F32), ((16, 32, UNITS), BF16), ((16, 32, UNITS), BF16), ((16, 32, UNITS), BF16), ((16, 32, UNITS), BF16),
+        ((2, 128, D), F32), ((128, D), BF16), ((128, D), BF16),
+        ((16, 32, D), F32), ((16, 32, D), BF16), ((16, 32, D), BF16),
+        ((8, 32, D), BF16), ((8, 32, D), BF16), ((8, 32, D), BF16), ((8, 32, D), BF16),
+        ((8, D), F32), ((8, D), F32), ((8, D), F32), ((16, 8, 128), F32), ((2, 64, D), BF16),
+        ((2, 64, D), F32), ((2, 64, D), F32), ((2, 192, D), BF16),
+        ((16, 32, UNITS), BF16), ((16, 32, UNITS), BF16), ((16, 32, UNITS), BF16), ((16, 32, UNITS), BF16),
+        ((8, 256), F32), ((8, 256), F32), ((16, 8, 256), F32),
+    ]
+    sems = [(2, 32)] * 2 + [(2, 8)] * 2 + [(2, 2, 8)] * 4 + [(3, 2, 8)] * 4 + [(2, 8)] * 4 + [(8, 16)] * 2 + [(10,)] * 2 + [(8,)] * 2
+    vmem = pl.BlockSpec(memory_space=pltpu.VMEM)
+    shapes = [((2, BLK, D), BF16), ((2, BLK, D), F32), ((32, 3 * D), F32), ((32, D), F32), ((32, 4 * D), F32), ((128, D), F32), ((8, 128), F32), ((24, 128), F32)]
+    output, token_grad, qkv_grad, out_grad, up_grad, down_grad, small, qkv_small = pl.pallas_call(
+        layer_kernel,
+        out_shape=[jax.ShapeDtypeStruct(s, t) for s, t in shapes],
+        in_specs=[vmem] * 8,
+        out_specs=[vmem] * 8,
+        scratch_shapes=[pltpu.VMEM(s, t) for s, t in scratch] + [pltpu.SemaphoreType.DMA(s) for s in sems],
+        compiler_params=pltpu.CompilerParams(collective_id=0, has_side_effects=True, vmem_limit_bytes=VMEM_LIMIT),
+        name="layer",
+    )(tokens[:, 0], cotangent[:, 0], qkv_weight, out_weight, up_weight, down_weight, vec, jnp.asarray(rope_tables()))
+    index = lax.axis_index("ctx") * 2 + lax.axis_index("fsdp")
+    part = lax.dynamic_slice_in_dim(small, 32 * lax.rem(index, 4), 32, 1)
+    qkv_part = lax.dynamic_slice_in_dim(qkv_small.reshape(3 * D), 96 * index, 96, 0)
+    return (
+        output[:, None], token_grad[:, None], qkv_grad, out_grad, up_grad, down_grad,
+        qkv_part, part[0], small[6], part[1], part[2], part[3], part[4], part[5],
+    )
+
+
+VMEM_LIMIT = 63 * 1024 * 1024
 
 
 def layernorm(resid, gain, shift):
@@ -456,4 +1147,5 @@
         P(("ctx", "fsdp")),
         P(("ctx", "fsdp")),
     )
-    return jax.shard_map(body, mesh=mesh, in_specs=in_specs, out_specs=out_specs, check_vma=False)
+    fused = mesh.shape["ctx"] == NCTX and mesh.shape["fsdp"] == 2
+    return jax.shard_map(fused_body if fused else body, mesh=mesh, in_specs=in_specs, out_specs=out_specs, check_vma=False)

time: 1810 us -> 290 us (0.16)
  waiting for transfers between devices: 1330 us -> 0 us
  Pallas kernels: 0 us -> 275 us
  blocking collectives: 150 us -> 0 us
  matrix products: 128 us -> 0 us
  local copies, waits for them, and re-layouts: 141 us -> 13.7 us
  other arithmetic: 30.4 us -> 0.6 us
    reduce_scatter x3 -> x0, waiting for transfers between devices: 757 us -> none  [the longest x1 361 us: body(): lax.psum_scatter(totals[3], ('ctx', 'fsdp'), scatter_dimension=0, tiled=T...]
    all_gather x8 -> x0, waiting for transfers between devices: 288 us -> none  [the longest x1 72.2 us: body(): lax.all_gather(down_weight, ('ctx', 'fsdp'), axis=0, tiled=True)]
    unnamed x17 -> x0, waiting for transfers between devices: 288 us -> none
    pallas_call x0 -> x1, Pallas kernels: none -> 275 us  [fused_body(): pl.pallas_call(layer_kernel, out_shape=[jax.ShapeDtypeStruct(s, t) for s,...]
    dot_general x52 -> x0, matrix products: 128 us -> none  [the longest x4 13.3 us: fill(): jnp.einsum('hqk,qhd->khd', score_grad, query_heads, preferred_element_typ...]
    unnamed x2 -> x0, blocking collectives: 84.3 us -> none
    all_gather x1 -> x0, blocking collectives: 65.8 us -> none  [body(): lax.all_gather(up_bias, ('ctx', 'fsdp'), axis=0, tiled=True)]
    unnamed x217 -> x32, local copies, waits for them, and re-layouts: 50.7 us -> 9.82 us
  transfers between devices with their start and end apart: 14 -> 0, of which waited for: 13 -> 0; matrix products, arithmetic and copies ran while one was open for 11% -> 0% of each run, Pallas kernels for 0% -> 0%
where the time goes in v1:
time: 290 us
  Pallas kernels  275 us (95%)
  local copies, waits for them, and re-layouts  13.7 us (5%)
    pallas_call x1, Pallas kernels, fused_body(): pl.pallas_call(layer_kernel, out_shape=[jax.ShapeDtypeStruct(s, t) for s,...  275 us
    unnamed x32, local copies, waits for them, and re-layouts  9.82 us

profile of v1, /device:TPU:0, one launch (start us, length us, event | category | flops | bytes accessed | tf_op | source)
XLA Modules:
  0.0 289.5 jit_solution(14044529628234503692)
XLA Ops:
  0.7 0.0 copy-start.6
  0.7 0.0 copy-start.7
  0.7 0.6 copy-done.6
  1.3 0.0 copy-done.7
  1.3 0.0 copy-start.8
  1.3 0.0 copy-start.9
  1.3 0.6 copy-done.8
  2.0 0.0 copy-done.9
  2.0 0.0 copy-start.10
  2.0 0.0 copy-start.11
  2.0 0.6 copy-done.10
  2.7 0.0 copy-done.11
  2.7 0.0 copy-start.12
  2.7 0.7 copy-done.12
  3.3 0.0 copy-start.5
  3.4 0.7 copy-done.5
  4.0 0.6 stack.46.vec_ref
  4.6 274.5 %layer.1 = (bf16[2,64,1024]{2,1,0:T(8,128)(2,1)}, f32[2,64,1024]{2,1,0:T(8,128)}, f32[32,3072]{1,0:T(8,128)}, f32[32,1024]{1,0:T(8,128)}, f32[32,4096]{1,0:T(8,1...) custom-call(bf16[2,64,1024]{2,1,0:T(8,128)(2,1)} %bitcast.40, bf16[2,64,1024]{2,1,0:T(8,128)(2,1)} %bitcast.41, ...), custom_call_target="tpu_custom_call" | custom-call | tf_op jit(solution)/shard_map/layer/pallas_call | solution.py:684
  279.2 0.0 copy-start.2
  279.2 0.8 constant_dynamic-slice_fusion
  280.0 0.5 slice_bitcast_fusion
  280.5 1.3 dynamic_slice.6
  281.8 1.2 slice_bitcast_fusion.5
  283.0 1.7 copy.37
  284.6 0.0 copy-done.2
  284.6 0.0 copy-start.3
  284.7 0.8 copy.38
  285.4 0.4 copy-done.3
  285.8 0.0 copy-start.4
  285.8 0.0 copy-start.1
  285.8 0.7 copy.39
  286.6 0.2 copy-done.4
  286.8 0.7 copy.40
  287.5 0.0 copy-done.1
  287.5 0.0 copy-start
  287.5 0.8 copy.41
  288.3 0.4 copy-done
  288.7 0.8 copy.42
  (5 shorter events, 0.1 us)
Async XLA Ops:
  0.7 0.7 copy-start.6
  0.7 0.7 copy-start.7
  1.3 0.7 copy-start.8
  1.3 0.7 copy-start.9
  2.0 0.7 copy-start.10
  2.0 0.7 copy-start.11
  2.7 0.7 copy-start.12
  3.3 0.7 copy-start.5
  279.2 5.5 %copy-start.2 = (f32[2,64,1024]{2,1,0:T(8,128)S(1)}, f32[2,64,1024]{2,1,0:T(8,128)}, u32[]{:S(2)}) copy-start(f32[2,64,1024]{2,1,0:T(8,128)} %get-tuple-element.23) | copy-start | bytes 1572868
  284.6 1.2 copy-start.3
  285.8 1.0 copy-start.4
  285.8 1.7 copy-start.1
  287.5 1.2 copy-start

commit v2 on v1

--- a/solution.py
+++ b/solution.py
@@ -23,6 +23,9 @@
 D = 1024
 UNITS = 256
 CHUNK = 256
+AQS = 2
+RQS = 2
+ROWS = BLK // RQS
 
 
 def chip_at(place):
@@ -51,14 +54,13 @@
 
 
 def layer_kernel(
-    x_ref, ct_ref, wq_ref, wo_ref, wu_ref, wd_ref, vec_ref, rope_ref,
+    x_ref, ct_ref, wq_ref, wo_ref, wu_ref, wd_ref, rope_ref, v0, v1, v2, v3, v4, v5, v6, v7,
     out_ref, tg_ref, gq_ref, go_ref, gu_ref, gd_ref, gs_ref, gb_ref,
-    XF, HF, BG, WP, WB, WO, WD, VB, VF, UB, QBR, BQ, WHT, QT, KT, VT, KN, VN, PT, ATD, ATS, AT, AGT,
-    H1, Z1, R1, SEC, G2, DG, ACT, PG, PB, SS, SR, RSD, RR, TT, TMP,
-    GU, XSU, XRU, AU, RU, GD, XSD, XRD, GO, XSO, XRO, SSO, SRO, PO, RO, SG, SGR, SGT, SGC, AGQ,
+    VEC, XF, HF, BG, WP, WB, WU, WO, WD, VB, VF, UB, QBR, BQ, WHT, QT, KT, VT, KN, VN, PT, ATD, ATS, AT, AGT,
+    H1, Z1, R1, SEC, G2, DG, ACT, PG, PB, SS, SR, RSD, RR, TT,
+    GU, XSU, XRU, AU, RU, GD, XSD, XRD, GO, XSO, XRO, SSO, SRO, SG, SGR, SGT, SGC, AGQ,
     DK, DV, JG, XSQ, XRQ, AQ, RQ, QB1, QB2, QB3,
-    agx_s, agx_r, sbx_s, sbx_r, ag_s, ag_r, sb_s, sb_r, ss_s, ss_r, rs_s, rs_r, wo_s, wo_r, wos_s, wos_r,
-    all_s, all_r, pair_s, pair_r, po_s, po_r,
+    one, ag_r, sb_r, ss_r, rs_r, wo_r, all_s, all_r, pair_s, pair_r,
 ):
     c = lax.axis_index("ctx")
     f = lax.axis_index("fsdp")
@@ -90,23 +92,18 @@
         @pl.loop(1, NCTX)
         def _(o):
             to = lax.rem(c + o, NCTX)
-            remote(src_at(to), dst, all_s.at[e, o], all_r.at[e, o], "ctx", to).start()
-
-    def recv_all(e, dst_at):
-        @pl.loop(1, NCTX)
-        def _(o):
-            at = dst_at(lax.rem(c + NCTX - o, NCTX))
-            remote(at, at, all_s.at[e, o], all_r.at[e, o], "ctx", sib).wait_recv()
-
-    def sent_all(e, src_at):
-        @pl.loop(1, NCTX)
-        def _(o):
-            at = src_at(lax.rem(c + o, NCTX))
-            remote(at, at, all_s.at[e, o], all_r.at[e, o], "ctx", sib).wait_send()
+            remote(src_at(to), dst, all_s.at[e], all_r.at[e], "ctx", to).start()
+
+    def recv_all(e, slab):
+        remote(slab, slab, all_s.at[e], all_r.at[e], "ctx", sib).wait_recv()
+
+    def sent_all(e, slab):
+        remote(slab, slab, all_s.at[e], all_r.at[e], "ctx", sib).wait_send()
 
     def pair(i, src, dst):
         return remote(src, dst, pair_s.at[i], pair_r.at[i], "fsdp", 1 - f)
 
+    agx_s, sbx_s, sbx_r, ag_s, sb_s, ss_s, rs_s, wo_s, wos_s, wos_r, po_s, po_r = (one.at[i] for i in range(12))
     barrier = pltpu.get_barrier_semaphore()
 
     @pl.loop(1, NCTX)
@@ -120,35 +117,51 @@
         return buf.at[m, ch, pl.ds(row0, BLK)]
 
     def sub(m, ch, q):
-        return XF.at[m, ch, pl.ds(pl.multiple_of(core * BLK + 16 * q, 16), 16)]
+        return XF.at[m, ch, pl.ds(pl.multiple_of(core * BLK + (BLK // AQS) * q, BLK // AQS), BLK // AQS)]
 
     for m in range(2):
         XF[m, chip, pl.ds(mine, BLK)] = x_ref[m]
     WO[c, f] = wo_ref[...]
     WD[f] = wd_ref[...]
-    VB[c, f] = vec_ref[...]
+    VEC[...] = jnp.zeros((8, 128), F32)
+    for i, v in enumerate((v0, v1, v2, v3, v4, v5, v6, v7)):
+        VEC[i : i + 1, 0 : v.shape[1]] = v[...].astype(F32)
+    VB[c, f] = VEC[...]
 
     def gather_x(k):
         for d in range(2):
             ch = chip_of(d, k)
-            for q in range(4):
+            for q in range(AQS):
                 at = sub(d, ch, q)
 
                 @pl.when(k > 0)
                 def _():
-                    remote(at, at, agx_s.at[d, 0], agx_r.at[d, (k - 1) * 4 + q], "ctx", target(d)).wait_recv()
+                    remote(at, at, agx_s, ag_r.at[d, (k - 1) * AQS + q], "ctx", target(d)).wait_recv()
 
                 @pl.when(k < 7)
                 def _():
-                    remote(at, at, agx_s.at[d, k * 4 + q], agx_r.at[d, k * 4 + q], "ctx", target(d)).start()
+                    remote(at, at, agx_s, ag_r.at[d, k * AQS + q], "ctx", target(d)).start()
 
             whole = block(XF, d, ch, mine)
-            remote(whole, whole, sbx_s.at[d, k], sbx_r.at[d, k], "ctx", sib).start()
+            remote(whole, whole, sbx_s, sbx_r, "ctx", sib).start()
+
+    def gather_wo(k):
+        for d in range(2):
+            at = WO.at[chip_of(d, k) * 2 + core, d]
+
+            @pl.when(k > 0)
+            def _():
+                remote(at, at, wo_s, wo_r.at[d, k - 1], "ctx", target(d)).wait_recv()
+
+            @pl.when(k < 7)
+            def _():
+                remote(at, at, wo_s, wo_r.at[d, k], "ctx", target(d)).start()
+
+            remote(at, at, wos_s, wos_r, "ctx", sib).start()
 
     pl.loop(0, 1)(gather_x)
-    pair(0, vec_ref, VB.at[c, f]).start()
+    pair(0, VEC, VB.at[c, f]).start()
     pair(1, wo_ref, WO.at[c, f]).start()
-    pair(2, wd_ref, WD.at[f]).start()
 
     for j in range(8):
         qt = wq_ref[:, 128 * j : 128 * j + 128].astype(F32)
@@ -156,28 +169,29 @@
         vt = wq_ref[:, 2 * D + 128 * j : 2 * D + 128 * j + 128].astype(F32)
         for e in range(2):
             w = 2 * j + e
-            WP[w, :, 0:256] = wu_ref[:, 256 * w : 256 * w + 256]
             qk = jnp.where(low_half, qt, pltpu.roll(kt, 64, 1)) if e == 0 else jnp.where(low_half, pltpu.roll(qt, 64, 1), kt)
-            WP[w, :, 256:384] = qk.astype(BF16)
-            WP[w, :, 384:512] = (vt if e == 0 else pltpu.roll(vt, 64, 1)).astype(BF16)
+            WP[w, :, 0:128] = qk.astype(BF16)
+            WP[w, :, 128:256] = (vt if e == 0 else pltpu.roll(vt, 64, 1)).astype(BF16)
     WB[c, f] = WP[c]
     send_all(0, lambda to: WP.at[to], WB.at[c, f])
-    pl.loop(1, 5)(gather_x)
+    pl.loop(1, 4)(gather_x)
     pair(0, VB.at[c, 1 - f], VB.at[c, 1 - f]).wait_recv()
     send_all(1, lambda to: VB.at[c], VB.at[c])
-    recv_all(0, lambda s: WB.at[s, f])
+    recv_all(0, WB.at[0:15, 0])
     pair(3, WB.at[:, f], WB.at[:, f]).start()
-    pl.loop(5, 8)(gather_x)
-
-    @pl.loop(0, 8)
+    pair(1, WO.at[c, 1 - f], WO.at[c, 1 - f]).wait_recv()
+
+    @pl.loop(4, 8)
     def _(k):
-        for d in range(2):
-            at = block(XF, d, chip_of(d, k), other)
-            remote(at, at, sbx_s.at[d, k], sbx_r.at[d, k], "ctx", sib).wait_recv()
-
-    pair(1, WO.at[c, 1 - f], WO.at[c, 1 - f]).wait_recv()
-    pair(2, WD.at[1 - f], WD.at[1 - f]).wait_recv()
-    recv_all(1, lambda s: VB.at[s])
+        gather_x(k)
+        gather_wo(k - 4)
+
+    WU[c, f] = wu_ref[:, pl.ds(pl.multiple_of(c * UNITS, UNITS), UNITS)]
+    send_all(8, lambda to: wu_ref.at[:, pl.ds(pl.multiple_of(to * UNITS, UNITS), UNITS)], WU.at[c, f])
+    pair(2, wd_ref, WD.at[f]).start()
+
+    remote(XF.at[0], XF.at[0], sbx_s, sbx_r, "ctx", sib).wait_recv()
+    recv_all(1, VB.at[0:15])
 
     for j in range(8):
         tiles = [VB[2 * j + q // 2, q % 2] for q in range(4)]
@@ -201,7 +215,7 @@
         row = QBR[pl.ds(8 * i + chip, 1), :]
         BQ[i] = jnp.broadcast_to(row, (128, 128)).T
     pair(3, WB.at[:, 1 - f], WB.at[:, 1 - f]).wait_recv()
-    WHT[...] = WB[:, :, :, 256:512].reshape(D, 256).T
+    WHT[...] = WB[...].reshape(D, 256).T
 
     def lanes(n):
         return pl.ds(pl.multiple_of(n * CHUNK, CHUNK), CHUNK)
@@ -234,23 +248,17 @@
         KN[m, rows, :] = k.T.astype(BF16)
         VN[m, rows, :] = v.T.astype(BF16)
 
-    def gather_wo(k):
-        for d in range(2):
-            at = WO.at[chip_of(d, k) * 2 + core, d]
-
-            @pl.when(k > 0)
-            def _():
-                remote(at, at, wo_s.at[d, 0], wo_r.at[d, k - 1], "ctx", target(d)).wait_recv()
-
-            @pl.when(k < 7)
-            def _():
-                remote(at, at, wo_s.at[d, k], wo_r.at[d, k], "ctx", target(d)).start()
-
-            remote(at, at, wos_s.at[d, k], wos_r.at[d, k], "ctx", sib).start()
-
     @pl.loop(0, 8)
     def _(it):
-        gather_wo(it)
+        @pl.when(lax.rem(it, 2) == 0)
+        def _():
+            gather_wo(4 + lax.div(it, 2))
+
+        @pl.when(it == 5)
+        def _():
+            recv_all(8, WU.at[0:15, 0])
+            pair(10, WU.at[:, f], WU.at[:, f]).start()
+
         m = lax.div(it, 4)
         n = lax.rem(it, 4)
         s = nn(KN[m], QT[m, :, lanes(n)]) * 0.125
@@ -267,13 +275,8 @@
     AT[c] = ATS[c]
     send_all(2, lambda to: ATS.at[to], AT.at[c])
 
-    @pl.loop(0, 8)
-    def _(k):
-        for d in range(2):
-            at = WO.at[chip_of(d, k) * 2 + 1 - core, d]
-            remote(at, at, wos_s.at[d, k], wos_r.at[d, k], "ctx", sib).wait_recv()
-
-    recv_all(2, lambda s: AT.at[s])
+    remote(WO.at[0:8], WO.at[0:8], wos_s, wos_r, "ctx", sib).wait_recv()
+    recv_all(2, AT.at[0:15])
 
     att_rows = AT[...].reshape(D, 128).T
     resid = x_ref[...].reshape(128, D).astype(F32) + nn(att_rows, WO[...].reshape(D, D)) + VF[2:3, :]
@@ -288,6 +291,9 @@
     for m in range(2):
         HF[m, chip, pl.ds(mine, BLK)] = hidden_low[m * BLK : (m + 1) * BLK]
 
+    pair(2, WD.at[1 - f], WD.at[1 - f]).wait_recv()
+    pair(10, WU.at[:, 1 - f], WU.at[:, 1 - f]).wait_recv()
+
     def ring(p, buf, make, extra, finish):
         def first(k):
             slot = 2 - lax.div(k + 7, 8) * (2 - lax.rem(k, 2))
@@ -298,41 +304,62 @@
 
                     @pl.when(k > 0)
                     def _():
-                        remote(at, at, ag_s.at[p, d, 0], ag_r.at[p, d, k - 1], "ctx", target(d)).wait_recv()
+                        remote(at, at, ag_s, ag_r.at[d, k - 1], "ctx", target(d)).wait_recv()
 
                     @pl.when(k < 7)
                     def _():
-                        remote(at, at, ag_s.at[p, d, k], ag_r.at[p, d, k], "ctx", target(d)).start()
-
-                    remote(at, at, sb_s.at[p, d, k], sb_r.at[p, d, k], "ctx", sib).start()
+                        remote(at, at, ag_s, ag_r.at[d, k], "ctx", target(d)).start()
+
+                    remote(at, at, sb_s, sb_r.at[d, k], "ctx", sib).start()
             for d in range(2):
                 ch = chip_of(d, k)
                 if buf is not None:
                     at = block(buf, d, ch, other)
-                    remote(at, at, sb_s.at[p, d, k], sb_r.at[p, d, k], "ctx", sib).wait_recv()
+                    remote(at, at, sb_s, sb_r.at[d, k], "ctx", sib).wait_recv()
                 PB[d, slot] = make(d, ch)
                 SS[d, k] = PB[d, slot, pl.ds(other, BLK)].astype(BF16)
-                remote(SS.at[d, k], SR.at[d, k], ss_s.at[p, d, k], ss_r.at[p, d, k], "ctx", sib).start()
+                remote(SS.at[d, k], SR.at[d, k], ss_s, ss_r.at[d, k], "ctx", sib).start()
+
+        def sums(d, k):
+            at = SR.at[d, k]
+            remote(at, at, ss_s, ss_r.at[d, k], "ctx", sib).wait_recv()
+
+        def arrived(d, q, k):
+            got = RR.at[d, k, rows_of(q)]
+            remote(got, got, rs_s, rs_r.at[d, k * RQS + q], "ctx", sib).wait_recv()
+
+        def rows_of(q):
+            return pl.ds(q * ROWS, ROWS if p < 2 or q < RQS - 1 else ROWS + 16)
 
         def second(k):
             slot = lax.rem(k, 2)
             for d in range(2):
-                at = SR.at[d, k]
-                remote(at, at, ss_s.at[p, d, k], ss_r.at[p, d, k], "ctx", sib).wait_recv()
-
-                @pl.when(k > 1)
-                def _():
-                    got = RR.at[d, k - 1]
-                    remote(got, got, rs_s.at[p, d, k], rs_r.at[p, d, k - 1], "ctx", sib).wait_recv()
-                    total = PB[d, slot, pl.ds(mine, BLK)] + SR[d, k].astype(F32) + RR[d, k - 1].astype(F32)
-                    RSD[d, k] = total.astype(BF16)
-
-                @pl.when(k == 1)
-                def _():
-                    total = PB[d, slot, pl.ds(mine, BLK)] + SR[d, k].astype(F32)
-                    RSD[d, k] = total.astype(BF16)
-
-                remote(RSD.at[d, k], RR.at[d, k], rs_s.at[p, d, k], rs_r.at[p, d, k], "ctx", target(d)).start()
+                sums(d, k)
+            for q in range(RQS):
+                for d in range(2):
+                    part = pl.ds(q * ROWS, ROWS)
+                    total = PB[d, slot, pl.ds(pl.multiple_of(core * BLK + q * ROWS, ROWS), ROWS)] + SR[d, k, part].astype(F32)
+                    rider = p == 2 and q == RQS - 1
+                    if rider:
+                        ride = riders(d, chip_of(d, k))
+
+                    @pl.when(k > 1)
+                    def _():
+                        arrived(d, q, k - 1)
+                        RSD[d, k, part] = (total + RR[d, k - 1, part].astype(F32)).astype(BF16)
+                        if rider:
+                            RSD[d, k, BLK : BLK + 16] = (ride + RR[d, k - 1, BLK : BLK + 16].astype(F32)).astype(BF16)
+
+                    @pl.when(k == 1)
+                    def _():
+                        RSD[d, k, part] = total.astype(BF16)
+                        if rider:
+                            RSD[d, k, BLK : BLK + 16] = ride.astype(BF16)
+
+                    remote(
+                        RSD.at[d, k, rows_of(q)], RR.at[d, k, rows_of(q)], rs_s, rs_r.at[d, k * RQS + q],
+                        "ctx", target(d),
+                    ).start()
 
         @pl.loop(0, 9)
         def _(it):
@@ -347,34 +374,23 @@
             extra(it)
 
         for d in range(2):
-            at = SR.at[d, 0]
-            remote(at, at, ss_s.at[p, d, 0], ss_r.at[p, d, 0], "ctx", sib).wait_recv()
-            got = RR.at[d, 7]
-            remote(got, got, rs_s.at[p, d, 7], rs_r.at[p, d, 7], "ctx", sib).wait_recv()
-            finish(d, PB[d, 2, pl.ds(mine, BLK)] + SR[d, 0].astype(F32) + RR[d, 7].astype(F32))
-
-        @pl.loop(0, 8)
-        def _(k):
-            for d in range(2):
-                if buf is not None:
-                    at = block(buf, d, chip_of(d, k), mine)
-
-                    @pl.when(k < 7)
-                    def _():
-                        remote(at, at, ag_s.at[p, d, k], ag_r.at[p, d, k], "ctx", sib).wait_send()
-
-                    remote(at, at, sb_s.at[p, d, k], sb_r.at[p, d, k], "ctx", sib).wait_send()
-                remote(SS.at[d, k], SS.at[d, k], ss_s.at[p, d, k], ss_r.at[p, d, k], "ctx", sib).wait_send()
-
-                @pl.when(k > 0)
-                def _():
-                    remote(RSD.at[d, k], RSD.at[d, k], rs_s.at[p, d, k], rs_r.at[p, d, k], "ctx", sib).wait_send()
+            sums(d, 0)
+            for q in range(RQS):
+                arrived(d, q, 7)
+            finish(d, PB[d, 2, pl.ds(mine, BLK)] + SR[d, 0].astype(F32) + RR[d, 7, 0:BLK].astype(F32))
+
+        if buf is not None:
+            remote(buf.at[0, 0:7], buf.at[0, 0:7], ag_s, sbx_r, "ctx", sib).wait_send()
+            remote(buf.at[0], buf.at[0], sb_s, sbx_r, "ctx", sib).wait_send()
+        remote(SS, SS, ss_s, sbx_r, "ctx", sib).wait_send()
+        sent = SS.at[:, 0:7] if p < 2 else RSD.at[:, 0:7]
+        remote(sent, sent, rs_s, sbx_r, "ctx", sib).wait_send()
 
     def nothing(it):
         pass
 
     def up_w():
-        return WB[:, :, :, 0:256].reshape(D, UNITS)
+        return WU[...].reshape(D, UNITS)
 
     def down_w():
         return WD[...].reshape(UNITS, D)
@@ -419,7 +435,23 @@
         rows = slice(d * BLK, (d + 1) * BLK)
         SEC[rows, :] = G2[rows, :] + total
 
-    ring(1, BG, make_down, nothing, finish_down)
+    def ff_grads():
+        TT[...] = ACT[...].reshape(2048, UNITS).T
+        for n in range(4):
+            g = nn(TT[...], BG[:, :, :, CHUNK * n : CHUNK * (n + 1)].reshape(2048, CHUNK))
+            GD[:, :, CHUNK * n : CHUNK * (n + 1)] = g.reshape(2, 128, CHUNK)
+        XSD[...] = GD[1 - f].astype(BF16)
+        pair(7, XSD, XRD).start()
+        ones = jnp.ones((8, 2048), BF16)
+        SG[6:7, 0:256] = nn(ones, PG[...].reshape(2048, UNITS))[0:1, :]
+        TT[...] = PG[...].reshape(2048, UNITS).T
+        for n in range(4):
+            g = nn(TT[...], HF[:, :, :, CHUNK * n : CHUNK * (n + 1)].reshape(2048, CHUNK))
+            GU[4 * n : 4 * n + 4] = g.T.reshape(4, 2, 32, UNITS)
+        XSU[...] = GU[:, 1 - f].astype(BF16)
+        pair(6, XSU, XRU).start()
+
+    ring(1, BG, make_down, lambda it: pl.when(it == 8)(ff_grads), finish_down)
 
     hid = SEC[...]
     z = Z1[...]
@@ -430,37 +462,24 @@
     H1[...] = grad
     proj = grad.astype(BF16)
     SG[0:1, :] = col_sum(proj.astype(F32))
-    sent_all(2, lambda to: ATS.at[to])
+    sent_all(2, ATS.at[0:15])
     ATS[...] = nt(WO[...].reshape(D, D), proj).astype(BF16).reshape(NCTX, HEAD, 128)
     AGT[c] = ATS[c]
     send_all(3, lambda to: ATS.at[to], AGT.at[c])
 
-    TT[...] = PG[...].reshape(2048, UNITS).T
-    ones = jnp.ones((8, 2048), BF16)
-    SG[6:7, 0:256] = nn(ones, PG[...].reshape(2048, UNITS))[0:1, :]
+    for j in range(NCHIP):
+        SSO[j] = nn(AT[2 * j + 1 - core], proj).astype(BF16)
+    remote(SSO, SRO, po_s, po_r, "ctx", sib).start()
     pair(4, SG, SGR).start()
-
-    @pl.loop(0, NCTX)
-    def _(w):
-        TMP[...] = nn(AT[w], proj)
-        GO[w] = TMP[pl.ds(pl.multiple_of(f * 32, 32), 32)]
-        XSO[w] = TMP[pl.ds(pl.multiple_of((1 - f) * 32, 32), 32)].astype(BF16)
-
+    for j in range(NCHIP):
+        GO[j] = nn(AT[2 * j + core], proj)
+    remote(SRO, SRO, po_s, po_r, "ctx", sib).wait_recv()
+    for j in range(NCHIP):
+        GO[j] = GO[j] + SRO[j].astype(F32)
+        XSO[j] = GO[j, pl.ds(pl.multiple_of((1 - f) * 32, 32), 32)].astype(BF16)
     pair(5, XSO, XRO).start()
-
-    for n in range(4):
-        g = nn(TT[...], HF[:, :, :, CHUNK * n : CHUNK * (n + 1)].reshape(2048, CHUNK))
-        GU[4 * n : 4 * n + 4] = g.T.reshape(4, 2, 32, UNITS)
-    XSU[...] = GU[:, 1 - f].astype(BF16)
-    pair(6, XSU, XRU).start()
-    TT[...] = ACT[...].reshape(2048, UNITS).T
-    for n in range(4):
-        g = nn(TT[...], BG[:, :, :, CHUNK * n : CHUNK * (n + 1)].reshape(2048, CHUNK))
-        GD[:, :, CHUNK * n : CHUNK * (n + 1)] = g.reshape(2, 128, CHUNK)
-    XSD[...] = GD[1 - f].astype(BF16)
-    pair(7, XSD, XRD).start()
-    recv_all(3, lambda s: AGT.at[s])
-    sent_all(3, lambda to: ATS.at[to])
+    recv_all(3, AGT.at[0:15])
+    sent_all(3, ATS.at[0:15])
 
     for j in range(8):
         t0 = AGT[2 * j].astype(F32)
@@ -471,25 +490,6 @@
     DK[...] = jnp.zeros((2, HEAD, D), F32)
     DV[...] = jnp.zeros((2, HEAD, D), F32)
 
-    def go_sum():
-        pair(5, XRO, XRO).wait_recv()
-        for j in range(NCHIP):
-            w = 2 * j + core
-            v = 2 * j + 1 - core
-            GO[w] = GO[w] + XRO[w].astype(F32)
-            SSO[j] = (GO[v] + XRO[v].astype(F32)).astype(BF16)
-        remote(SSO, SRO, po_s.at[0], po_r.at[0], "ctx", sib).start()
-
-    def go_push():
-        remote(SRO, SRO, po_s.at[0], po_r.at[0], "ctx", sib).wait_recv()
-        for j in range(NCHIP):
-            w = 2 * j + core
-            GO[w] = GO[w] + SRO[j].astype(F32)
-            PO[j] = GO[w].astype(BF16)
-        for o in range(1, NCHIP):
-            j = lax.rem(chip + o, NCHIP)
-            remote(PO.at[j], RO.at[chip], po_s.at[o], po_r.at[o], "ctx", 2 * j + core).start()
-
     def small_push():
         pair(4, SGR, SGR).wait_recv()
         SGT[...] = SG[...] + SGR[...]
@@ -505,9 +505,7 @@
     @pl.loop(0, 8)
     def _(it):
         pl.when(it == 2)(small_push)
-        pl.when(it == 3)(go_sum)
-        pl.when(it == 5)(go_push)
-        pl.when(it == 6)(up_push)
+        pl.when(it == 4)(up_push)
         m = lax.div(it, 4)
         n = lax.rem(it, 4)
         q = QT[m, :, lanes(n)]
@@ -530,6 +528,7 @@
 
     def finish_token(d, total):
         tg_ref[d] = H1[d * BLK : (d + 1) * BLK, :] + total
+        go_ref[16 * d : 16 * d + 16, :] = riders(d, chip) + RR[d, 7, BLK : BLK + 16].astype(F32)
 
     def qkv_grad():
         for n in range(4):
@@ -555,17 +554,11 @@
         QB3[c] = QB1[...]
         send_all(7, lambda to: QB1, QB3.at[c])
 
-    def out_rest():
-        for o in range(1, NCHIP):
-            j = lax.rem(chip + NCHIP - o, NCHIP)
-            remote(RO.at[j], RO.at[j], po_s.at[o], po_r.at[o], "ctx", sib).wait_recv()
-        total = GO[c]
-        for o in range(1, NCHIP):
-            total = total + RO[lax.rem(chip + o, NCHIP)].astype(F32)
-        go_ref[...] = total
+    def riders(d, ch):
+        return GO[ch, pl.ds(pl.multiple_of(f * 32 + 16 * d, 16), 16)] + XRO[ch, 16 * d : 16 * d + 16].astype(F32)
 
     def small_rest():
-        recv_all(4, lambda s: SGC.at[s])
+        recv_all(4, SGC.at[0:15])
         total = SGC[0]
         for w in range(1, NCTX):
             total = total + SGC[w]
@@ -575,7 +568,7 @@
         gd_ref[...] = GD[f] + XRD[...].astype(F32)
 
     def up_rest():
-        recv_all(5, lambda s: RU.at[s])
+        recv_all(5, RU.at[0:15])
         for w in range(NCTX):
             gu_ref[:, UNITS * w : UNITS * (w + 1)] = RU[w].astype(F32)
 
@@ -583,12 +576,12 @@
         pl.when(it == 1)(qkv_grad)
         pl.when(it == 3)(small_rest)
         pl.when(it == 4)(qkv_push)
-        pl.when(it == 5)(out_rest)
         pl.when(it == 6)(up_rest)
 
+    pair(5, XRO, XRO).wait_recv()
     ring(2, None, make_token, on_the_way, finish_token)
 
-    recv_all(6, lambda s: RQ.at[s])
+    recv_all(6, RQ.at[0:15])
     for j in range(8):
         a = RQ[2 * j].astype(F32)
         b = RQ[2 * j + 1].astype(F32)
@@ -596,7 +589,7 @@
         gq_ref[:, cols] = jnp.where(low_half, a[:, 0:128], pltpu.roll(b[:, 0:128], 64, 1))
         gq_ref[:, D + 128 * j : D + 128 * (j + 1)] = jnp.where(low_half, pltpu.roll(a[:, 0:128], 64, 1), b[:, 0:128])
         gq_ref[:, 2 * D + 128 * j : 2 * D + 128 * (j + 1)] = jnp.where(low_half, a[:, 128:256], pltpu.roll(b[:, 128:256], 64, 1))
-    recv_all(7, lambda s: QB3.at[s])
+    recv_all(7, QB3.at[0:15])
     for j in range(8):
         a = QB3[2 * j]
         b = QB3[2 * j + 1]
@@ -608,36 +601,21 @@
         for i in range(3):
             gb_ref[8 * i + j : 8 * i + j + 1, :] = rows[i][0:1, :]
 
-    @pl.loop(0, 8)
-    def _(k):
-        for d in range(2):
-            ch = chip_of(d, k)
-
-            @pl.when(k < 7)
-            def _():
-                for q in range(4):
-                    at = sub(d, ch, q)
-                    remote(at, at, agx_s.at[d, k * 4 + q], agx_r.at[d, k * 4 + q], "ctx", sib).wait_send()
-                at = WO.at[ch * 2 + core, d]
-                remote(at, at, wo_s.at[d, k], wo_r.at[d, k], "ctx", sib).wait_send()
-
-            at = WO.at[ch * 2 + core, d]
-            remote(at, at, wos_s.at[d, k], wos_r.at[d, k], "ctx", sib).wait_send()
-            whole = block(XF, d, ch, mine)
-            remote(whole, whole, sbx_s.at[d, k], sbx_r.at[d, k], "ctx", sib).wait_send()
-
-    sent_all(0, lambda to: WP.at[to])
-    sent_all(1, lambda to: VB.at[c])
-    sent_all(4, lambda to: SGT.at[:, pl.ds(pl.multiple_of(lax.div(to, 2) * 128, 128), 128)])
-    sent_all(5, lambda to: AU.at[to])
-    sent_all(6, lambda to: AQ.at[to])
-    sent_all(7, lambda to: QB1)
-    remote(SSO, SSO, po_s.at[0], po_r.at[0], "ctx", sib).wait_send()
-    for o in range(1, NCHIP):
-        j = lax.rem(chip + o, NCHIP)
-        remote(PO.at[j], PO.at[j], po_s.at[o], po_r.at[o], "ctx", sib).wait_send()
-    for i, at in enumerate((vec_ref, wo_ref, wd_ref, WB.at[:, f], SG, XSO, XSU, XSD, XSQ)):
+    remote(XF.at[0, 0:7], XF.at[0, 0:7], agx_s, sbx_r, "ctx", sib).wait_send()
+    remote(XF.at[0], XF.at[0], sbx_s, sbx_r, "ctx", sib).wait_send()
+    remote(WO.at[0:7], WO.at[0:7], wo_s, sbx_r, "ctx", sib).wait_send()
+    remote(WO.at[0:8], WO.at[0:8], wos_s, sbx_r, "ctx", sib).wait_send()
+    sent_all(0, WP.at[0:15])
+    sent_all(1, VB.at[0:15])
+    sent_all(4, SGC.at[0:15])
+    sent_all(5, AU.at[0:15])
+    sent_all(6, AQ.at[0:15])
+    sent_all(7, QB3.at[0:15])
+    remote(SSO, SSO, po_s, po_r, "ctx", sib).wait_send()
+    sent_all(8, WU.at[0:15, 0])
+    for i, at in enumerate((VEC, wo_ref, wd_ref, WB.at[:, f], SG, XSO, XSU, XSD, XSQ)):
         pair(i, at, at).wait_send()
+    pair(10, WU.at[:, f], WU.at[:, f]).wait_send()
 
 
 def rope_tables():
@@ -650,15 +628,10 @@
     tokens, cotangent, qkv_weight, out_weight, up_weight, down_weight, qkv_bias, out_bias, up_bias, down_bias,
     first_gain, first_shift, second_gain, second_shift,
 ):
-    def wide(v):
-        return jnp.pad(v.astype(F32), (0, 128 - v.shape[0]))
-
-    vec = jnp.stack(
-        [wide(v) for v in (up_bias, qkv_bias, out_bias, down_bias, first_gain, first_shift, second_gain, second_shift)]
-    )
     scratch = [
+        ((8, 128), F32),
         ((2, 8, 128, D), BF16), ((2, 8, 128, D), BF16), ((2, 8, 128, D), BF16),
-        ((16, 32, 512), BF16), ((16, 2, 32, 512), BF16), ((16, 2, 32, D), BF16), ((2, 128, D), BF16),
+        ((16, 32, 256), BF16), ((16, 2, 32, 256), BF16), ((16, 2, 32, UNITS), BF16), ((16, 2, 32, D), BF16), ((2, 128, D), BF16),
         ((16, 2, 8, 128), F32), ((8, D), F32), ((8, UNITS), F32), ((24, 128), F32), ((3, 128, 128), F32),
         ((256, D), BF16),
         ((2, 64, D), BF16), ((2, 64, D), BF16), ((2, 64, D), BF16), ((2, D, 64), BF16), ((2, D, 64), BF16),
@@ -667,36 +640,64 @@
         ((128, D), F32), ((128, D), F32), ((128, 128), F32), ((128, D), F32), ((128, D), F32),
         ((2, 8, 128, UNITS), F32), ((2, 8, 128, UNITS), BF16), ((2, 8, 128, UNITS), BF16),
         ((2, 3, 128, D), F32),
-        ((2, 8, BLK, D), BF16), ((2, 8, BLK, D), BF16), ((2, 8, BLK, D), BF16), ((2, 8, BLK, D), BF16),
-        ((UNITS, 2048), BF16), ((64, D), F32),
+        ((2, 8, BLK, D), BF16), ((2, 8, BLK, D), BF16), ((2, 8, 80, D), BF16), ((2, 8, 80, D), BF16),
+        ((UNITS, 2048), BF16),
         ((16, 2, 32, UNITS), F32), ((16, 32, UNITS), BF16), ((16, 32, UNITS), BF16), ((16, 32, UNITS), BF16), ((16, 32, UNITS), BF16),
         ((2, 128, D), F32), ((128, D), BF16), ((128, D), BF16),
-        ((16, 32, D), F32), ((16, 32, D), BF16), ((16, 32, D), BF16),
-        ((8, 32, D), BF16), ((8, 32, D), BF16), ((8, 32, D), BF16), ((8, 32, D), BF16),
+        ((8, BLK, D), F32), ((8, 32, D), BF16), ((8, 32, D), BF16), ((8, BLK, D), BF16), ((8, BLK, D), BF16),
         ((8, D), F32), ((8, D), F32), ((8, D), F32), ((16, 8, 128), F32), ((2, 64, D), BF16),
         ((2, 64, D), F32), ((2, 64, D), F32), ((2, 192, D), BF16),
         ((16, 32, UNITS), BF16), ((16, 32, UNITS), BF16), ((16, 32, UNITS), BF16), ((16, 32, UNITS), BF16),
         ((8, 256), F32), ((8, 256), F32), ((16, 8, 256), F32),
     ]
-    sems = [(2, 32)] * 2 + [(2, 8)] * 2 + [(2, 2, 8)] * 4 + [(3, 2, 8)] * 4 + [(2, 8)] * 4 + [(8, 16)] * 2 + [(10,)] * 2 + [(8,)] * 2
+    sems = [(12,), (2, 8 * AQS), (2, 8), (2, 8), (2, 8 * RQS), (2, 8), (9,), (9,), (11,), (11,)]
     vmem = pl.BlockSpec(memory_space=pltpu.VMEM)
     shapes = [((2, BLK, D), BF16), ((2, BLK, D), F32), ((32, 3 * D), F32), ((32, D), F32), ((32, 4 * D), F32), ((128, D), F32), ((8, 128), F32), ((24, 128), F32)]
-    output, token_grad, qkv_grad, out_grad, up_grad, down_grad, small, qkv_small = pl.pallas_call(
+    bias = (up_bias, qkv_bias, out_bias, down_bias, first_gain, first_shift, second_gain, second_shift)
+    made = pl.pallas_call(
         layer_kernel,
         out_shape=[jax.ShapeDtypeStruct(s, t) for s, t in shapes],
-        in_specs=[vmem] * 8,
+        in_specs=[vmem] * 15,
         out_specs=[vmem] * 8,
         scratch_shapes=[pltpu.VMEM(s, t) for s, t in scratch] + [pltpu.SemaphoreType.DMA(s) for s in sems],
         compiler_params=pltpu.CompilerParams(collective_id=0, has_side_effects=True, vmem_limit_bytes=VMEM_LIMIT),
         name="layer",
-    )(tokens[:, 0], cotangent[:, 0], qkv_weight, out_weight, up_weight, down_weight, vec, jnp.asarray(rope_tables()))
+    )(
+        tokens[:, 0], cotangent[:, 0], qkv_weight, out_weight, up_weight, down_weight, jnp.asarray(rope_tables()),
+        *(v[None] for v in bias),
+    )
+    anywhere = pl.BlockSpec(memory_space=pl.ANY)
+    widths = (96, 32, 128, 32, 32, 32, 32, 32)
+    last = pl.pallas_call(
+        finish_kernel,
+        out_shape=[jax.ShapeDtypeStruct(s, t) for s, t in shapes[:6]] + [jax.ShapeDtypeStruct((1, w), F32) for w in widths],
+        in_specs=[anywhere] * 6 + [vmem] * 2,
+        out_specs=[vmem] * 14,
+        scratch_shapes=[pltpu.SemaphoreType.DMA((6,))],
+        name="finish",
+    )(*made)
+    return (last[0][:, None], last[1][:, None], *last[2:6], *(v[0] for v in last[6:]))
+
+
+def finish_kernel(*refs):
+    big, (gs, gb), done, small, sems = refs[:6], refs[6:8], refs[8:14], refs[14:22], refs[22]
+    copies = [pltpu.make_async_copy(a, b, sems.at[i]) for i, (a, b) in enumerate(zip(big, done))]
+    for copy in copies:
+        copy.start()
     index = lax.axis_index("ctx") * 2 + lax.axis_index("fsdp")
-    part = lax.dynamic_slice_in_dim(small, 32 * lax.rem(index, 4), 32, 1)
-    qkv_part = lax.dynamic_slice_in_dim(qkv_small.reshape(3 * D), 96 * index, 96, 0)
-    return (
-        output[:, None], token_grad[:, None], qkv_grad, out_grad, up_grad, down_grad,
-        qkv_part, part[0], small[6], part[1], part[2], part[3], part[4], part[5],
-    )
+    place = lax.rem(index, 4)
+    turned = pltpu.roll(gs[...], lax.rem(128 - 32 * place, 128), 1)
+    for ref, row in zip(small[1:], (0, 6, 1, 2, 3, 4, 5)):
+        ref[...] = gs[6:7, :] if row == 6 else turned[row : row + 1, 0:32]
+    offset = lax.rem(96 * index, 128)
+    row = lax.div(96 * index, 128)
+    lane = lax.broadcasted_iota(jnp.int32, (1, 128), 1)
+    back = lax.rem(128 - offset, 128)
+    one = pltpu.roll(gb[pl.ds(row, 1), :], back, 1)
+    two = pltpu.roll(gb[pl.ds(lax.rem(row + 1, 24), 1), :], back, 1)
+    small[0][...] = jnp.where(lane < 128 - offset, one, two)[:, 0:96]
+    for copy in copies:
+        copy.wait()
 
 
 VMEM_LIMIT = 63 * 1024 * 1024

time: 290 us -> 233 us (0.80)
  Pallas kernels: 275 us -> 232 us
  local copies, waits for them, and re-layouts: 13.7 us -> 0 us
    pallas_call x1, Pallas kernels: 275 us -> 228 us  [fused_body(): pl.pallas_call(layer_kernel, out_shape=[jax.ShapeDtypeStruct(s, t) for s,...]
    unnamed x32 -> x0, local copies, waits for them, and re-layouts: 9.82 us -> none
    pallas_call x0 -> x1, Pallas kernels: none -> 3.79 us  [fused_body(): pl.pallas_call(finish_kernel, out_shape=[jax.ShapeDtypeStruct(s, t) for s...]
where the time goes in v2:
time: 233 us
  Pallas kernels  232 us (100%)
    pallas_call x1, Pallas kernels, fused_body(): pl.pallas_call(layer_kernel, out_shape=[jax.ShapeDtypeStruct(s, t) for s,...  228 us

profile of v2, /device:TPU:0, one launch (start us, length us, event | category | flops | bytes accessed | tf_op | source)
XLA Modules:
  0.0 232.9 jit_solution(8301680160885735630)
XLA Ops:
  0.7 228.3 %layer.1 = (bf16[2,64,1024]{2,1,0:T(8,128)(2,1)}, f32[2,64,1024]{2,1,0:T(8,128)}, f32[32,3072]{1,0:T(8,128)}, f32[32,1024]{1,0:T(8,128)}, f32[32,4096]{1,0:T(8,1...) custom-call(bf16[2,64,1024]{2,1,0:T(8,128)(2,1)} %bitcast.24, bf16[2,64,1024]{2,1,0:T(8,128)(2,1)} %bitcast.25, ...), custom_call_target="tpu_custom_call" | custom-call | tf_op jit(solution)/shard_map/layer/pallas_call | solution.py:657
  228.9 3.8 %finish.1 = (bf16[2,64,1024]{2,1,0:T(8,128)(2,1)}, f32[2,64,1024]{2,1,0:T(8,128)}, f32[32,3072]{1,0:T(8,128)}, f32[32,1024]{1,0:T(8,128)}, f32[32,4096]{1,0:T(8,...) custom-call(bf16[2,64,1024]{2,1,0:T(8,128)(2,1)} %get-tuple-element., ...), custom_call_target="tpu_custom_call" | custom-call | tf_op jit(solution)/shard_map/finish/pallas_call | solution.py:671

commit v3 on v2

--- a/solution.py
+++ b/solution.py
@@ -22,9 +22,10 @@
 BLK = 64
 D = 1024
 UNITS = 256
+FF_UNITS = 512
 CHUNK = 256
 AQS = 2
-RQS = 2
+RQS = 4
 ROWS = BLK // RQS
 
 
@@ -55,12 +56,13 @@
 
 def layer_kernel(
     x_ref, ct_ref, wq_ref, wo_ref, wu_ref, wd_ref, rope_ref, v0, v1, v2, v3, v4, v5, v6, v7,
-    out_ref, tg_ref, gq_ref, go_ref, gu_ref, gd_ref, gs_ref, gb_ref,
-    VEC, XF, HF, BG, WP, WB, WU, WO, WD, VB, VF, UB, QBR, BQ, WHT, QT, KT, VT, KN, VN, PT, ATD, ATS, AT, AGT,
+    out_ref, tg_ref, RQ, go_ref, RU, gd_ref, gs_ref,
+    VEC, XF, HF, BG, WP, WB, WUS, WU, WO, WD, VB, VF, UB, QBR, BQ, WHT, QT, KT, VT, KN, VN, PT, ATD, ATS, AT, AGT,
     H1, Z1, R1, SEC, G2, DG, ACT, PG, PB, SS, SR, RSD, RR, TT,
-    GU, XSU, XRU, AU, RU, GD, XSD, XRD, GO, XSO, XRO, SSO, SRO, SG, SGR, SGT, SGC, AGQ,
-    DK, DV, JG, XSQ, XRQ, AQ, RQ, QB1, QB2, QB3,
-    one, ag_r, sb_r, ss_r, rs_r, wo_r, all_s, all_r, pair_s, pair_r,
+    GU, PUS, DWU, DWD, ZRU, ZRD, GO, XSO, XRO, SSO, SRO, SG, SGR, SGT, SGC, AGQ,
+    DK, DV, JG, XSQ, XRQ, AQ, QBP,
+    one, ag_r, ss_r, rs_r, wo_r, all_s, all_r, pair_s, pair_r, plane_s, plane_r,
+    pa_r, pb_r, ps_r, pr_r, z_s, z_r, q_s, q_r,
 ):
     c = lax.axis_index("ctx")
     f = lax.axis_index("fsdp")
@@ -100,18 +102,113 @@
     def sent_all(e, slab):
         remote(slab, slab, all_s.at[e], all_r.at[e], "ctx", sib).wait_send()
 
+    pp = lax.rem(c, 4) * 2 + f
+    grp = yy * 2 + f
+
+    def send_plane(e, src_at, dst):
+        @pl.loop(1, 8)
+        def _(o):
+            to = lax.rem(pp + o, 8)
+            pltpu.make_async_remote_copy(
+                src_ref=src_at(to), dst_ref=dst, send_sem=plane_s.at[e], recv_sem=plane_r.at[e],
+                device_id={"ctx": zz * 4 + lax.div(to, 2), "fsdp": lax.rem(to, 2)}, device_id_type=MESH,
+            ).start()
+
+    def recv_plane(e, slab):
+        remote(slab, slab, plane_s.at[e], plane_r.at[e], "ctx", sib).wait_recv()
+
+    def sent_plane(e, slab):
+        remote(slab, slab, plane_s.at[e], plane_r.at[e], "ctx", sib).wait_send()
+
+    def at_plane(body):
+        for place in range(4):
+
+            @pl.when(zz == place)
+            def _():
+                body(place)
+
+    def z_block(kd, b, dr, s, place):
+        at = (WU, WD)[kd].at[b]
+        return remote(at, at, z_s.at[kd, dr * 3 + s], z_r.at[kd, b], "ctx", c + (4 if dr == 0 else -4))
+
+    def z_gather(kd, s, sent=False):
+        def body(place):
+            for dr in range(2):
+                b = place - s if dr == 0 else place + s
+                more = place < 3 if dr == 0 else place > 0
+                if not 0 <= b < 4:
+                    continue
+                if s > 0 and not sent:
+                    z_block(kd, b, dr, s - 1, place).wait_recv()
+                if s < 3 and more:
+                    copy = z_block(kd, b, dr, s, place)
+                    copy.wait_send() if sent else copy.start()
+
+        at_plane(body)
+
+    def z_slot(source, t):
+        return (source - t) % 4 - 1
+
+    def z_term(kd, t, there, slot, place):
+        src, got = ((DWU, ZRU), (DWD, ZRD))[kd]
+        return remote(src.at[t], got.at[slot], q_s.at[kd, t], q_r.at[kd, slot], "ctx", c + 4 * (there - place))
+
+    def z_start(kd, sent=False):
+        def body(place):
+            for t in (3, 2, 1, 0) if place < 2 else (0, 1, 2, 3):
+                if t == place or (place, t) in ((1, 3), (2, 0)):
+                    continue
+                far = (place, t) in ((0, 3), (3, 0))
+                there = (1 if place == 0 else 2) if far else t
+                copy = z_term(kd, t, there, 3 if far else z_slot(place, t), place)
+                copy.wait_send() if sent else copy.start()
+
+        at_plane(body)
+
+    def z_relay(kd, sent=False):
+        def body(place):
+            if place in (1, 2):
+                t = 3 if place == 1 else 0
+                src, got = ((DWU, ZRU), (DWD, ZRD))[kd]
+                copy = z_term(kd, t, t, z_slot(place, t), place)
+                if sent:
+                    copy.wait_send()
+                else:
+                    z_term(kd, t, t, 3, place).wait_recv()
+                    src[t] = (src[t].astype(F32) + got[3].astype(F32)).astype(BF16)
+                    copy.start()
+
+        at_plane(body)
+
+    def z_total(kd, put):
+        def body(place):
+            src, got = ((DWU, ZRU), (DWD, ZRD))[kd]
+            total = src[place].astype(F32)
+            for source in range(4):
+                if source != place and (source, place) not in ((0, 3), (3, 0)):
+                    slot = z_slot(source, place)
+                    z_term(kd, place, place, slot, place).wait_recv()
+                    total = total + got[slot].astype(F32)
+            put(total)
+
+        at_plane(body)
+
     def pair(i, src, dst):
         return remote(src, dst, pair_s.at[i], pair_r.at[i], "fsdp", 1 - f)
 
-    agx_s, sbx_s, sbx_r, ag_s, sb_s, ss_s, rs_s, wo_s, wos_s, wos_r, po_s, po_r = (one.at[i] for i in range(12))
+    agx_s, sbx_s, sbx_r, ss_s, rs_s, wo_s, wos_s, wos_r, po_s, po_r, pa_s, pb_s, ps_s, pr_s = (one.at[i] for i in range(14))
     barrier = pltpu.get_barrier_semaphore()
 
     @pl.loop(1, NCTX)
     def _(o):
         pl.semaphore_signal(barrier, inc=1, device_id={"ctx": lax.rem(c + o, NCTX)}, device_id_type=MESH)
 
-    pl.semaphore_signal(barrier, inc=1, device_id={"fsdp": 1 - f}, device_id_type=MESH)
-    pl.semaphore_wait(barrier, NCTX)
+    @pl.loop(0, 4)
+    def _(o):
+        there = lax.div(c, 4) * 4 + lax.rem(c + o, 4)
+        pl.semaphore_signal(barrier, inc=1, device_id={"ctx": there, "fsdp": 1 - f}, device_id_type=MESH)
+
+    pl.semaphore_wait(barrier, NCTX + 3)
 
     def block(buf, m, ch, row0):
         return buf.at[m, ch, pl.ds(row0, BLK)]
@@ -122,7 +219,7 @@
     for m in range(2):
         XF[m, chip, pl.ds(mine, BLK)] = x_ref[m]
     WO[c, f] = wo_ref[...]
-    WD[f] = wd_ref[...]
+    WD[zz] = wd_ref[...]
     VEC[...] = jnp.zeros((8, 128), F32)
     for i, v in enumerate((v0, v1, v2, v3, v4, v5, v6, v7)):
         VEC[i : i + 1, 0 : v.shape[1]] = v[...].astype(F32)
@@ -174,21 +271,26 @@
             WP[w, :, 128:256] = (vt if e == 0 else pltpu.roll(vt, 64, 1)).astype(BF16)
     WB[c, f] = WP[c]
     send_all(0, lambda to: WP.at[to], WB.at[c, f])
+    for w in range(8):
+        for i in range(4):
+            WUS[w, :, 128 * i : 128 * (i + 1)] = wu_ref[:, 128 * (8 * i + w) : 128 * (8 * i + w + 1)]
+    WU[zz, pp] = WUS[pp]
+    send_plane(0, lambda to: WUS.at[to], WU.at[zz, pp])
     pl.loop(1, 4)(gather_x)
     pair(0, VB.at[c, 1 - f], VB.at[c, 1 - f]).wait_recv()
     send_all(1, lambda to: VB.at[c], VB.at[c])
     recv_all(0, WB.at[0:15, 0])
     pair(3, WB.at[:, f], WB.at[:, f]).start()
     pair(1, WO.at[c, 1 - f], WO.at[c, 1 - f]).wait_recv()
+    recv_plane(0, WU.at[zz, 0:7])
 
     @pl.loop(4, 8)
     def _(k):
         gather_x(k)
         gather_wo(k - 4)
-
-    WU[c, f] = wu_ref[:, pl.ds(pl.multiple_of(c * UNITS, UNITS), UNITS)]
-    send_all(8, lambda to: wu_ref.at[:, pl.ds(pl.multiple_of(to * UNITS, UNITS), UNITS)], WU.at[c, f])
-    pair(2, wd_ref, WD.at[f]).start()
+        pl.when(k == 4)(lambda: z_gather(0, 0))
+        pl.when(k == 6)(lambda: z_gather(1, 0))
+
 
     remote(XF.at[0], XF.at[0], sbx_s, sbx_r, "ctx", sib).wait_recv()
     recv_all(1, VB.at[0:15])
@@ -209,8 +311,8 @@
         )
         for i in range(3):
             QBR[3 * j + i : 3 * j + i + 1, :] = rows[i][1:2, :]
-    UB[0:1, 0:128] = VB[c, 0, 0:1, :]
-    UB[0:1, 128:256] = VB[c, 1, 0:1, :]
+    for i in range(4):
+        UB[0:1, 128 * i : 128 * (i + 1)] = VB[4 * i + lax.rem(c, 4), f, 0:1, :]
     for i in range(3):
         row = QBR[pl.ds(8 * i + chip, 1), :]
         BQ[i] = jnp.broadcast_to(row, (128, 128)).T
@@ -254,11 +356,12 @@
         def _():
             gather_wo(4 + lax.div(it, 2))
 
-        @pl.when(it == 5)
+        @pl.when(it == 4)
         def _():
-            recv_all(8, WU.at[0:15, 0])
-            pair(10, WU.at[:, f], WU.at[:, f]).start()
-
+            pass
+
+        pl.when(it == 0)(lambda: z_gather(0, 1))
+        pl.when(it == 5)(lambda: z_gather(1, 1))
         m = lax.div(it, 4)
         n = lax.rem(it, 4)
         s = nn(KN[m], QT[m, :, lanes(n)]) * 0.125
@@ -276,8 +379,10 @@
     send_all(2, lambda to: ATS.at[to], AT.at[c])
 
     remote(WO.at[0:8], WO.at[0:8], wos_s, wos_r, "ctx", sib).wait_recv()
+    z_gather(0, 2)
     recv_all(2, AT.at[0:15])
 
+    z_gather(1, 2)
     att_rows = AT[...].reshape(D, 128).T
     resid = x_ref[...].reshape(128, D).astype(F32) + nn(att_rows, WO[...].reshape(D, D)) + VF[2:3, :]
     center = resid - row_mean(resid)
@@ -289,33 +394,91 @@
     H1[...] = hidden
     hidden_low = hidden.astype(BF16)
     for m in range(2):
-        HF[m, chip, pl.ds(mine, BLK)] = hidden_low[m * BLK : (m + 1) * BLK]
-
-    pair(2, WD.at[1 - f], WD.at[1 - f]).wait_recv()
-    pair(10, WU.at[:, 1 - f], WU.at[:, 1 - f]).wait_recv()
-
-    def ring(p, buf, make, extra, finish):
+        HF[grp, m, pl.ds(mine, BLK)] = hidden_low[m * BLK : (m + 1) * BLK]
+
+    def plane(buf, make, ready, after_one, after_two, finish):
+        far = ((yy * 2 + 1 - f), ((1 - yy) * 2 + f))
+        groups = tuple((grp, far[m], far[1 - m], (1 - yy) * 2 + 1 - f) for m in range(2))
+
+        def to(axis, src, dst, ss, rs):
+            if axis == 0:
+                return remote(src, dst, ss, rs, "fsdp", 1 - f)
+            return remote(src, dst, ss, rs, "ctx", c + 2 - 4 * yy)
+
+        def at(m, i, row0):
+            return buf.at[groups[m][i], m, pl.ds(row0, BLK)]
+
+        def hand_over(m, i):
+            remote(at(m, i, mine), at(m, i, mine), pb_s, pb_r.at[m, i], "ctx", sib).start()
+
+        def arrive(m, i, n):
+            to(m, at(m, i, mine), at(m, i, mine), pa_s, pa_r.at[m, n]).wait_recv()
+
+        def work(m, i):
+            remote(at(m, i, other), at(m, i, other), pb_s, pb_r.at[m, i], "ctx", sib).wait_recv()
+            PB[m, i] = make(groups[m][i], m)
+            SS[m, i] = PB[m, i, pl.ds(other, BLK)].astype(BF16)
+            remote(SS.at[m, i], SR.at[m, i], ps_s, ps_r.at[m, i], "ctx", sib).start()
+
+        def share(m, i):
+            remote(SR.at[m, i], SR.at[m, i], ps_s, ps_r.at[m, i], "ctx", sib).wait_recv()
+            return PB[m, i, pl.ds(mine, BLK)] + SR[m, i].astype(F32)
+
+        def push(m, n, value, axis):
+            RSD[m, n, 0:BLK] = value.astype(BF16)
+            to(axis, RSD.at[m, n, pl.ds(0, BLK)], RR.at[m, n, pl.ds(0, BLK)], pr_s, pr_r.at[m, n]).start()
+
+        def pulled(m, n):
+            got = RR.at[m, n, pl.ds(0, BLK)]
+            to(m, got, got, pr_s, pr_r.at[m, n]).wait_recv()
+            return RR[m, n, 0:BLK].astype(F32)
+
+        for m in range(2):
+            to(m, at(m, 0, mine), at(m, 0, mine), pa_s, pa_r.at[m, 0]).start()
+        for m in range(2):
+            hand_over(m, 0)
+            to(1 - m, at(m, 0, mine), at(m, 0, mine), pa_s, pa_r.at[m, 1]).start()
+        if ready is None:
+            for m in range(2):
+                work(m, 0)
+        for m in range(2):
+            arrive(m, 1, 0)
+            to(1 - m, at(m, 1, mine), at(m, 1, mine), pa_s, pa_r.at[m, 2]).start()
+            hand_over(m, 1)
+        for m in range(2):
+            arrive(m, 2, 1)
+            hand_over(m, 2)
+        if ready is None:
+            for m in range(2):
+                work(m, 1)
+        for m in range(2):
+            arrive(m, 3, 2)
+            hand_over(m, 3)
+        if ready is not None:
+            ready()
+        for i in (2, 3) if ready is None else (3, 2, 1, 0):
+            for m in range(2):
+                work(m, i)
+        for m in range(2):
+            push(m, 1, share(m, 3), 1 - m)
+        for m in range(2):
+            push(m, 0, share(m, 2), 1 - m)
+        after_one()
+        for m in range(2):
+            push(m, 2, share(m, 1) + pulled(m, 1), m)
+        after_two()
+        for m in range(2):
+            finish(m, share(m, 0) + pulled(m, 0) + pulled(m, 2))
+        remote(XF.at[0, 0:3], XF.at[0, 0:3], pa_s, sbx_r, "ctx", sib).wait_send()
+        remote(XF.at[0, 0:4], XF.at[0, 0:4], pb_s, sbx_r, "ctx", sib).wait_send()
+        remote(XF.at[0, 0:4], XF.at[0, 0:4], ps_s, sbx_r, "ctx", sib).wait_send()
+        remote(XF.at[0, 0:3], XF.at[0, 0:3], pr_s, sbx_r, "ctx", sib).wait_send()
+
+    def ring(make, extra, finish):
         def first(k):
             slot = 2 - lax.div(k + 7, 8) * (2 - lax.rem(k, 2))
             for d in range(2):
                 ch = chip_of(d, k)
-                if buf is not None:
-                    at = block(buf, d, ch, mine)
-
-                    @pl.when(k > 0)
-                    def _():
-                        remote(at, at, ag_s, ag_r.at[d, k - 1], "ctx", target(d)).wait_recv()
-
-                    @pl.when(k < 7)
-                    def _():
-                        remote(at, at, ag_s, ag_r.at[d, k], "ctx", target(d)).start()
-
-                    remote(at, at, sb_s, sb_r.at[d, k], "ctx", sib).start()
-            for d in range(2):
-                ch = chip_of(d, k)
-                if buf is not None:
-                    at = block(buf, d, ch, other)
-                    remote(at, at, sb_s, sb_r.at[d, k], "ctx", sib).wait_recv()
                 PB[d, slot] = make(d, ch)
                 SS[d, k] = PB[d, slot, pl.ds(other, BLK)].astype(BF16)
                 remote(SS.at[d, k], SR.at[d, k], ss_s, ss_r.at[d, k], "ctx", sib).start()
@@ -329,7 +492,7 @@
             remote(got, got, rs_s, rs_r.at[d, k * RQS + q], "ctx", sib).wait_recv()
 
         def rows_of(q):
-            return pl.ds(q * ROWS, ROWS if p < 2 or q < RQS - 1 else ROWS + 16)
+            return pl.ds(q * ROWS, ROWS if q < RQS - 1 else ROWS + 16)
 
         def second(k):
             slot = lax.rem(k, 2)
@@ -339,7 +502,7 @@
                 for d in range(2):
                     part = pl.ds(q * ROWS, ROWS)
                     total = PB[d, slot, pl.ds(pl.multiple_of(core * BLK + q * ROWS, ROWS), ROWS)] + SR[d, k, part].astype(F32)
-                    rider = p == 2 and q == RQS - 1
+                    rider = q == RQS - 1
                     if rider:
                         ride = riders(d, chip_of(d, k))
 
@@ -379,35 +542,35 @@
                 arrived(d, q, 7)
             finish(d, PB[d, 2, pl.ds(mine, BLK)] + SR[d, 0].astype(F32) + RR[d, 7, 0:BLK].astype(F32))
 
-        if buf is not None:
-            remote(buf.at[0, 0:7], buf.at[0, 0:7], ag_s, sbx_r, "ctx", sib).wait_send()
-            remote(buf.at[0], buf.at[0], sb_s, sbx_r, "ctx", sib).wait_send()
         remote(SS, SS, ss_s, sbx_r, "ctx", sib).wait_send()
-        sent = SS.at[:, 0:7] if p < 2 else RSD.at[:, 0:7]
-        remote(sent, sent, rs_s, sbx_r, "ctx", sib).wait_send()
-
-    def nothing(it):
+        remote(RSD.at[:, 0:7], RSD.at[:, 0:7], rs_s, sbx_r, "ctx", sib).wait_send()
+
+    def nothing():
         pass
 
     def up_w():
-        return WU[...].reshape(D, UNITS)
+        return WU[...].reshape(D, FF_UNITS)
 
     def down_w():
-        return WD[...].reshape(UNITS, D)
-
-    def make_up(m, ch):
-        u = nn(HF[m, ch], up_w()) + UB[0:1, :]
+        return WD[...].reshape(FF_UNITS, D)
+
+    def make_up(g, m):
+        u = nn(HF[g, m], up_w()) + UB[0:1, :]
         phi = 0.5 * (1.0 + lax.erf(u * 0.7071067811865476))
         a = (u * phi).astype(BF16)
-        DG[m, ch] = phi + u * (jnp.exp(-0.5 * u * u) * 0.3989422804014327)
-        ACT[m, ch] = a
+        DG[g, m] = phi + u * (jnp.exp(-0.5 * u * u) * 0.3989422804014327)
+        ACT[g, m] = a
         return nn(a, down_w())
 
     def finish_up(d, total):
         rows = slice(d * BLK, (d + 1) * BLK)
         SEC[rows, :] = H1[rows, :] + total + VF[3:4, :]
 
-    ring(0, HF, make_up, nothing, finish_up)
+    def weights_in():
+        z_gather(0, 3)
+        z_gather(1, 3)
+
+    plane(HF, make_up, weights_in, nothing, nothing, finish_up)
 
     resid = SEC[...]
     center = resid - row_mean(resid)
@@ -424,34 +587,34 @@
     grad_low = grad.astype(BF16)
     SG[1:2, :] = col_sum(grad_low.astype(F32))
     for m in range(2):
-        BG[m, chip, pl.ds(mine, BLK)] = grad_low[m * BLK : (m + 1) * BLK]
-
-    def make_down(m, ch):
-        pg = (nt(BG[m, ch], down_w()) * DG[m, ch]).astype(BF16)
-        PG[m, ch] = pg
+        BG[grp, m, pl.ds(mine, BLK)] = grad_low[m * BLK : (m + 1) * BLK]
+
+    def make_down(g, m):
+        pg = (nt(BG[g, m], down_w()) * DG[g, m]).astype(BF16)
+        PG[g, m] = pg
         return nt(pg, up_w())
 
     def finish_down(d, total):
         rows = slice(d * BLK, (d + 1) * BLK)
         SEC[rows, :] = G2[rows, :] + total
 
-    def ff_grads():
-        TT[...] = ACT[...].reshape(2048, UNITS).T
-        for n in range(4):
-            g = nn(TT[...], BG[:, :, :, CHUNK * n : CHUNK * (n + 1)].reshape(2048, CHUNK))
-            GD[:, :, CHUNK * n : CHUNK * (n + 1)] = g.reshape(2, 128, CHUNK)
-        XSD[...] = GD[1 - f].astype(BF16)
-        pair(7, XSD, XRD).start()
-        ones = jnp.ones((8, 2048), BF16)
-        SG[6:7, 0:256] = nn(ones, PG[...].reshape(2048, UNITS))[0:1, :]
-        TT[...] = PG[...].reshape(2048, UNITS).T
-        for n in range(4):
-            g = nn(TT[...], HF[:, :, :, CHUNK * n : CHUNK * (n + 1)].reshape(2048, CHUNK))
-            GU[4 * n : 4 * n + 4] = g.T.reshape(4, 2, 32, UNITS)
-        XSU[...] = GU[:, 1 - f].astype(BF16)
-        pair(6, XSU, XRU).start()
-
-    ring(1, BG, make_down, lambda it: pl.when(it == 8)(ff_grads), finish_down)
+    def down_grads():
+        TT[...] = ACT[...].reshape(1024, FF_UNITS).T
+        for i in range(4):
+            DWD[i] = nn(TT[128 * i : 128 * (i + 1), :], BG[...].reshape(1024, D)).astype(BF16)
+        z_start(1)
+
+    def up_grads():
+        TT[...] = PG[...].reshape(1024, FF_UNITS).T
+        for i in range(4):
+            g = nn(TT[...], HF[:, :, :, CHUNK * i : CHUNK * (i + 1)].reshape(1024, CHUNK))
+            DWU[i] = g.T.astype(BF16).reshape(8, 32, FF_UNITS)
+        z_start(0)
+        sums = nn(jnp.ones((8, 1024), BF16), PG[...].reshape(1024, FF_UNITS))[0:1, :]
+        for i in range(8):
+            SG[6:7, 128 * i : 128 * (i + 1)] = sums[:, 128 * (i // 2) : 128 * (i // 2) + 128]
+
+    plane(BG, make_down, None, down_grads, up_grads, finish_down)
 
     hid = SEC[...]
     z = Z1[...]
@@ -493,19 +656,23 @@
     def small_push():
         pair(4, SGR, SGR).wait_recv()
         SGT[...] = SG[...] + SGR[...]
+        SGT[6:7, :] = SG[6:7, :]
         SGC[c] = SGT[:, pl.ds(pl.multiple_of(chip * 128, 128), 128)]
         send_all(4, lambda to: SGT.at[:, pl.ds(pl.multiple_of(lax.div(to, 2) * 128, 128), 128)], SGC.at[c])
 
     def up_push():
-        pair(6, XRU, XRU).wait_recv()
-        AU[...] = (GU[:, f] + XRU[...].astype(F32)).astype(BF16)
-        RU[c] = AU[c]
-        send_all(5, lambda to: AU.at[to], RU.at[c])
+        def put(total):
+            PUS[...] = total.astype(BF16)
+
+        z_total(0, put)
+        RU[pp] = PUS[pp]
+        send_plane(1, lambda to: PUS.at[to], RU.at[pp])
 
     @pl.loop(0, 8)
     def _(it):
         pl.when(it == 2)(small_push)
-        pl.when(it == 4)(up_push)
+        pl.when(it == 0)(lambda: z_relay(1))
+        pl.when(it == 5)(lambda: z_relay(0))
         m = lax.div(it, 4)
         n = lax.rem(it, 4)
         q = QT[m, :, lanes(n)]
@@ -530,29 +697,29 @@
         tg_ref[d] = H1[d * BLK : (d + 1) * BLK, :] + total
         go_ref[16 * d : 16 * d + 16, :] = riders(d, chip) + RR[d, 7, BLK : BLK + 16].astype(F32)
 
-    def qkv_grad():
-        for n in range(4):
-            cols = slice(CHUNK * n, CHUNK * (n + 1))
-            g = nn(JG[0], XF[0, :, :, cols].reshape(D, CHUNK)) + nn(JG[1], XF[1, :, :, cols].reshape(D, CHUNK))
-            g = jnp.concatenate([g, jnp.zeros((64, CHUNK), F32)], axis=0)
-            GU[4 * n : 4 * n + 4] = g.T.reshape(4, 2, 32, UNITS)
+    def qkv_bias_rows():
+        b = nt(jnp.ones((8, D), BF16), JG[0]) + nt(jnp.ones((8, D), BF16), JG[1])
+        b = jnp.concatenate([b, jnp.zeros((8, 64), F32)], axis=1)
+        QBP[...] = jnp.zeros((32, UNITS), F32)
+        QBP[0:1, 128:256] = jnp.where(low_half, 0.0, pltpu.roll(b[0:1, 0:128], 64, 1))
+        QBP[1:2, 128:256] = jnp.where(low_half, 0.0, b[0:1, 0:128])
+        QBP[2:3, 128:256] = jnp.where(low_half, 0.0, pltpu.roll(b[0:1, 128:256], 64, 1))
+
+    def qkv_grad(n):
+        cols = slice(CHUNK * n, CHUNK * (n + 1))
+        g = nn(JG[0], XF[0, :, :, cols].reshape(D, CHUNK)) + nn(JG[1], XF[1, :, :, cols].reshape(D, CHUNK))
+        g = jnp.concatenate([g, jnp.zeros((64, CHUNK), F32)], axis=0)
+        GU[4 * n : 4 * n + 4] = g.T.reshape(4, 2, 32, UNITS) + QBP[...]
+
+    def qkv_pair():
         XSQ[...] = GU[:, 1 - f].astype(BF16)
         pair(8, XSQ, XRQ).start()
-        ones8 = jnp.ones((8, D), BF16)
-        b = nt(ones8, JG[0]) + nt(ones8, JG[1])
-        QB1[...] = jnp.concatenate([b, jnp.zeros((8, 64), F32)], axis=1)
-        pair(9, QB1, QB2).start()
 
     def qkv_push():
         pair(8, XRQ, XRQ).wait_recv()
         AQ[...] = (GU[:, f] + XRQ[...].astype(F32)).astype(BF16)
         RQ[c] = AQ[c]
         send_all(6, lambda to: AQ.at[to], RQ.at[c])
-        pair(9, QB2, QB2).wait_recv()
-        pair(9, QB1, QB1).wait_send()
-        QB1[...] = QB1[...] + QB2[...]
-        QB3[c] = QB1[...]
-        send_all(7, lambda to: QB1, QB3.at[c])
 
     def riders(d, ch):
         return GO[ch, pl.ds(pl.multiple_of(f * 32 + 16 * d, 16), 16)] + XRO[ch, 16 * d : 16 * d + 16].astype(F32)
@@ -563,43 +730,29 @@
         for w in range(1, NCTX):
             total = total + SGC[w]
         gs_ref[...] = total
-        gs_ref[6:7, :] = SGT[6:7, pl.ds(pl.multiple_of(f * 128, 128), 128)]
-        pair(7, XRD, XRD).wait_recv()
-        gd_ref[...] = GD[f] + XRD[...].astype(F32)
-
-    def up_rest():
-        recv_all(5, RU.at[0:15])
-        for w in range(NCTX):
-            gu_ref[:, UNITS * w : UNITS * (w + 1)] = RU[w].astype(F32)
+        here = lax.rem(c, 4)
+        gs_ref[6:7, :] = SGC[here, 6:7, :] + SGC[4 + here, 6:7, :] + SGC[8 + here, 6:7, :] + SGC[12 + here, 6:7, :]
+
+    def down_rest():
+        def put(total):
+            gd_ref[...] = total
+
+        z_total(1, put)
 
     def on_the_way(it):
-        pl.when(it == 1)(qkv_grad)
-        pl.when(it == 3)(small_rest)
-        pl.when(it == 4)(qkv_push)
-        pl.when(it == 6)(up_rest)
+        pl.when(it == 0)(qkv_bias_rows)
+        for n in range(4):
+            pl.when(it == n)(partial(qkv_grad, n))
+        pl.when(it == 3)(qkv_pair)
+        pl.when(it == 4)(small_rest)
+        pl.when(it == 5)(qkv_push)
+        pl.when(it == 6)(down_rest)
+        pl.when(it == 8)(up_push)
 
     pair(5, XRO, XRO).wait_recv()
-    ring(2, None, make_token, on_the_way, finish_token)
-
+    ring(make_token, on_the_way, finish_token)
+    recv_plane(1, RU.at[0:7])
     recv_all(6, RQ.at[0:15])
-    for j in range(8):
-        a = RQ[2 * j].astype(F32)
-        b = RQ[2 * j + 1].astype(F32)
-        cols = slice(128 * j, 128 * (j + 1))
-        gq_ref[:, cols] = jnp.where(low_half, a[:, 0:128], pltpu.roll(b[:, 0:128], 64, 1))
-        gq_ref[:, D + 128 * j : D + 128 * (j + 1)] = jnp.where(low_half, pltpu.roll(a[:, 0:128], 64, 1), b[:, 0:128])
-        gq_ref[:, 2 * D + 128 * j : 2 * D + 128 * (j + 1)] = jnp.where(low_half, a[:, 128:256], pltpu.roll(b[:, 128:256], 64, 1))
-    recv_all(7, QB3.at[0:15])
-    for j in range(8):
-        a = QB3[2 * j]
-        b = QB3[2 * j + 1]
-        rows = (
-            jnp.where(low_half, a[:, 0:128], pltpu.roll(b[:, 0:128], 64, 1)),
-            jnp.where(low_half, pltpu.roll(a[:, 0:128], 64, 1), b[:, 0:128]),
-            jnp.where(low_half, a[:, 128:256], pltpu.roll(b[:, 128:256], 64, 1)),
-        )
-        for i in range(3):
-            gb_ref[8 * i + j : 8 * i + j + 1, :] = rows[i][0:1, :]
 
     remote(XF.at[0, 0:7], XF.at[0, 0:7], agx_s, sbx_r, "ctx", sib).wait_send()
     remote(XF.at[0], XF.at[0], sbx_s, sbx_r, "ctx", sib).wait_send()
@@ -608,14 +761,17 @@
     sent_all(0, WP.at[0:15])
     sent_all(1, VB.at[0:15])
     sent_all(4, SGC.at[0:15])
-    sent_all(5, AU.at[0:15])
     sent_all(6, AQ.at[0:15])
-    sent_all(7, QB3.at[0:15])
     remote(SSO, SSO, po_s, po_r, "ctx", sib).wait_send()
-    sent_all(8, WU.at[0:15, 0])
-    for i, at in enumerate((VEC, wo_ref, wd_ref, WB.at[:, f], SG, XSO, XSU, XSD, XSQ)):
+    sent_plane(0, WUS.at[0:7])
+    sent_plane(1, PUS.at[0:7])
+    for kd in range(2):
+        for s in range(3):
+            z_gather(kd, s, True)
+        z_start(kd, True)
+        z_relay(kd, True)
+    for i, at in ((0, VEC), (1, wo_ref), (3, WB.at[:, f]), (4, SG), (5, XSO), (8, XSQ)):
         pair(i, at, at).wait_send()
-    pair(10, WU.at[:, f], WU.at[:, f]).wait_send()
 
 
 def rope_tables():
@@ -630,35 +786,37 @@
 ):
     scratch = [
         ((8, 128), F32),
-        ((2, 8, 128, D), BF16), ((2, 8, 128, D), BF16), ((2, 8, 128, D), BF16),
-        ((16, 32, 256), BF16), ((16, 2, 32, 256), BF16), ((16, 2, 32, UNITS), BF16), ((16, 2, 32, D), BF16), ((2, 128, D), BF16),
-        ((16, 2, 8, 128), F32), ((8, D), F32), ((8, UNITS), F32), ((24, 128), F32), ((3, 128, 128), F32),
+        ((2, 8, 128, D), BF16), ((4, 2, 128, D), BF16), ((4, 2, 128, D), BF16),
+        ((16, 32, 256), BF16), ((16, 2, 32, 256), BF16), ((8, 32, FF_UNITS), BF16), ((4, 8, 32, FF_UNITS), BF16),
+        ((16, 2, 32, D), BF16), ((4, 128, D), BF16),
+        ((16, 2, 8, 128), F32), ((8, D), F32), ((8, FF_UNITS), F32), ((24, 128), F32), ((3, 128, 128), F32),
         ((256, D), BF16),
         ((2, 64, D), BF16), ((2, 64, D), BF16), ((2, 64, D), BF16), ((2, D, 64), BF16), ((2, D, 64), BF16),
         ((2, D, D), BF16), ((2, 64, D), F32),
         ((16, 64, 128), BF16), ((16, 64, 128), BF16), ((16, 64, 128), BF16),
         ((128, D), F32), ((128, D), F32), ((128, 128), F32), ((128, D), F32), ((128, D), F32),
-        ((2, 8, 128, UNITS), F32), ((2, 8, 128, UNITS), BF16), ((2, 8, 128, UNITS), BF16),
-        ((2, 3, 128, D), F32),
+        ((4, 2, 128, FF_UNITS), F32), ((4, 2, 128, FF_UNITS), BF16), ((4, 2, 128, FF_UNITS), BF16),
+        ((2, 4, 128, D), F32),
         ((2, 8, BLK, D), BF16), ((2, 8, BLK, D), BF16), ((2, 8, 80, D), BF16), ((2, 8, 80, D), BF16),
-        ((UNITS, 2048), BF16),
-        ((16, 2, 32, UNITS), F32), ((16, 32, UNITS), BF16), ((16, 32, UNITS), BF16), ((16, 32, UNITS), BF16), ((16, 32, UNITS), BF16),
-        ((2, 128, D), F32), ((128, D), BF16), ((128, D), BF16),
+        ((FF_UNITS, 1024), BF16),
+        ((16, 2, 32, UNITS), F32), ((8, 32, FF_UNITS), BF16),
+        ((4, 8, 32, FF_UNITS), BF16), ((4, 128, D), BF16), ((4, 8, 32, FF_UNITS), BF16), ((4, 128, D), BF16),
         ((8, BLK, D), F32), ((8, 32, D), BF16), ((8, 32, D), BF16), ((8, BLK, D), BF16), ((8, BLK, D), BF16),
         ((8, D), F32), ((8, D), F32), ((8, D), F32), ((16, 8, 128), F32), ((2, 64, D), BF16),
         ((2, 64, D), F32), ((2, 64, D), F32), ((2, 192, D), BF16),
-        ((16, 32, UNITS), BF16), ((16, 32, UNITS), BF16), ((16, 32, UNITS), BF16), ((16, 32, UNITS), BF16),
-        ((8, 256), F32), ((8, 256), F32), ((16, 8, 256), F32),
+        ((16, 32, UNITS), BF16), ((16, 32, UNITS), BF16), ((16, 32, UNITS), BF16), ((32, UNITS), F32),
     ]
-    sems = [(12,), (2, 8 * AQS), (2, 8), (2, 8), (2, 8 * RQS), (2, 8), (9,), (9,), (11,), (11,)]
+    sems = [(14,), (2, 8 * AQS), (2, 8), (2, 8 * RQS), (2, 8), (9,), (9,), (11,), (11,), (2,), (2,)]
+    sems += [(2, 3), (2, 4), (2, 4), (2, 3), (2, 6), (2, 4), (2, 4), (2, 4)]
     vmem = pl.BlockSpec(memory_space=pltpu.VMEM)
-    shapes = [((2, BLK, D), BF16), ((2, BLK, D), F32), ((32, 3 * D), F32), ((32, D), F32), ((32, 4 * D), F32), ((128, D), F32), ((8, 128), F32), ((24, 128), F32)]
+    shapes = [((2, BLK, D), BF16), ((2, BLK, D), F32), ((16, 32, UNITS), BF16), ((32, D), F32), ((8, 32, FF_UNITS), BF16), ((128, D), F32), ((8, 128), F32)]
+    final = shapes[:2] + [((32, 3 * D), F32), shapes[3], ((32, 4 * D), F32), shapes[5]]
     bias = (up_bias, qkv_bias, out_bias, down_bias, first_gain, first_shift, second_gain, second_shift)
     made = pl.pallas_call(
         layer_kernel,
         out_shape=[jax.ShapeDtypeStruct(s, t) for s, t in shapes],
         in_specs=[vmem] * 15,
-        out_specs=[vmem] * 8,
+        out_specs=[vmem] * 7,
         scratch_shapes=[pltpu.VMEM(s, t) for s, t in scratch] + [pltpu.SemaphoreType.DMA(s) for s in sems],
         compiler_params=pltpu.CompilerParams(collective_id=0, has_side_effects=True, vmem_limit_bytes=VMEM_LIMIT),
         name="layer",
@@ -670,20 +828,37 @@
     widths = (96, 32, 128, 32, 32, 32, 32, 32)
     last = pl.pallas_call(
         finish_kernel,
-        out_shape=[jax.ShapeDtypeStruct(s, t) for s, t in shapes[:6]] + [jax.ShapeDtypeStruct((1, w), F32) for w in widths],
-        in_specs=[anywhere] * 6 + [vmem] * 2,
+        out_shape=[jax.ShapeDtypeStruct(s, t) for s, t in final] + [jax.ShapeDtypeStruct((1, w), F32) for w in widths],
+        in_specs=[anywhere, anywhere, vmem, anywhere, vmem, anywhere, vmem],
         out_specs=[vmem] * 14,
-        scratch_shapes=[pltpu.SemaphoreType.DMA((6,))],
+        scratch_shapes=[pltpu.VMEM((24, 128), F32), pltpu.SemaphoreType.DMA((4,))],
         name="finish",
     )(*made)
     return (last[0][:, None], last[1][:, None], *last[2:6], *(v[0] for v in last[6:]))
 
 
 def finish_kernel(*refs):
-    big, (gs, gb), done, small, sems = refs[:6], refs[6:8], refs[8:14], refs[14:22], refs[22]
-    copies = [pltpu.make_async_copy(a, b, sems.at[i]) for i, (a, b) in enumerate(zip(big, done))]
+    (out, tg, rq, go, ru, gd, gs), done, small, (gb, sems) = refs[:7], refs[7:13], refs[13:21], refs[21:]
+    pairs = ((out, done[0]), (tg, done[1]), (go, done[3]), (gd, done[5]))
+    copies = [pltpu.make_async_copy(a, b, sems.at[i]) for i, (a, b) in enumerate(pairs)]
     for copy in copies:
         copy.start()
+    gq, gu = done[2], done[4]
+    low_half = lax.broadcasted_iota(jnp.int32, (1, 128), 1) < 64
+    for j in range(8):
+        a = rq[2 * j].astype(F32)
+        b = rq[2 * j + 1].astype(F32)
+        a0, a1, b0, b1 = a[:, 0:128], a[:, 128:256], b[:, 0:128], b[:, 128:256]
+        v = pltpu.roll(b1, 64, 1)
+        gq[:, 128 * j : 128 * (j + 1)] = jnp.where(low_half, a0, pltpu.roll(b0, 64, 1))
+        gq[:, D + 128 * j : D + 128 * (j + 1)] = jnp.where(low_half, pltpu.roll(a0, 64, 1), b0)
+        gq[:, 2 * D + 128 * j : 2 * D + 128 * (j + 1)] = jnp.where(low_half, a1, v)
+        bias = jnp.where(low_half, pltpu.roll(a1, 64, 1), b1)
+        for i in range(3):
+            gb[8 * i + j : 8 * i + j + 1, :] = bias[i : i + 1, :]
+    for w in range(8):
+        for i in range(4):
+            gu[:, 128 * (8 * i + w) : 128 * (8 * i + w + 1)] = ru[w, :, 128 * i : 128 * (i + 1)].astype(F32)
     index = lax.axis_index("ctx") * 2 + lax.axis_index("fsdp")
     place = lax.rem(index, 4)
     turned = pltpu.roll(gs[...], lax.rem(128 - 32 * place, 128), 1)

time: 233 us -> 220 us (0.944)
  Pallas kernels: 232 us -> 219 us
    pallas_call x1, Pallas kernels: 228 us -> 215 us  [fused_body(): pl.pallas_call(layer_kernel, out_shape=[jax.ShapeDtypeStruct(s, t) for s,...]
where the time goes in v3:
time: 220 us
  Pallas kernels  219 us (100%)
    pallas_call x1, Pallas kernels, fused_body(): pl.pallas_call(layer_kernel, out_shape=[jax.ShapeDtypeStruct(s, t) for s,...  215 us

profile of v3, /device:TPU:0, one launch (start us, length us, event | category | flops | bytes accessed | tf_op | source)
XLA Modules:
  0.0 219.8 jit_solution(333976393663503689)
XLA Ops:
  0.7 215.1 %layer.1 = (bf16[2,64,1024]{2,1,0:T(8,128)(2,1)}, f32[2,64,1024]{2,1,0:T(8,128)}, bf16[16,32,256]{2,1,0:T(8,128)(2,1)}, f32[32,1024]{1,0:T(8,128)}, bf16[8,32,51...) custom-call(bf16[2,64,1024]{2,1,0:T(8,128)(2,1)} %bitcast.24, bf16[2,64,1024]{2,1,0:T(8,128)(2,1)} %bitcast.25, ...), custom_call_target="tpu_custom_call" | custom-call | tf_op jit(solution)/shard_map/layer/pallas_call | solution.py:815
  215.8 3.9 %finish.1 = (bf16[2,64,1024]{2,1,0:T(8,128)(2,1)}, f32[2,64,1024]{2,1,0:T(8,128)}, f32[32,3072]{1,0:T(8,128)}, f32[32,1024]{1,0:T(8,128)}, f32[32,4096]{1,0:T(8,...) custom-call(bf16[2,64,1024]{2,1,0:T(8,128)(2,1)} %get-tuple-element., ...), custom_call_target="tpu_custom_call" | custom-call | tf_op jit(solution)/shard_map/finish/pallas_call | solution.py:829

commit v4 on v3

--- a/solution.py
+++ b/solution.py
@@ -24,7 +24,7 @@
 UNITS = 256
 FF_UNITS = 512
 CHUNK = 256
-AQS = 2
+AQS = 4
 RQS = 4
 ROWS = BLK // RQS
 
@@ -128,7 +128,7 @@
                 body(place)
 
     def z_block(kd, b, dr, s, place):
-        at = (WU, WD)[kd].at[b]
+        at = WU.at[b, pl.ds(4 * kd, 4)] if kd < 2 else WD.at[b, pl.ds(64 * kd - 128, 64)]
         return remote(at, at, z_s.at[kd, dr * 3 + s], z_r.at[kd, b], "ctx", c + (4 if dr == 0 else -4))
 
     def z_gather(kd, s, sent=False):
@@ -218,7 +218,7 @@
 
     for m in range(2):
         XF[m, chip, pl.ds(mine, BLK)] = x_ref[m]
-    WO[c, f] = wo_ref[...]
+    WO[chip, core, f] = wo_ref[...]
     WD[zz] = wd_ref[...]
     VEC[...] = jnp.zeros((8, 128), F32)
     for i, v in enumerate((v0, v1, v2, v3, v4, v5, v6, v7)):
@@ -244,7 +244,7 @@
 
     def gather_wo(k):
         for d in range(2):
-            at = WO.at[chip_of(d, k) * 2 + core, d]
+            at = WO.at[chip_of(d, k), core, f, pl.ds(16 * d, 16)]
 
             @pl.when(k > 0)
             def _():
@@ -254,11 +254,8 @@
             def _():
                 remote(at, at, wo_s, wo_r.at[d, k], "ctx", target(d)).start()
 
-            remote(at, at, wos_s, wos_r, "ctx", sib).start()
-
     pl.loop(0, 1)(gather_x)
     pair(0, VEC, VB.at[c, f]).start()
-    pair(1, wo_ref, WO.at[c, f]).start()
 
     for j in range(8):
         qt = wq_ref[:, 128 * j : 128 * j + 128].astype(F32)
@@ -276,48 +273,65 @@
             WUS[w, :, 128 * i : 128 * (i + 1)] = wu_ref[:, 128 * (8 * i + w) : 128 * (8 * i + w + 1)]
     WU[zz, pp] = WUS[pp]
     send_plane(0, lambda to: WUS.at[to], WU.at[zz, pp])
-    pl.loop(1, 4)(gather_x)
+
+    @pl.loop(1, 4)
+    def _(k):
+        gather_x(k)
+        gather_wo(k - 1)
+
     pair(0, VB.at[c, 1 - f], VB.at[c, 1 - f]).wait_recv()
     send_all(1, lambda to: VB.at[c], VB.at[c])
     recv_all(0, WB.at[0:15, 0])
     pair(3, WB.at[:, f], WB.at[:, f]).start()
-    pair(1, WO.at[c, 1 - f], WO.at[c, 1 - f]).wait_recv()
     recv_plane(0, WU.at[zz, 0:7])
+
+    def head_weights():
+        pair(3, WB.at[:, 1 - f], WB.at[:, 1 - f]).wait_recv()
+        WHT[...] = WB[...].reshape(D, 256).T
+
+    def vectors():
+        recv_all(1, VB.at[0:15])
+        for j in range(8):
+            tiles = [VB[2 * j + q // 2, q % 2] for q in range(4)]
+            total = tiles[0]
+            for q in range(1, 4):
+                total = total + pltpu.roll(tiles[q], 32 * q, 1)
+            VF[:, 128 * j : 128 * j + 128] = total
+            v1 = pltpu.roll(tiles[1], 96, 1)
+            v2 = pltpu.roll(tiles[2], 64, 1)
+            v3 = pltpu.roll(tiles[3], 32, 1)
+            rows = (
+                tiles[0] + jnp.where(lane >= 96, v1, 0.0),
+                jnp.where(lane < 64, v1, 0.0) + jnp.where(lane >= 64, v2, 0.0),
+                jnp.where(lane < 32, v2, 0.0) + v3,
+            )
+            for i in range(3):
+                QBR[3 * j + i : 3 * j + i + 1, :] = rows[i][1:2, :]
+        for i in range(4):
+            UB[0:1, 128 * i : 128 * (i + 1)] = VB[4 * i + lax.rem(c, 4), f, 0:1, :]
+        for i in range(3):
+            row = QBR[pl.ds(8 * i + chip, 1), :]
+            BQ[i] = jnp.broadcast_to(row, (128, 128)).T
 
     @pl.loop(4, 8)
     def _(k):
         gather_x(k)
-        gather_wo(k - 4)
-        pl.when(k == 4)(lambda: z_gather(0, 0))
-        pl.when(k == 6)(lambda: z_gather(1, 0))
-
-
+        gather_wo(k - 1)
+        pl.when(k == 6)(vectors)
+        pl.when(k == 7)(head_weights)
+
+        @pl.when(k == 6)
+        def _():
+            z_gather(0, 0)
+            z_gather(1, 0)
+
+
+    gather_wo(jnp.int32(7))
+    pair(1, WO.at[:, core, f], WO.at[:, core, f]).start()
+    z_gather(2, 0)
+    z_gather(3, 0)
     remote(XF.at[0], XF.at[0], sbx_s, sbx_r, "ctx", sib).wait_recv()
-    recv_all(1, VB.at[0:15])
-
-    for j in range(8):
-        tiles = [VB[2 * j + q // 2, q % 2] for q in range(4)]
-        total = tiles[0]
-        for q in range(1, 4):
-            total = total + pltpu.roll(tiles[q], 32 * q, 1)
-        VF[:, 128 * j : 128 * j + 128] = total
-        v1 = pltpu.roll(tiles[1], 96, 1)
-        v2 = pltpu.roll(tiles[2], 64, 1)
-        v3 = pltpu.roll(tiles[3], 32, 1)
-        rows = (
-            tiles[0] + jnp.where(lane >= 96, v1, 0.0),
-            jnp.where(lane < 64, v1, 0.0) + jnp.where(lane >= 64, v2, 0.0),
-            jnp.where(lane < 32, v2, 0.0) + v3,
-        )
-        for i in range(3):
-            QBR[3 * j + i : 3 * j + i + 1, :] = rows[i][1:2, :]
-    for i in range(4):
-        UB[0:1, 128 * i : 128 * (i + 1)] = VB[4 * i + lax.rem(c, 4), f, 0:1, :]
-    for i in range(3):
-        row = QBR[pl.ds(8 * i + chip, 1), :]
-        BQ[i] = jnp.broadcast_to(row, (128, 128)).T
-    pair(3, WB.at[:, 1 - f], WB.at[:, 1 - f]).wait_recv()
-    WHT[...] = WB[...].reshape(D, 256).T
+
 
     def lanes(n):
         return pl.ds(pl.multiple_of(n * CHUNK, CHUNK), CHUNK)
@@ -352,16 +366,21 @@
 
     @pl.loop(0, 8)
     def _(it):
-        @pl.when(lax.rem(it, 2) == 0)
+        @pl.when(it == 0)
         def _():
-            gather_wo(4 + lax.div(it, 2))
+            z_gather(0, 1)
+            z_gather(1, 1)
 
         @pl.when(it == 4)
         def _():
-            pass
-
-        pl.when(it == 0)(lambda: z_gather(0, 1))
-        pl.when(it == 5)(lambda: z_gather(1, 1))
+            z_gather(2, 1)
+            z_gather(3, 1)
+
+        @pl.when(it == 5)
+        def _():
+            pair(1, WO.at[:, core, 1 - f], WO.at[:, core, 1 - f]).wait_recv()
+            remote(WO.at[:, core], WO.at[:, core], wos_s, wos_r, "ctx", sib).start()
+
         m = lax.div(it, 4)
         n = lax.rem(it, 4)
         s = nn(KN[m], QT[m, :, lanes(n)]) * 0.125
@@ -378,11 +397,13 @@
     AT[c] = ATS[c]
     send_all(2, lambda to: ATS.at[to], AT.at[c])
 
-    remote(WO.at[0:8], WO.at[0:8], wos_s, wos_r, "ctx", sib).wait_recv()
     z_gather(0, 2)
+    z_gather(1, 2)
+    remote(WO.at[:, 1 - core], WO.at[:, 1 - core], wos_s, wos_r, "ctx", sib).wait_recv()
     recv_all(2, AT.at[0:15])
 
-    z_gather(1, 2)
+    z_gather(2, 2)
+    z_gather(3, 2)
     att_rows = AT[...].reshape(D, 128).T
     resid = x_ref[...].reshape(128, D).astype(F32) + nn(att_rows, WO[...].reshape(D, D)) + VF[2:3, :]
     center = resid - row_mean(resid)
@@ -396,7 +417,7 @@
     for m in range(2):
         HF[grp, m, pl.ds(mine, BLK)] = hidden_low[m * BLK : (m + 1) * BLK]
 
-    def plane(buf, make, ready, after_one, after_two, finish):
+    def plane(buf, make, early, ready, after_one, after_two, finish):
         far = ((yy * 2 + 1 - f), ((1 - yy) * 2 + f))
         groups = tuple((grp, far[m], far[1 - m], (1 - yy) * 2 + 1 - f) for m in range(2))
 
@@ -415,10 +436,12 @@
             to(m, at(m, i, mine), at(m, i, mine), pa_s, pa_r.at[m, n]).wait_recv()
 
         def work(m, i):
-            remote(at(m, i, other), at(m, i, other), pb_s, pb_r.at[m, i], "ctx", sib).wait_recv()
             PB[m, i] = make(groups[m][i], m)
             SS[m, i] = PB[m, i, pl.ds(other, BLK)].astype(BF16)
             remote(SS.at[m, i], SR.at[m, i], ps_s, ps_r.at[m, i], "ctx", sib).start()
+
+        def both(m, i):
+            remote(at(m, i, other), at(m, i, other), pb_s, pb_r.at[m, i], "ctx", sib).wait_recv()
 
         def share(m, i):
             remote(SR.at[m, i], SR.at[m, i], ps_s, ps_r.at[m, i], "ctx", sib).wait_recv()
@@ -438,7 +461,9 @@
         for m in range(2):
             hand_over(m, 0)
             to(1 - m, at(m, 0, mine), at(m, 0, mine), pa_s, pa_r.at[m, 1]).start()
-        if ready is None:
+        for m in range(2):
+            both(m, 0)
+        if early is not None:
             for m in range(2):
                 work(m, 0)
         for m in range(2):
@@ -448,17 +473,24 @@
         for m in range(2):
             arrive(m, 2, 1)
             hand_over(m, 2)
-        if ready is None:
+        for m in range(2):
+            both(m, 1)
+        if early is not None:
             for m in range(2):
                 work(m, 1)
         for m in range(2):
             arrive(m, 3, 2)
             hand_over(m, 3)
+        for m in range(2):
+            both(m, 2)
+            both(m, 3)
         if ready is not None:
             ready()
-        for i in (2, 3) if ready is None else (3, 2, 1, 0):
+        for i in (3, 2, 1, 0) if early is None else (3, 2):
             for m in range(2):
                 work(m, i)
+        if early is not None:
+            early()
         for m in range(2):
             push(m, 1, share(m, 3), 1 - m)
         for m in range(2):
@@ -567,10 +599,10 @@
         SEC[rows, :] = H1[rows, :] + total + VF[3:4, :]
 
     def weights_in():
-        z_gather(0, 3)
-        z_gather(1, 3)
-
-    plane(HF, make_up, weights_in, nothing, nothing, finish_up)
+        for kd in range(4):
+            z_gather(kd, 3)
+
+    plane(HF, make_up, None, weights_in, nothing, nothing, finish_up)
 
     resid = SEC[...]
     center = resid - row_mean(resid)
@@ -609,12 +641,11 @@
         for i in range(4):
             g = nn(TT[...], HF[:, :, :, CHUNK * i : CHUNK * (i + 1)].reshape(1024, CHUNK))
             DWU[i] = g.T.astype(BF16).reshape(8, 32, FF_UNITS)
-        z_start(0)
         sums = nn(jnp.ones((8, 1024), BF16), PG[...].reshape(1024, FF_UNITS))[0:1, :]
         for i in range(8):
             SG[6:7, 128 * i : 128 * (i + 1)] = sums[:, 128 * (i // 2) : 128 * (i // 2) + 128]
 
-    plane(BG, make_down, None, down_grads, up_grads, finish_down)
+    plane(BG, make_down, nothing, down_grads, nothing, up_grads, finish_down)
 
     hid = SEC[...]
     z = Z1[...]
@@ -642,6 +673,7 @@
         XSO[j] = GO[j, pl.ds(pl.multiple_of((1 - f) * 32, 32), 32)].astype(BF16)
     pair(5, XSO, XRO).start()
     recv_all(3, AGT.at[0:15])
+    z_start(0)
     sent_all(3, ATS.at[0:15])
 
     for j in range(8):
@@ -756,8 +788,8 @@
 
     remote(XF.at[0, 0:7], XF.at[0, 0:7], agx_s, sbx_r, "ctx", sib).wait_send()
     remote(XF.at[0], XF.at[0], sbx_s, sbx_r, "ctx", sib).wait_send()
-    remote(WO.at[0:7], WO.at[0:7], wo_s, sbx_r, "ctx", sib).wait_send()
-    remote(WO.at[0:8], WO.at[0:8], wos_s, sbx_r, "ctx", sib).wait_send()
+    remote(WO.at[0:7, 0, 0], WO.at[0:7, 0, 0], wo_s, sbx_r, "ctx", sib).wait_send()
+    remote(WO.at[:, 0], WO.at[:, 0], wos_s, sbx_r, "ctx", sib).wait_send()
     sent_all(0, WP.at[0:15])
     sent_all(1, VB.at[0:15])
     sent_all(4, SGC.at[0:15])
@@ -768,9 +800,10 @@
     for kd in range(2):
         for s in range(3):
             z_gather(kd, s, True)
+            z_gather(kd + 2, s, True)
         z_start(kd, True)
         z_relay(kd, True)
-    for i, at in ((0, VEC), (1, wo_ref), (3, WB.at[:, f]), (4, SG), (5, XSO), (8, XSQ)):
+    for i, at in ((0, VEC), (1, WO.at[:, core, f]), (3, WB.at[:, f]), (4, SG), (5, XSO), (8, XSQ)):
         pair(i, at, at).wait_send()
 
 
@@ -788,7 +821,7 @@
         ((8, 128), F32),
         ((2, 8, 128, D), BF16), ((4, 2, 128, D), BF16), ((4, 2, 128, D), BF16),
         ((16, 32, 256), BF16), ((16, 2, 32, 256), BF16), ((8, 32, FF_UNITS), BF16), ((4, 8, 32, FF_UNITS), BF16),
-        ((16, 2, 32, D), BF16), ((4, 128, D), BF16),
+        ((8, 2, 2, 32, D), BF16), ((4, 128, D), BF16),
         ((16, 2, 8, 128), F32), ((8, D), F32), ((8, FF_UNITS), F32), ((24, 128), F32), ((3, 128, 128), F32),
         ((256, D), BF16),
         ((2, 64, D), BF16), ((2, 64, D), BF16), ((2, 64, D), BF16), ((2, D, 64), BF16), ((2, D, 64), BF16),
@@ -807,7 +840,7 @@
         ((16, 32, UNITS), BF16), ((16, 32, UNITS), BF16), ((16, 32, UNITS), BF16), ((32, UNITS), F32),
     ]
     sems = [(14,), (2, 8 * AQS), (2, 8), (2, 8 * RQS), (2, 8), (9,), (9,), (11,), (11,), (2,), (2,)]
-    sems += [(2, 3), (2, 4), (2, 4), (2, 3), (2, 6), (2, 4), (2, 4), (2, 4)]
+    sems += [(2, 3), (2, 4), (2, 4), (2, 3), (4, 6), (4, 4), (2, 4), (2, 4)]
     vmem = pl.BlockSpec(memory_space=pltpu.VMEM)
     shapes = [((2, BLK, D), BF16), ((2, BLK, D), F32), ((16, 32, UNITS), BF16), ((32, D), F32), ((8, 32, FF_UNITS), BF16), ((128, D), F32), ((8, 128), F32)]
     final = shapes[:2] + [((32, 3 * D), F32), shapes[3], ((32, 4 * D), F32), shapes[5]]

time: 220 us -> 204 us (0.927)
  Pallas kernels: 219 us -> 203 us
    pallas_call x1, Pallas kernels: 215 us -> 199 us  [fused_body(): pl.pallas_call(layer_kernel, out_shape=[jax.ShapeDtypeStruct(s, t) for s,...]
where the time goes in v4:
time: 204 us
  Pallas kernels  203 us (100%)
    pallas_call x1, Pallas kernels, fused_body(): pl.pallas_call(layer_kernel, out_shape=[jax.ShapeDtypeStruct(s, t) for s,...  199 us

profile of v4, /device:TPU:0, one launch (start us, length us, event | category | flops | bytes accessed | tf_op | source)
XLA Modules:
  0.0 203.6 jit_solution(5638377102567260156)
XLA Ops:
  0.7 198.9 %layer.1 = (bf16[2,64,1024]{2,1,0:T(8,128)(2,1)}, f32[2,64,1024]{2,1,0:T(8,128)}, bf16[16,32,256]{2,1,0:T(8,128)(2,1)}, f32[32,1024]{1,0:T(8,128)}, bf16[8,32,51...) custom-call(bf16[2,64,1024]{2,1,0:T(8,128)(2,1)} %bitcast.24, bf16[2,64,1024]{2,1,0:T(8,128)(2,1)} %bitcast.25, ...), custom_call_target="tpu_custom_call" | custom-call | tf_op jit(solution)/shard_map/layer/pallas_call | solution.py:848
  199.5 3.9 %finish.1 = (bf16[2,64,1024]{2,1,0:T(8,128)(2,1)}, f32[2,64,1024]{2,1,0:T(8,128)}, f32[32,3072]{1,0:T(8,128)}, f32[32,1024]{1,0:T(8,128)}, f32[32,4096]{1,0:T(8,...) custom-call(bf16[2,64,1024]{2,1,0:T(8,128)(2,1)} %get-tuple-element., ...), custom_call_target="tpu_custom_call" | custom-call | tf_op jit(solution)/shard_map/finish/pallas_call | solution.py:862

commit v5 on v4

--- a/solution.py
+++ b/solution.py
@@ -254,6 +254,8 @@
             def _():
                 remote(at, at, wo_s, wo_r.at[d, k], "ctx", target(d)).start()
 
+            pair(1, at, at).start()
+
     pl.loop(0, 1)(gather_x)
     pair(0, VEC, VB.at[c, f]).start()
 
@@ -327,7 +329,6 @@
 
 
     gather_wo(jnp.int32(7))
-    pair(1, WO.at[:, core, f], WO.at[:, core, f]).start()
     z_gather(2, 0)
     z_gather(3, 0)
     remote(XF.at[0], XF.at[0], sbx_s, sbx_r, "ctx", sib).wait_recv()
@@ -358,7 +359,7 @@
         q = turn(q, cosine, sine)
         k = turn(k, cosine, sine)
         rows = pl.ds(pl.multiple_of(n * CHUNK, CHUNK), CHUNK)
-        QT[m, :, lanes(n)] = q.astype(BF16)
+        QT[m, :, lanes(n)] = (q.astype(BF16).astype(F32) * 0.125).astype(BF16)
         KT[m, :, lanes(n)] = k.astype(BF16)
         VT[m, :, lanes(n)] = v.astype(BF16)
         KN[m, rows, :] = k.T.astype(BF16)
@@ -376,14 +377,14 @@
             z_gather(2, 1)
             z_gather(3, 1)
 
-        @pl.when(it == 5)
+        @pl.when(it == 3)
         def _():
             pair(1, WO.at[:, core, 1 - f], WO.at[:, core, 1 - f]).wait_recv()
             remote(WO.at[:, core], WO.at[:, core], wos_s, wos_r, "ctx", sib).start()
 
         m = lax.div(it, 4)
         n = lax.rem(it, 4)
-        s = nn(KN[m], QT[m, :, lanes(n)]) * 0.125
+        s = nn(KN[m], QT[m, :, lanes(n)])
         e = jnp.exp(s - jnp.max(s, axis=0, keepdims=True))
         p = (e * (1.0 / jnp.sum(e, axis=0, keepdims=True))).astype(BF16)
         PT[m, :, lanes(n)] = p
@@ -435,10 +436,14 @@
         def arrive(m, i, n):
             to(m, at(m, i, mine), at(m, i, mine), pa_s, pa_r.at[m, n]).wait_recv()
 
-        def work(m, i):
-            PB[m, i] = make(groups[m][i], m)
-            SS[m, i] = PB[m, i, pl.ds(other, BLK)].astype(BF16)
-            remote(SS.at[m, i], SR.at[m, i], ps_s, ps_r.at[m, i], "ctx", sib).start()
+        def work(places):
+            part = make(groups[0][places[0]])
+            for m in range(2):
+                PB[m, places[m]] = part[128 * m : 128 * (m + 1)]
+            for m in range(2):
+                i = places[m]
+                SS[m, i] = PB[m, i, pl.ds(other, BLK)].astype(BF16)
+                remote(SS.at[m, i], SR.at[m, i], ps_s, ps_r.at[m, i], "ctx", sib).start()
 
         def both(m, i):
             remote(at(m, i, other), at(m, i, other), pb_s, pb_r.at[m, i], "ctx", sib).wait_recv()
@@ -464,8 +469,7 @@
         for m in range(2):
             both(m, 0)
         if early is not None:
-            for m in range(2):
-                work(m, 0)
+            work((0, 0))
         for m in range(2):
             arrive(m, 1, 0)
             to(1 - m, at(m, 1, mine), at(m, 1, mine), pa_s, pa_r.at[m, 2]).start()
@@ -473,28 +477,33 @@
         for m in range(2):
             arrive(m, 2, 1)
             hand_over(m, 2)
-        for m in range(2):
-            both(m, 1)
+        for i in (1, 2):
+            for m in range(2):
+                both(m, i)
         if early is not None:
-            for m in range(2):
-                work(m, 1)
+            work((1, 2))
         for m in range(2):
             arrive(m, 3, 2)
             hand_over(m, 3)
+        if early is not None:
+            work((2, 1))
         for m in range(2):
-            both(m, 2)
             both(m, 3)
         if ready is not None:
             ready()
-        for i in (3, 2, 1, 0) if early is None else (3, 2):
-            for m in range(2):
-                work(m, i)
+        work((3, 3))
         if early is not None:
             early()
+        else:
+            work((1, 2))
         for m in range(2):
             push(m, 1, share(m, 3), 1 - m)
+        if early is None:
+            work((2, 1))
         for m in range(2):
             push(m, 0, share(m, 2), 1 - m)
+        if early is None:
+            work((0, 0))
         after_one()
         for m in range(2):
             push(m, 2, share(m, 1) + pulled(m, 1), m)
@@ -528,6 +537,7 @@
 
         def second(k):
             slot = lax.rem(k, 2)
+            pl.when(k == 1)(lambda: pair(5, XRO, XRO).wait_recv())
             for d in range(2):
                 sums(d, k)
             for q in range(RQS):
@@ -586,12 +596,12 @@
     def down_w():
         return WD[...].reshape(FF_UNITS, D)
 
-    def make_up(g, m):
-        u = nn(HF[g, m], up_w()) + UB[0:1, :]
+    def make_up(g):
+        u = nn(HF[g].reshape(256, D), up_w()) + UB[0:1, :]
         phi = 0.5 * (1.0 + lax.erf(u * 0.7071067811865476))
         a = (u * phi).astype(BF16)
-        DG[g, m] = phi + u * (jnp.exp(-0.5 * u * u) * 0.3989422804014327)
-        ACT[g, m] = a
+        DG[g] = (phi + u * (jnp.exp(-0.5 * u * u) * 0.3989422804014327)).reshape(2, 128, FF_UNITS)
+        ACT[g] = a.reshape(2, 128, FF_UNITS)
         return nn(a, down_w())
 
     def finish_up(d, total):
@@ -621,9 +631,9 @@
     for m in range(2):
         BG[grp, m, pl.ds(mine, BLK)] = grad_low[m * BLK : (m + 1) * BLK]
 
-    def make_down(g, m):
-        pg = (nt(BG[g, m], down_w()) * DG[g, m]).astype(BF16)
-        PG[g, m] = pg
+    def make_down(g):
+        pg = (nt(BG[g].reshape(256, D), down_w()) * DG[g].reshape(256, FF_UNITS)).astype(BF16)
+        PG[g] = pg.reshape(2, 128, FF_UNITS)
         return nt(pg, up_w())
 
     def finish_down(d, total):
@@ -660,6 +670,7 @@
     ATS[...] = nt(WO[...].reshape(D, D), proj).astype(BF16).reshape(NCTX, HEAD, 128)
     AGT[c] = ATS[c]
     send_all(3, lambda to: ATS.at[to], AGT.at[c])
+    z_start(0)
 
     for j in range(NCHIP):
         SSO[j] = nn(AT[2 * j + 1 - core], proj).astype(BF16)
@@ -673,7 +684,6 @@
         XSO[j] = GO[j, pl.ds(pl.multiple_of((1 - f) * 32, 32), 32)].astype(BF16)
     pair(5, XSO, XRO).start()
     recv_all(3, AGT.at[0:15])
-    z_start(0)
     sent_all(3, ATS.at[0:15])
 
     for j in range(8):
@@ -704,7 +714,7 @@
     def _(it):
         pl.when(it == 2)(small_push)
         pl.when(it == 0)(lambda: z_relay(1))
-        pl.when(it == 5)(lambda: z_relay(0))
+        pl.when(it == 7)(lambda: z_relay(0))
         m = lax.div(it, 4)
         n = lax.rem(it, 4)
         q = QT[m, :, lanes(n)]
@@ -718,7 +728,7 @@
         JG[m, 0:64, lanes(n)] = unturn(dq, rope_ref[0, :, lanes(n)], rope_ref[1, :, lanes(n)]).astype(BF16)
 
     for m in range(2):
-        JG[m, 64:128, :] = unturn(DK[m] * 0.125, rope_ref[0], rope_ref[1]).astype(BF16)
+        JG[m, 64:128, :] = unturn(DK[m], rope_ref[0], rope_ref[1]).astype(BF16)
         JG[m, 128:192, :] = DV[m].astype(BF16)
 
     def make_token(m, ch):
@@ -781,7 +791,6 @@
         pl.when(it == 6)(down_rest)
         pl.when(it == 8)(up_push)
 
-    pair(5, XRO, XRO).wait_recv()
     ring(make_token, on_the_way, finish_token)
     recv_plane(1, RU.at[0:7])
     recv_all(6, RQ.at[0:15])

time: 204 us -> 197 us (0.966)
  Pallas kernels: 203 us -> 196 us
    pallas_call x1, Pallas kernels: 199 us -> 192 us  [fused_body(): pl.pallas_call(layer_kernel, out_shape=[jax.ShapeDtypeStruct(s, t) for s,...]
where the time goes in v5:
time: 197 us
  Pallas kernels  196 us (99%)
    pallas_call x1, Pallas kernels, fused_body(): pl.pallas_call(layer_kernel, out_shape=[jax.ShapeDtypeStruct(s, t) for s,...  192 us

profile of v5, /device:TPU:0, one launch (start us, length us, event | category | flops | bytes accessed | tf_op | source)
XLA Modules:
  0.0 197.1 jit_solution(13234022138171467410)
XLA Ops:
  0.7 192.4 %layer.1 = (bf16[2,64,1024]{2,1,0:T(8,128)(2,1)}, f32[2,64,1024]{2,1,0:T(8,128)}, bf16[16,32,256]{2,1,0:T(8,128)(2,1)}, f32[32,1024]{1,0:T(8,128)}, bf16[8,32,51...) custom-call(bf16[2,64,1024]{2,1,0:T(8,128)(2,1)} %bitcast.24, bf16[2,64,1024]{2,1,0:T(8,128)(2,1)} %bitcast.25, ...), custom_call_target="tpu_custom_call" | custom-call | tf_op jit(solution)/shard_map/layer/pallas_call | solution.py:857
  193.1 3.9 %finish.1 = (bf16[2,64,1024]{2,1,0:T(8,128)(2,1)}, f32[2,64,1024]{2,1,0:T(8,128)}, f32[32,3072]{1,0:T(8,128)}, f32[32,1024]{1,0:T(8,128)}, f32[32,4096]{1,0:T(8,...) custom-call(bf16[2,64,1024]{2,1,0:T(8,128)(2,1)} %get-tuple-element., ...), custom_call_target="tpu_custom_call" | custom-call | tf_op jit(solution)/shard_map/finish/pallas_call | solution.py:871

commit v6 on v5

--- a/solution.py
+++ b/solution.py
@@ -436,6 +436,9 @@
         def arrive(m, i, n):
             to(m, at(m, i, mine), at(m, i, mine), pa_s, pa_r.at[m, n]).wait_recv()
 
+        def half(m, i, h):
+            return buf.at[groups[m][i], m, pl.ds(pl.multiple_of(core * BLK + 32 * h, 32), 32)]
+
         def work(places):
             part = make(groups[0][places[0]])
             for m in range(2):
@@ -453,16 +456,22 @@
             return PB[m, i, pl.ds(mine, BLK)] + SR[m, i].astype(F32)
 
         def push(m, n, value, axis):
-            RSD[m, n, 0:BLK] = value.astype(BF16)
-            to(axis, RSD.at[m, n, pl.ds(0, BLK)], RR.at[m, n, pl.ds(0, BLK)], pr_s, pr_r.at[m, n]).start()
-
-        def pulled(m, n):
-            got = RR.at[m, n, pl.ds(0, BLK)]
-            to(m, got, got, pr_s, pr_r.at[m, n]).wait_recv()
-            return RR[m, n, 0:BLK].astype(F32)
+            for h in range(2):
+                rows = pl.ds(32 * h, 32)
+                RSD[m, n, rows] = value[32 * h : 32 * (h + 1)].astype(BF16)
+                to(axis, RSD.at[m, n, rows], RR.at[m, n, rows], pr_s, pr_r.at[m, 2 * n + h]).start()
+
+        def pulled(m, n, h):
+            got = RR.at[m, n, pl.ds(32 * h, 32)]
+            to(m, got, got, pr_s, pr_r.at[m, 2 * n + h]).wait_recv()
+            return RR[m, n, 32 * h : 32 * (h + 1)].astype(F32)
+
+        def pulled_all(m, n):
+            return jnp.concatenate([pulled(m, n, h) for h in range(2)], axis=0)
 
         for m in range(2):
-            to(m, at(m, 0, mine), at(m, 0, mine), pa_s, pa_r.at[m, 0]).start()
+            for h in range(2):
+                to(m, half(m, 0, h), half(m, 0, h), pa_s, pa_r.at[m, 3 * h]).start()
         for m in range(2):
             hand_over(m, 0)
             to(1 - m, at(m, 0, mine), at(m, 0, mine), pa_s, pa_r.at[m, 1]).start()
@@ -471,8 +480,9 @@
         if early is not None:
             work((0, 0))
         for m in range(2):
-            arrive(m, 1, 0)
-            to(1 - m, at(m, 1, mine), at(m, 1, mine), pa_s, pa_r.at[m, 2]).start()
+            for h in range(2):
+                to(m, half(m, 1, h), half(m, 1, h), pa_s, pa_r.at[m, 3 * h]).wait_recv()
+                to(1 - m, half(m, 1, h), half(m, 1, h), pa_s, pa_r.at[m, 2 + 2 * h]).start()
             hand_over(m, 1)
         for m in range(2):
             arrive(m, 2, 1)
@@ -483,7 +493,8 @@
         if early is not None:
             work((1, 2))
         for m in range(2):
-            arrive(m, 3, 2)
+            for h in range(2):
+                to(m, half(m, 3, h), half(m, 3, h), pa_s, pa_r.at[m, 2 + 2 * h]).wait_recv()
             hand_over(m, 3)
         if early is not None:
             work((2, 1))
@@ -506,10 +517,14 @@
             work((0, 0))
         after_one()
         for m in range(2):
-            push(m, 2, share(m, 1) + pulled(m, 1), m)
+            value = share(m, 1)
+            for h in range(2):
+                rows = pl.ds(32 * h, 32)
+                RSD[m, 2, rows] = (value[32 * h : 32 * (h + 1)] + pulled(m, 1, h)).astype(BF16)
+                to(m, RSD.at[m, 2, rows], RR.at[m, 2, rows], pr_s, pr_r.at[m, 4 + h]).start()
         after_two()
         for m in range(2):
-            finish(m, share(m, 0) + pulled(m, 0) + pulled(m, 2))
+            finish(m, share(m, 0) + pulled_all(m, 0) + pulled_all(m, 2))
         remote(XF.at[0, 0:3], XF.at[0, 0:3], pa_s, sbx_r, "ctx", sib).wait_send()
         remote(XF.at[0, 0:4], XF.at[0, 0:4], pb_s, sbx_r, "ctx", sib).wait_send()
         remote(XF.at[0, 0:4], XF.at[0, 0:4], ps_s, sbx_r, "ctx", sib).wait_send()
@@ -849,7 +864,7 @@
         ((16, 32, UNITS), BF16), ((16, 32, UNITS), BF16), ((16, 32, UNITS), BF16), ((32, UNITS), F32),
     ]
     sems = [(14,), (2, 8 * AQS), (2, 8), (2, 8 * RQS), (2, 8), (9,), (9,), (11,), (11,), (2,), (2,)]
-    sems += [(2, 3), (2, 4), (2, 4), (2, 3), (4, 6), (4, 4), (2, 4), (2, 4)]
+    sems += [(2, 5), (2, 4), (2, 4), (2, 6), (4, 6), (4, 4), (2, 4), (2, 4)]
     vmem = pl.BlockSpec(memory_space=pltpu.VMEM)
     shapes = [((2, BLK, D), BF16), ((2, BLK, D), F32), ((16, 32, UNITS), BF16), ((32, D), F32), ((8, 32, FF_UNITS), BF16), ((128, D), F32), ((8, 128), F32)]
     final = shapes[:2] + [((32, 3 * D), F32), shapes[3], ((32, 4 * D), F32), shapes[5]]

time: 197 us -> 197 us (level)
  no operation moved by 1% of the time
where the time goes in v6:
time: 197 us
  Pallas kernels  196 us (99%)
    pallas_call x1, Pallas kernels, fused_body(): pl.pallas_call(layer_kernel, out_shape=[jax.ShapeDtypeStruct(s, t) for s,...  192 us

profile of v6, /device:TPU:0, one launch (start us, length us, event | category | flops | bytes accessed | tf_op | source)
XLA Modules:
  0.0 197.1 jit_solution(7554777455107162525)
XLA Ops:
  0.7 192.4 %layer.1 = (bf16[2,64,1024]{2,1,0:T(8,128)(2,1)}, f32[2,64,1024]{2,1,0:T(8,128)}, bf16[16,32,256]{2,1,0:T(8,128)(2,1)}, f32[32,1024]{1,0:T(8,128)}, bf16[8,32,51...) custom-call(bf16[2,64,1024]{2,1,0:T(8,128)(2,1)} %bitcast.24, bf16[2,64,1024]{2,1,0:T(8,128)(2,1)} %bitcast.25, ...), custom_call_target="tpu_custom_call" | custom-call | tf_op jit(solution)/shard_map/layer/pallas_call | solution.py:872
  193.0 3.9 %finish.1 = (bf16[2,64,1024]{2,1,0:T(8,128)(2,1)}, f32[2,64,1024]{2,1,0:T(8,128)}, f32[32,3072]{1,0:T(8,128)}, f32[32,1024]{1,0:T(8,128)}, f32[32,4096]{1,0:T(8,...) custom-call(bf16[2,64,1024]{2,1,0:T(8,128)(2,1)} %get-tuple-element., ...), custom_call_target="tpu_custom_call" | custom-call | tf_op jit(solution)/shard_map/finish/pallas_call | solution.py:886
